TPU v7x, 512 devices: a whole 4x4x16 slice. The times are simulated.
512 devices in a mesh: section: 64 (over y, z), head: 8 (over x, core).
Axes of the slice: x: 4, y: 4, z: 16, core: 2. Of those that a mesh axis runs over, the one named last changes fastest.
Arguments:
- queries: bfloat16 [12288, 4096], P('section', 'head'), may hold values from -20 to 20
- keys: bfloat16 [12288, 1024], P('section', 'head'), may hold values from -20 to 20
- values: bfloat16 [12288, 1024], P('section', 'head'), may hold values from -6 to 6
- d_attn: bfloat16 [12288, 4096], P('section', 'head'), may hold values from -72 to 72
- d_out: bfloat16 [12288, 4096], P('section', 'head'), may hold values from -6 to 6
- w_query: bfloat16 [4096, 4096], P(None, 'head'), may hold values from -0.09375 to 0.09375
- prefix_len: int32 [64], replicated, may hold values from 0 to 12096, as said below
Outputs:
- grad_prev: bfloat16 [12288, 4096], P('section', 'head')
Inputs may be any that keep to these rules, and one draw needn't show every extreme that they name: prefix_len[s] <= s * 192 for every slice s; the first slice's is 0 and the last slice's is 12096.
All inputs are finite; a program needn't handle non-finite values.
Results may differ from a plain program's by a relative error of at most 0.035.
Values may be sent and summed in bfloat16 or wider, within the bound.
No kernel may reach another device: no remote copies, remote signals or barrier semaphores. Data moves between devices by JAX's collectives and lax.ppermute only.
A program may use at most 64 MiB of HBM per device.

v0:
```python
import jax
import jax.numpy as jnp
from jax import lax
from jax.sharding import PartitionSpec as P

masked_score = -1e30
key_block = 512


def shifted(value, axis, steps):
    count = lax.axis_size(axis)
    first, last = (max(0, -steps), min(count, count - steps))
    return lax.ppermute(value, axis, [(source, source + steps) for source in range(first, last)])


def head_rows(matrix, head_count):
    row_count = matrix.shape[0]
    head_width = matrix.shape[1] // head_count
    return (
        matrix.reshape(row_count, head_count, head_width)
        .transpose(1, 0, 2)
        .reshape(head_count * row_count, head_width)
    )


def row_heads(matrix, head_count):
    row_count = matrix.shape[0] // head_count
    head_width = matrix.shape[1]
    return (
        matrix.reshape(head_count, row_count, head_width)
        .transpose(1, 0, 2)
        .reshape(row_count, head_count * head_width)
    )


def empty_state(slot_count, head_width):
    return (
        jnp.full((slot_count,), masked_score, jnp.float32),
        jnp.zeros((slot_count,), jnp.float32),
        jnp.zeros((slot_count,), jnp.float32),
        jnp.zeros((slot_count, head_width), jnp.float32),
        jnp.zeros((slot_count, head_width), jnp.float32),
    )


def absorb(running, query_set, key_part, value_part, first_key):
    query_rows, grad_rows, positions, lower_key, upper_key = query_set
    run_max, run_sum, run_delta, total_grad, total_key = running
    key_count = key_part.shape[0]
    key_position = first_key + jnp.arange(key_count, dtype=jnp.int32)
    allowed = (
        (key_position[None, :] >= lower_key)
        & (key_position[None, :] < upper_key)
        & (key_position[None, :] <= positions[:, None])
    )
    scores = lax.dot_general(
        query_rows, key_part, (((1,), (1,)), ((), ())), preferred_element_type=jnp.float32
    ) * query_rows.shape[1] ** (-0.5)
    scores = jnp.where(allowed, scores, masked_score)
    new_max = jnp.maximum(run_max, jnp.max(scores, axis=1))
    factor = jnp.exp(run_max - new_max)
    weights = jnp.where(allowed, jnp.exp(scores - new_max[:, None]), 0.0)
    grad_prob = lax.dot_general(
        grad_rows, value_part, (((1,), (1,)), ((), ())), preferred_element_type=jnp.float32
    )
    weighted = weights * grad_prob
    run_sum = run_sum * factor + jnp.sum(weights, axis=1)
    run_delta = run_delta * factor + jnp.sum(weighted, axis=1)
    total_grad = total_grad * factor[:, None] + jnp.dot(
        weighted.astype(jnp.bfloat16), key_part, preferred_element_type=jnp.float32
    )
    total_key = total_key * factor[:, None] + jnp.dot(
        weights.astype(jnp.bfloat16), key_part, preferred_element_type=jnp.float32
    )
    return (new_max, run_sum, run_delta, total_grad, total_key)


def sweep_keys(running, query_set, portion, anchor):
    piece_rows = portion.shape[0]
    block_count = (piece_rows + key_block - 1) // key_block
    head_width = portion.shape[1] // 2
    lower_key = query_set[3]
    upper_key = jnp.minimum(query_set[4], anchor + piece_rows)
    clipped_set = (query_set[0], query_set[1], query_set[2], lower_key, upper_key)

    def visit_block(turn_index, held):
        offset = turn_index * key_block
        sub_block = lax.dynamic_slice_in_dim(portion, offset, key_block, 0)
        within = (offset + key_block > lower_key) & (offset < upper_key)
        return lax.cond(
            within,
            lambda inner: absorb(
                inner, clipped_set, sub_block[:, :head_width], sub_block[:, head_width:], offset
            ),
            lambda inner: inner,
            held,
        )

    return lax.fori_loop(0, block_count, visit_block, running)


def shards(queries, keys, values, d_attn, d_out, w_query, prefix_len):
    row_count = queries.shape[0]
    head_width = keys.shape[1]
    head_count = queries.shape[1] // head_width
    slot_count = head_count * row_count
    section_count = lax.axis_size("section")
    section_id = lax.axis_index("section")
    key_values = jnp.concatenate([keys, values], axis=1)
    base_row = section_id * row_count
    positions = jnp.tile(base_row + jnp.arange(row_count, dtype=jnp.int32), head_count)
    lower_key = jnp.maximum(base_row - prefix_len[section_id], 0)
    upper_key = jnp.minimum(base_row + row_count, section_count * row_count)
    own_set = (
        head_rows(queries, head_count),
        head_rows(d_attn, head_count),
        positions,
        lower_key,
        upper_key,
    )
    attention_state = sweep_keys(
        empty_state(slot_count, head_width),
        own_set,
        lax.all_gather(key_values, "section", axis=0, tiled=True),
        jnp.int32(0),
    )
    run_max, run_sum, run_delta, total_grad, total_key = attention_state
    delta_rows = run_delta / run_sum
    query_grad = (
        (total_grad - delta_rows[:, None] * total_key) / run_sum[:, None] * head_width ** (-0.5)
    )
    grad_query = row_heads(query_grad, head_count).astype(jnp.bfloat16)
    summed = lax.psum_scatter(
        lax.dot_general(
            w_query, grad_query, (((1,), (1,)), ((), ())), preferred_element_type=jnp.float32
        ).astype(jnp.bfloat16),
        "head",
        scatter_dimension=0,
        tiled=True,
    ).astype(jnp.float32)
    hidden = (d_out.astype(jnp.float32) + summed.T).astype(jnp.bfloat16)
    return shifted(hidden, "section", -1)


def solution(mesh):
    placed = (
        P("section", "head"),
        P("section", "head"),
        P("section", "head"),
        P("section", "head"),
        P("section", "head"),
        P(None, "head"),
        P(),
    )
    return jax.shard_map(
        shards, mesh=mesh, in_specs=placed, out_specs=P("section", "head"), check_vma=False
    )
```

profile of v0, /device:TPU:24, one launch (start us, length us, event | category | flops | bytes accessed | tf_op | source)
XLA Modules:
  0.0 389.9 jit_solution(3691444782243468771)
XLA Ops:
  6.5 0.0 copy-start
  6.5 0.0 all-gather.2.cloned.1.call-start
  6.5 1.5 pad_maximum_fusion
  8.1 0.0 all-gather.2.cloned.1.call-update
  8.1 0.0 reduce-scatter.2.cloned.1.call-start
  8.1 1.3 dynamic_slice.15
  10.2 0.0 copy-done
  10.2 1.0 copy_bitcast_fusion
  11.2 152.1 %all-gather.2.cloned.1.call-done = bf16[12288,256]{1,0:T(8,128)(2,1)} async-done(((bf16[192,256]{1,0:T(8,128)(2,1)}), bf16[12288,256]{1,0:T(8,128)(2,1)}) %all-gather.2.cloned.1.call-update) | async-done | bytes 6291472 | tf_op jit(solution)/shard_map/all_gather | solution.py:124
  163.4 22.3 %while.22 = (s32[]{:T(128)}, f32[768]{0:T(1024)S(1)}, f32[768]{0:T(1024)S(1)}, f32[768]{0:T(1024)S(1)}, f32[768,128]{1,0:T(8,128)S(1)}, /*index=5*/f32[768,128]{...) while((s32[]{:T(128)}, f32[768]{0:T(1024)S(1)}, ...), condition=%wide.region_6.7_spmd.clone, body=%wide.region_0.6_spmd.clone.sunk | while | flops 411702016 | bytes 10460873 | solution.py:99
  164.3 7.0 %conditional.3 = ((f32[768]{0:T(1024)S(1)}, f32[768]{0:T(1024)S(1)}, f32[768]{0:T(1024)S(1)}, f32[768,128]{1,0:T(8,128)S(1)}, f32[768,128]{1,0:T(8,128)S(1)})) conditional(s32[]{:T(128)} %convert_element_type.62, (f32[768]{0:T(1024)S(1)}, f32[768]{0:T(1024)S(1)}, f32[768]{0:T(1024)S(1)}, f32[768,128]{1,0:T(8,128)S(1)}, ...), branch_computations={%region_1.0_spmd, %region_2.5_spmd} | conditional | flops 411702016 | bytes 10460546 | solution.py:90
  164.3 0.1 le.21
  164.4 1.4 fusion.16
  165.9 1.6 fusion.17
  167.5 0.5 fusion.11
  168.1 1.5 convolution_add_fusion.1
  169.6 1.8 convolution_add_fusion
  171.4 7.0 %conditional.3 = ((f32[768]{0:T(1024)S(1)}, f32[768]{0:T(1024)S(1)}, f32[768]{0:T(1024)S(1)}, f32[768,128]{1,0:T(8,128)S(1)}, f32[768,128]{1,0:T(8,128)S(1)})) conditional(s32[]{:T(128)} %convert_element_type.62, (f32[768]{0:T(1024)S(1)}, f32[768]{0:T(1024)S(1)}, f32[768]{0:T(1024)S(1)}, f32[768,128]{1,0:T(8,128)S(1)}, ...), branch_computations={%region_1.0_spmd, %region_2.5_spmd} | conditional | flops 411702016 | bytes 10460546 | solution.py:90
  171.4 0.1 le.21
  171.5 1.4 fusion.16
  173.0 1.6 fusion.17
  174.6 0.5 fusion.11
  175.1 1.5 convolution_add_fusion.1
  176.6 1.8 convolution_add_fusion
  178.4 7.0 %conditional.3 = ((f32[768]{0:T(1024)S(1)}, f32[768]{0:T(1024)S(1)}, f32[768]{0:T(1024)S(1)}, f32[768,128]{1,0:T(8,128)S(1)}, f32[768,128]{1,0:T(8,128)S(1)})) conditional(s32[]{:T(128)} %convert_element_type.62, (f32[768]{0:T(1024)S(1)}, f32[768]{0:T(1024)S(1)}, f32[768]{0:T(1024)S(1)}, f32[768,128]{1,0:T(8,128)S(1)}, ...), branch_computations={%region_1.0_spmd, %region_2.5_spmd} | conditional | flops 411702016 | bytes 10460546 | solution.py:90
  178.5 0.1 le.21
  178.6 1.4 fusion.16
  180.0 1.6 fusion.17
  181.7 0.5 fusion.11
  182.2 1.5 convolution_add_fusion.1
  183.7 1.8 convolution_add_fusion
  185.8 0.3 multiply_convert_fusion
  186.1 0.2 copy.12
  186.2 4.9 %fusion.12 = bf16[4096,192]{0,1:T(8,128)(2,1)} fusion(bf16[4096,512]{1,0:T(8,128)(2,1)} %param.16, bf16[24,8,4,128]{3,2,1,0:T(4,128)(2,1)S(1)} %bitcast.37), kind=kOutput, calls=%fused_computation.23 | convolution fusion | flops 806092800 | bytes 5963776 | tf_op jit(solution)/shard_map/dot_general | solution.py:134
  191.1 0.0 copy-start.1
  191.1 0.0 reduce-scatter.2.cloned.1.call-update
  191.1 180.8 %reduce-scatter.2.cloned.1.call-done = bf16[512,192]{0,1:T(8,128)(2,1)} async-done(((bf16[4096,192]{0,1:T(8,128)(2,1)}), bf16[512,192]{0,1:T(8,128)(2,1)}) %reduce-scatter.2.cloned.1.call-update) | async-done | bytes 196624 | tf_op jit(solution)/shard_map/reduce_scatter | solution.py:133
  372.0 0.0 copy-done.1
  372.0 1.0 fusion.13
  372.9 6.2 %collective-permute-start = (bf16[192,512]{1,0:T(8,128)(2,1)S(1)}, bf16[192,512]{1,0:T(8,128)(2,1)S(1)}, u32[]{:S(2)}, u32[]{:S(2)}) collective-permute-start(bf16[192,512]{1,0:T(8,128)(2,1)S(1)} %fusion.13), channel_id=1, source_target_pairs={{8,0},{16,8},{24,16},{32,24},{40,32},{48,40},{56,48},{64,56},{72,6... | collective-permute-start | bytes 589832 | tf_op jit(solution)/shard_map/ppermute | solution.py:13
  379.2 3.2 collective-permute-done
  382.3 0.7 copy.53
  (50 shorter events, 0.5 us)
Async XLA Ops:
  6.5 3.6 copy-start
  6.5 156.8 %all-gather.2.cloned.1.call-start = ((), (), s32[]{:S(2)}) async-start(), calls=%async_computation.1 | async-start | bytes 6389760 | tf_op jit(solution)/shard_map/all_gather | solution.py:124
  8.1 363.9 %reduce-scatter.2.cloned.1.call-start = ((), (), s32[]{:S(2)}) async-start(), calls=%async_computation.2 | async-start | bytes 1769472 | tf_op jit(solution)/shard_map/reduce_scatter | solution.py:133
  191.1 180.9 %copy-start.1 = (bf16[192,512]{1,0:T(8,128)(2,1)S(1)}, bf16[192,512]{1,0:T(8,128)(2,1)}, u32[]{:S(2)}) copy-start(bf16[192,512]{1,0:T(8,128)(2,1)} %param.15) | copy-start | bytes 589828
  372.9 9.4 %collective-permute-start = (bf16[192,512]{1,0:T(8,128)(2,1)S(1)}, bf16[192,512]{1,0:T(8,128)(2,1)S(1)}, u32[]{:S(2)}, u32[]{:S(2)}) collective-permute-start(bf16[192,512]{1,0:T(8,128)(2,1)S(1)} %fusion.13), channel_id=1, source_target_pairs={{8,0},{16,8},{24,16},{32,24},{40,32},{48,40},{56,48},{64,56},{72,6... | collective-permute-start | bytes 589832 | tf_op jit(solution)/shard_map/ppermute | solution.py:13
Sparse Core Ops, SparseCore 0:
  10.3 153.0 all-gather.1
  191.2 180.6 reduce-scatter.1
where the time goes:
time: 392 us; the launch traced here: 390 us
  waiting for transfers between devices  336 us (86%)
  matrix products  23.8 us (6%)
  between operations  14.2 us (4%)
  starting transfers between devices  6.27 us (2%)
  other arithmetic  4.38 us (1%)
    reduce_scatter x1, waiting for transfers between devices, shards(): lax.psum_scatter(lax.dot_general(w_query, grad_query, (((1,), (1,)), ((),...  181 us
    all_gather x1, waiting for transfers between devices, shards(): lax.all_gather(key_values, 'section', axis=0, tiled=True)  152 us
  transfers between devices with their start and end apart: 3, of which 3 were waited for; matrix products, arithmetic and copies ran while one was open for 1% of the time, Pallas kernels for 0%

commit v1 on v0

v1 whole, which is shorter than its diff:
```python
import functools
import math

import jax
import jax.numpy as jnp
from jax import lax
from jax.experimental import pallas as pl
from jax.experimental.pallas import tpu as pltpu
from jax.sharding import Mesh, PartitionSpec as P


ROWS = 192
WIDTH = 128
HEADS = 4
SLOTS = HEADS * ROWS
LOW = -1e30
SLACK = 8.0
SCALE = WIDTH ** -0.5
Y, Z, X, C = 4, 16, 4, 2


def attend(counts, group, offset, first, last, par_ref, pos_ref, *refs):
    refs = list(refs)
    q_ref, g_ref = refs[:2]
    kv_refs = refs[2 : 2 + len(counts)]
    refs = refs[2 + len(counts) :]
    if not first:
        sw_in, sp_in, st_in = refs[:3]
        refs = refs[3:]
    outs = refs[: 1 if last else 3]
    slot_pos, buf, q_s, g_s, m_s, w_s, p_s = refs[1 if last else 3 :]
    base = par_ref[0]
    lo = par_ref[1]

    for h in range(HEADS):
        rows = pl.ds(h * ROWS, ROWS)
        cols = pl.ds(h * WIDTH, WIDTH)
        scaled = q_ref[:, cols].astype(jnp.float32) * (SCALE * math.log2(math.e))
        high = scaled.astype(jnp.bfloat16)
        q_s[rows, :WIDTH] = high
        q_s[rows, WIDTH:] = (scaled - high.astype(jnp.float32)).astype(jnp.bfloat16)
        g_s[rows, :] = g_ref[:, cols]
    if first:
        m_s[...] = jnp.full((SLOTS, WIDTH), LOW, jnp.float32)
        w_s[...] = jnp.zeros((SLOTS, 2 * WIDTH), jnp.float32)
        p_s[...] = jnp.zeros((SLOTS, 2 * WIDTH), jnp.float32)
    else:
        st = st_in[...]
        shape = (SLOTS, WIDTH)
        m_s[...] = jnp.broadcast_to(st[:, 0:1], shape)
        p_s[:, :WIDTH] = sp_in[...]
        p_s[:, WIDTH:] = jnp.broadcast_to(st[:, 64:65], shape)
        w_s[:, :WIDTH] = sw_in[...]
        w_s[:, WIDTH:] = jnp.broadcast_to(st[:, 127:128], shape)

    def collect(used, chosen_of):
        at = offset
        for ref, n in zip(kv_refs, counts):

            def place(j, slot, ref=ref, at=at):
                p = pos_ref[at + j]
                chosen = chosen_of(p)

                @pl.when(chosen)
                def _():
                    buf[slot] = ref[j]
                    slot_pos[slot] = p

                return slot + chosen.astype(jnp.int32)

            used = lax.fori_loop(0, n, place, used)
            at += n
        return used

    full = collect(jnp.int32(0), lambda p: (p >= lo) & (p < base))
    used = collect(
        full, lambda p: (p + ROWS > lo) & (p <= base) & ((p < lo) | (p == base))
    )
    groups = (used + group - 1) // group
    for j in range(group - 1):

        @pl.when(used + j < groups * group)
        def _():
            buf[used + j] = jnp.zeros((ROWS, 2 * WIDTH), jnp.bfloat16)
            slot_pos[used + j] = jnp.int32(1 << 30)

    contract = (((1,), (1,)), ((), ()))

    def visit(g, rows, masked):
        start = g * group
        kv = jnp.concatenate([buf[start + j] for j in range(group)], axis=0)
        k, v = kv[:, :WIDTH], kv[:, WIDTH:]
        kk = jnp.concatenate([k, k], axis=1)
        k1 = jnp.concatenate([k, jnp.ones_like(k)], axis=1)
        s = lax.dot_general(q_s[rows, :], kk, contract, preferred_element_type=jnp.float32)
        if masked:
            lane = lax.broadcasted_iota(jnp.int32, (1, ROWS), 1)
            key_at = jnp.concatenate([lane + slot_pos[start + j] for j in range(group)], axis=1)
            row = lax.broadcasted_iota(jnp.int32, (ROWS, group * ROWS), 0) + base
            inside = (key_at >= lo) & (key_at <= row)
            s = jnp.where(inside, s, LOW)
        top = jnp.max(s, axis=1, keepdims=True)

        @pl.when(jnp.max(top - m_s[rows, 0:1]) > SLACK)
        def _():
            old = m_s[rows, :]
            new = jnp.maximum(old, top)
            factor = jnp.exp2(old - new)[:, 0:1]
            m_s[rows, :] = new
            w_s[rows, :] = w_s[rows, :] * factor
            p_s[rows, :] = p_s[rows, :] * factor

        prob = jnp.exp2(s - m_s[rows, 0:1])
        if masked:
            prob = jnp.where(inside, prob, 0.0)
        dp = lax.dot_general(g_s[rows, :], v, contract, preferred_element_type=jnp.float32)
        w_s[rows, :] += jnp.dot(
            (prob * dp).astype(jnp.bfloat16), k1, preferred_element_type=jnp.float32
        )
        p_s[rows, :] += jnp.dot(prob.astype(jnp.bfloat16), k1, preferred_element_type=jnp.float32)

    @pl.loop(0, groups)
    def _(g):
        whole = (g + 1) * group <= full
        pl.when(whole)(lambda: visit(g, pl.ds(0, SLOTS), False))

        @pl.when(jnp.logical_not(whole))
        def _():
            @pl.loop(0, HEADS)
            def _(h):
                visit(g, pl.ds(pl.multiple_of(h * ROWS, ROWS), ROWS), True)

    if last:
        l = p_s[:, WIDTH:]
        l = jnp.where(l > 0.0, l, 1.0)
        delta = w_s[:, WIDTH:] / l
        grad = (w_s[:, :WIDTH] - delta * p_s[:, :WIDTH]) / l * SCALE
        for h in range(HEADS):
            outs[0][:, pl.ds(h * WIDTH, WIDTH)] = grad[h * ROWS : (h + 1) * ROWS].astype(jnp.bfloat16)
    else:
        sw_out, sp_out, st_out = outs
        sw_out[...] = w_s[:, :WIDTH]
        sp_out[...] = p_s[:, :WIDTH]
        lane = lax.broadcasted_iota(jnp.int32, (SLOTS, WIDTH), 1)
        st_out[...] = jnp.where(
            lane < 43, m_s[...], jnp.where(lane < 86, p_s[:, WIDTH:], w_s[:, WIDTH:])
        )


def attention(par, pos, offset, q, g, arrays, state, last):
    counts = tuple(a.shape[0] for a in arrays)
    first = state is None
    total = sum(counts)
    group = {4: 4, 12: 6}.get(total, 8)
    shape = jax.ShapeDtypeStruct((SLOTS, WIDTH), jnp.float32)
    out_shape = jax.ShapeDtypeStruct((ROWS, HEADS * WIDTH), jnp.bfloat16) if last else [shape] * 3
    operands = [q, g, *arrays] + ([] if first else list(state))
    vmem = pl.BlockSpec(memory_space=pltpu.VMEM)
    smem = pl.BlockSpec(memory_space=pltpu.SMEM)
    return pl.pallas_call(
        functools.partial(attend, counts, group, offset, first, last),
        in_specs=[smem, smem] + [vmem] * len(operands),
        out_specs=vmem if last else [vmem] * 3,
        out_shape=out_shape,
        scratch_shapes=[
            pltpu.SMEM((total + group,), jnp.int32),
            pltpu.VMEM((total + group, ROWS, 2 * WIDTH), jnp.bfloat16),
            pltpu.VMEM((SLOTS, 2 * WIDTH), jnp.bfloat16),
            pltpu.VMEM((SLOTS, WIDTH), jnp.bfloat16),
            pltpu.VMEM((SLOTS, WIDTH), jnp.float32),
            pltpu.VMEM((SLOTS, 2 * WIDTH), jnp.float32),
            pltpu.VMEM((SLOTS, 2 * WIDTH), jnp.float32),
        ],
        compiler_params=pltpu.CompilerParams(vmem_limit_bytes=24 << 20),
        cost_estimate=pl.CostEstimate(
            flops=8 * total * ROWS * SLOTS * WIDTH // 2,
            transcendentals=total * ROWS * SLOTS // 2,
            bytes_accessed=total * ROWS * 2 * WIDTH * 2 + 3 * SLOTS * WIDTH * 8,
        ),
        name="attend",
    )(par, pos, *operands)


def project_body(index_ref, gq_ref, w_ref, out_ref):
    grad_query = gq_ref[...]
    width = grad_query.shape[1]
    for i in range(X):
        block = pl.ds(pl.multiple_of(index_ref[i] * width, width), width)
        out_ref[i] = lax.dot_general(
            grad_query,
            w_ref[block, :],
            (((1,), (1,)), ((), ())),
            preferred_element_type=jnp.float32,
        ).astype(jnp.bfloat16)


def project(index, grad_query, w_query):
    vmem = pl.BlockSpec(memory_space=pltpu.VMEM)
    return pl.pallas_call(
        project_body,
        in_specs=[pl.BlockSpec(memory_space=pltpu.SMEM), vmem, vmem],
        out_specs=vmem,
        out_shape=jax.ShapeDtypeStruct((X, ROWS, grad_query.shape[1]), jnp.bfloat16),
        compiler_params=pltpu.CompilerParams(vmem_limit_bytes=16 << 20),
        name="project",
    )(index, grad_query, w_query)


def exchange(value, axis, mask):
    count = lax.axis_size(axis)
    return lax.ppermute(value, axis, [(i, i ^ mask) for i in range(count)])


def add(a, b):
    return (a.astype(jnp.float32) + b.astype(jnp.float32)).astype(jnp.bfloat16)


def reduce_heads(grad_query, w_query, d_out):
    x_id = lax.axis_index("x")
    core = lax.axis_index("core")
    order = jnp.arange(X, dtype=jnp.int32)
    order = x_id ^ (order ^ (order >> 1))
    sent = exchange(project(order * C + (1 - core), grad_query, w_query), "core", 1)
    held = add(project(order * C + core, grad_query, w_query), sent)
    total = held[0].astype(jnp.float32) + d_out.astype(jnp.float32)
    for i, mask in ((3, 2), (1, 1), (2, 3)):
        total = total + exchange(held[i], "x", mask).astype(jnp.float32)
    return total.astype(jnp.bfloat16)


def shards(queries, keys, values, d_attn, d_out, w_query, prefix_len):
    y_id = lax.axis_index("y")
    z_id = lax.axis_index("z")
    owner = y_id * Z + z_id + 1
    base = owner * ROWS
    reach = prefix_len[jnp.minimum(owner, Y * Z - 1)]
    lo = jnp.where(owner < Y * Z, jnp.maximum(base - reach, 0), 1 << 28)
    par = jnp.where(jnp.arange(2) == 0, base, lo).astype(jnp.int32)

    own = jnp.concatenate([queries, d_attn, d_out], axis=1)
    own = lax.ppermute(own, ("y", "z"), [(i + 1, i) for i in range(Y * Z - 1)])
    width = queries.shape[1]
    q, g, d_out = own[:, :width], own[:, width : 2 * width], own[:, 2 * width :]

    mine = lax.all_gather(jnp.concatenate([keys, values], axis=1), "y", axis=0)

    up = [(z, (z + 1) % Z) for z in range(Z)]
    down = [(z, (z - 1) % Z) for z in range(Z)]

    turn = jnp.arange(Z * Y, dtype=jnp.int32)
    hop = turn // Y
    hop = jnp.where(hop % 2 == 1, (hop + 1) // 2, Z - hop // 2)
    pos = ((z_id + Z - hop) % Z + turn % Y * Z) * ROWS

    half = Z // 2
    below = above = mine
    arrays, done = [mine], 0
    state = None
    for step in range(1, half + 1):
        last = step == half
        below = lax.ppermute(below[: Y // 2] if last else below, "z", up)
        above = lax.ppermute(above[Y // 2 :] if last else above, "z", down)
        if step % 2 == 0:
            state = attention(par, pos, done, q, g, arrays, state, False)
            done += sum(a.shape[0] for a in arrays)
            arrays = []
        arrays += [below, above]
    state = attention(par, pos, done, q, g, arrays, state, True)
    return reduce_heads(state, w_query, d_out)


def solution(mesh):
    fine = Mesh(mesh.devices.reshape(Y, Z, X, C), ("y", "z", "x", "core"))
    split = P(("y", "z"), ("x", "core"))
    placed = (split, split, split, split, split, P(None, ("x", "core")), P())

    return jax.shard_map(shards, mesh=fine, in_specs=placed, out_specs=split, check_vma=False)
```

time: 392 us -> 186 us (0.47)
  waiting for transfers between devices: 336 us -> 34 us
  starting transfers between devices: 6.27 us -> 76.2 us
  Pallas kernels: 0 us -> 51.9 us
  matrix products: 23.8 us -> 0 us
  blocking collectives: 0 us -> 14.9 us
  between operations: 14.2 us -> 1.06 us
    reduce_scatter x1 -> x0, waiting for transfers between devices: 181 us -> none  [shards(): lax.psum_scatter(lax.dot_general(w_query, grad_query, (((1,), (1,)), ((),...]
    all_gather x1 -> x0, waiting for transfers between devices: 152 us -> none  [shards(): lax.all_gather(key_values, 'section', axis=0, tiled=True)]
    ppermute x1 -> x21, starting transfers between devices: 6.22 us -> 76.2 us  [the longest x8 45.1 us: shards(): above = lax.ppermute(above[Y // 2:] if last else above, 'z', down)]
    pallas_call x0 -> x7, Pallas kernels: none -> 51.9 us  [the longest x5 49.1 us: attention(): pl.pallas_call(functools.partial(attend, counts, group, offset, first, la...]
    ppermute x1 -> x21, waiting for transfers between devices: 3.17 us -> 34 us  [the longest x8 24.4 us: shards(): above = lax.ppermute(above[Y // 2:] if last else above, 'z', down)]
    dot_general x13 -> x0, matrix products: 23.8 us -> none  [the longest x3 5.27 us: absorb(): jnp.dot(weights.astype(jnp.bfloat16), key_part, preferred_element_type=jn...]
    all_gather x0 -> x1, blocking collectives: none -> 14.9 us  [shards(): mine = lax.all_gather(jnp.concatenate([keys, values], axis=1), 'y', axis=0)]
  transfers between devices with their start and end apart: 3 -> 21, of which waited for: 3 -> 14; matrix products, arithmetic and copies ran while one was open for 1% -> 2% of each run, Pallas kernels for 0% -> 24%
where the time goes in v1:
time: 186 us; the launch traced here: 185 us
  starting transfers between devices  76.2 us (41%)
  Pallas kernels  51.9 us (28%)
  waiting for transfers between devices  34 us (18%)
  blocking collectives  14.9 us (8%)
  other arithmetic  4.81 us (3%)
  local copies, waits for them, and re-layouts  2.49 us (1%)
    pallas_call x5, Pallas kernels, attention(): pl.pallas_call(functools.partial(attend, counts, group, offset, first, la...  49.1 us
    ppermute x8, starting transfers between devices, shards(): above = lax.ppermute(above[Y // 2:] if last else above, 'z', down)  45.1 us
    ppermute x8, waiting for transfers between devices, shards(): above = lax.ppermute(above[Y // 2:] if last else above, 'z', down)  24.4 us
    ppermute x8, starting transfers between devices, shards(): below = lax.ppermute(below[:Y // 2] if last else below, 'z', up)  17.3 us
    all_gather x1, blocking collectives, shards(): mine = lax.all_gather(jnp.concatenate([keys, values], axis=1), 'y', axis=0)  14.9 us
    ppermute x4, starting transfers between devices, exchange(): return lax.ppermute(value, axis, [(i, i ^ mask) for i in range(count)])  11.9 us
    ppermute x4, waiting for transfers between devices, exchange(): return lax.ppermute(value, axis, [(i, i ^ mask) for i in range(count)])  7.52 us
  transfers between devices with their start and end apart: 21, of which 14 were waited for; matrix products, arithmetic and copies ran while one was open for 2% of the time, Pallas kernels for 24%

profile of v1, /device:TPU:24, one launch (start us, length us, event | category | flops | bytes accessed | tf_op | source)
XLA Modules:
  0.0 185.3 jit_solution(13650204168944252924)
XLA Ops:
  0.0 0.8 pad_maximum_fusion.1
  0.9 14.9 %all-gather = bf16[768,256]{1,0:T(8,128)(2,1)S(1)} all-gather(bf16[192,256]{1,0:T(8,128)(2,1)S(1)} %pad_maximum_fusion.1), channel_id=2, replica_groups=mesh['y'=4,'z'=16,'x'=4,'core'=2] {'y'}, dimensions={0}, use_global_device_ids=true | all-gather | bytes 491520 | tf_op jit(solution)/shard_map/all_gather | solution.py:245
  15.7 9.5 %collective-permute-start.9 = (bf16[4,192,256]{2,1,0:T(8,128)(2,1)S(1)}, bf16[4,192,256]{2,1,0:T(8,128)(2,1)S(1)}, u32[]{:S(2)}, u32[]{:S(2)}) collective-permute-start(bf16[4,192,256]{2,1,0:T(8,128)(2,1)S(1)} %bitcast.13), channel_id=1, source_target_pairs={{0,120},{8,0},{16,8},{24,16},{32,24},{40,32},{48,40},{56,48},{64,5... | collective-permute-start | bytes 1179656 | tf_op jit(solution)/shard_map/ppermute | solution.py:262
  25.2 1.9 %collective-permute-start.1 = (bf16[4,192,256]{2,1,0:T(8,128)(2,1)S(1)}, bf16[4,192,256]{2,1,0:T(8,128)(2,1)S(1)}, u32[]{:S(2)}, u32[]{:S(2)}) collective-permute-start(bf16[4,192,256]{2,1,0:T(8,128)(2,1)S(1)} %bitcast.14), channel_id=1, source_target_pairs={{0,8},{8,16},{16,24},{24,32},{32,40},{40,48},{48,56},{56,64},{64,7... | collective-permute-start | bytes 1179656 | tf_op jit(solution)/shard_map/ppermute | solution.py:261
  27.2 3.3 %collective-permute-done.9.refs_4_ = bf16[4,192,256]{2,1,0:T(8,128)(2,1)S(1)} collective-permute-done((bf16[4,192,256]{2,1,0:T(8,128)(2,1)S(1)}, bf16[4,192,256]{2,1,0:T(8,128)(2,1)S(1)}, u32[]{:S(2)}, u32[]{:S(2)}) %collective-permute-start.9) | collective-permute-done | bytes 393248 | tf_op jit(solution)/shard_map/ppermute | solution.py:262
  30.5 5.6 %collective-permute-start.10 = (bf16[4,192,256]{2,1,0:T(8,128)(2,1)S(1)}, bf16[4,192,256]{2,1,0:T(8,128)(2,1)S(1)}, u32[]{:S(2)}, u32[]{:S(2)}) collective-permute-start(bf16[4,192,256]{2,1,0:T(8,128)(2,1)S(1)} %collective-permute-done.9.refs_4_), channel_id=1, source_target_pairs={{0,120},{8,0},{16,8},{24,16},{32,24},{40,32},{48,40},{56,48},{64,5... | collective-permute-start | bytes 1179656 | tf_op jit(solution)/shard_map/ppermute | solution.py:262
  36.1 1.9 %collective-permute-start.2 = (bf16[4,192,256]{2,1,0:T(8,128)(2,1)S(1)}, bf16[4,192,256]{2,1,0:T(8,128)(2,1)S(1)}, u32[]{:S(2)}, u32[]{:S(2)}) collective-permute-start(bf16[4,192,256]{2,1,0:T(8,128)(2,1)S(1)} %collective-permute-done.1.refs_3_), channel_id=1, source_target_pairs={{0,8},{8,16},{16,24},{24,32},{32,40},{40,48},{48,56},{56,64},{64,7... | collective-permute-start | bytes 1179656 | tf_op jit(solution)/shard_map/ppermute | solution.py:261
  38.0 3.5 %collective-permute-done.10.refs_3_ = bf16[4,192,256]{2,1,0:T(8,128)(2,1)S(1)} collective-permute-done((bf16[4,192,256]{2,1,0:T(8,128)(2,1)S(1)}, bf16[4,192,256]{2,1,0:T(8,128)(2,1)S(1)}, u32[]{:S(2)}, u32[]{:S(2)}) %collective-permute-start.10) | collective-permute-done | bytes 393248 | tf_op jit(solution)/shard_map/ppermute | solution.py:262
  41.5 5.6 %collective-permute-start.11 = (bf16[4,192,256]{2,1,0:T(8,128)(2,1)S(1)}, bf16[4,192,256]{2,1,0:T(8,128)(2,1)S(1)}, u32[]{:S(2)}, u32[]{:S(2)}) collective-permute-start(bf16[4,192,256]{2,1,0:T(8,128)(2,1)S(1)} %collective-permute-done.10.refs_3_), channel_id=1, source_target_pairs={{0,120},{8,0},{16,8},{24,16},{32,24},{40,32},{48,40},{56,48},{64,5... | collective-permute-start | bytes 1179656 | tf_op jit(solution)/shard_map/ppermute | solution.py:262
  47.1 0.3 collective-permute-done.2.refs_2_
  47.4 1.9 %collective-permute-start.3 = (bf16[4,192,256]{2,1,0:T(8,128)(2,1)S(1)}, bf16[4,192,256]{2,1,0:T(8,128)(2,1)S(1)}, u32[]{:S(2)}, u32[]{:S(2)}) collective-permute-start(bf16[4,192,256]{2,1,0:T(8,128)(2,1)S(1)} %collective-permute-done.2.refs_2_), channel_id=1, source_target_pairs={{0,8},{8,16},{16,24},{24,32},{32,40},{40,48},{48,56},{56,64},{64,7... | collective-permute-start | bytes 1179656 | tf_op jit(solution)/shard_map/ppermute | solution.py:261
  49.3 4.3 %collective-permute-done.11.refs_5_ = bf16[4,192,256]{2,1,0:T(8,128)(2,1)S(1)} collective-permute-done((bf16[4,192,256]{2,1,0:T(8,128)(2,1)S(1)}, bf16[4,192,256]{2,1,0:T(8,128)(2,1)S(1)}, u32[]{:S(2)}, u32[]{:S(2)}) %collective-permute-start.11) | collective-permute-done | bytes 393248 | tf_op jit(solution)/shard_map/ppermute | solution.py:262
  53.6 5.6 %collective-permute-start.12 = (bf16[4,192,256]{2,1,0:T(8,128)(2,1)S(1)}, bf16[4,192,256]{2,1,0:T(8,128)(2,1)S(1)}, u32[]{:S(2)}, u32[]{:S(2)}) collective-permute-start(bf16[4,192,256]{2,1,0:T(8,128)(2,1)S(1)} %collective-permute-done.11.refs_5_), channel_id=1, source_target_pairs={{0,120},{8,0},{16,8},{24,16},{32,24},{40,32},{48,40},{56,48},{64,5... | collective-permute-start | bytes 1179656 | tf_op jit(solution)/shard_map/ppermute | solution.py:262
  59.2 0.6 collective-permute-done.3.refs_4_
  59.8 1.9 %collective-permute-start.4 = (bf16[4,192,256]{2,1,0:T(8,128)(2,1)S(1)}, bf16[4,192,256]{2,1,0:T(8,128)(2,1)S(1)}, u32[]{:S(2)}, u32[]{:S(2)}) collective-permute-start(bf16[4,192,256]{2,1,0:T(8,128)(2,1)S(1)} %collective-permute-done.3.refs_4_), channel_id=1, source_target_pairs={{0,8},{8,16},{16,24},{24,32},{32,40},{40,48},{48,56},{56,64},{64,7... | collective-permute-start | bytes 1179656 | tf_op jit(solution)/shard_map/ppermute | solution.py:261
  61.8 0.8 copy-done.1
  62.5 4.4 %collective-permute-done.12.refs_3_ = bf16[4,192,256]{2,1,0:T(8,128)(2,1)S(1)} collective-permute-done((bf16[4,192,256]{2,1,0:T(8,128)(2,1)S(1)}, bf16[4,192,256]{2,1,0:T(8,128)(2,1)S(1)}, u32[]{:S(2)}, u32[]{:S(2)}) %collective-permute-start.12) | collective-permute-done | bytes 393248 | tf_op jit(solution)/shard_map/ppermute | solution.py:262
  66.9 5.6 %collective-permute-start.13 = (bf16[4,192,256]{2,1,0:T(8,128)(2,1)S(1)}, bf16[4,192,256]{2,1,0:T(8,128)(2,1)S(1)}, u32[]{:S(2)}, u32[]{:S(2)}) collective-permute-start(bf16[4,192,256]{2,1,0:T(8,128)(2,1)S(1)} %collective-permute-done.12.refs_3_), channel_id=1, source_target_pairs={{0,120},{8,0},{16,8},{24,16},{32,24},{40,32},{48,40},{56,48},{64,5... | collective-permute-start | bytes 1179656 | tf_op jit(solution)/shard_map/ppermute | solution.py:262
  72.5 0.9 collective-permute-done.4.refs_2_
  73.4 1.9 %collective-permute-start.5 = (bf16[4,192,256]{2,1,0:T(8,128)(2,1)S(1)}, bf16[4,192,256]{2,1,0:T(8,128)(2,1)}, u32[]{:S(2)}, u32[]{:S(2)}) collective-permute-start(bf16[4,192,256]{2,1,0:T(8,128)(2,1)S(1)} %collective-permute-done.4.refs_2_), channel_id=1, source_target_pairs={{0,8},{8,16},{16,24},{24,32},{32,40},{40,48},{48,56},{56,64},{64,7... | collective-permute-start | bytes 1179656 | tf_op jit(solution)/shard_map/ppermute | solution.py:261
  75.3 2.0 %pad_maximum_fusion = bf16[192,1536]{1,0:T(8,128)(2,1)} fusion(bf16[192,512]{1,0:T(8,128)(2,1)} %param.11, bf16[192,512]{1,0:T(8,128)(2,1)} %param.10, bf16[192,512]{1,0:T(8,128)(2,1)} %param.7), kind=kLoop, calls=%fused_computation.1 | loop fusion | flops 1769472 | bytes 1179648 | tf_op jit(solution)/shard_map/concatenate | solution.py:240
  77.3 1.9 %collective-permute-start = (bf16[192,1536]{1,0:T(8,128)(2,1)}, bf16[192,1536]{1,0:T(8,128)(2,1)}, u32[]{:S(2)}, u32[]{:S(2)}) collective-permute-start(bf16[192,1536]{1,0:T(8,128)(2,1)} %pad_maximum_fusion), channel_id=1, source_target_pairs={{8,0},{16,8},{24,16},{32,24},{40,32},{48,40},{56,48},{64,56},{72,6... | collective-permute-start | bytes 1769480 | tf_op jit(solution)/shard_map/ppermute | solution.py:241
  79.2 2.8 %collective-permute-done.13.refs_5_ = bf16[4,192,256]{2,1,0:T(8,128)(2,1)S(1)} collective-permute-done((bf16[4,192,256]{2,1,0:T(8,128)(2,1)S(1)}, bf16[4,192,256]{2,1,0:T(8,128)(2,1)S(1)}, u32[]{:S(2)}, u32[]{:S(2)}) %collective-permute-start.13) | collective-permute-done | bytes 393248 | tf_op jit(solution)/shard_map/ppermute | solution.py:262
  82.0 5.6 %collective-permute-start.14 = (bf16[4,192,256]{2,1,0:T(8,128)(2,1)S(1)}, bf16[4,192,256]{2,1,0:T(8,128)(2,1)}, u32[]{:S(2)}, u32[]{:S(2)}) collective-permute-start(bf16[4,192,256]{2,1,0:T(8,128)(2,1)S(1)} %collective-permute-done.13.refs_5_), channel_id=1, source_target_pairs={{0,120},{8,0},{16,8},{24,16},{32,24},{40,32},{48,40},{56,48},{64,5... | collective-permute-start | bytes 1179656 | tf_op jit(solution)/shard_map/ppermute | solution.py:262
  87.9 1.9 %collective-permute-start.6 = (bf16[4,192,256]{2,1,0:T(8,128)(2,1)}, bf16[4,192,256]{2,1,0:T(8,128)(2,1)}, u32[]{:S(2)}, u32[]{:S(2)}) collective-permute-start(bf16[4,192,256]{2,1,0:T(8,128)(2,1)} %collective-permute-done.5.refs_4_), channel_id=1, source_target_pairs={{0,8},{8,16},{16,24},{24,32},{32,40},{40,48},{48,56},{56,64},{64,7... | collective-permute-start | bytes 1179656 | tf_op jit(solution)/shard_map/ppermute | solution.py:261
  89.8 0.6 dynamic_slice.3
  91.1 6.1 %collective-permute-done.14.refs_3_ = bf16[4,192,256]{2,1,0:T(8,128)(2,1)} collective-permute-done((bf16[4,192,256]{2,1,0:T(8,128)(2,1)S(1)}, bf16[4,192,256]{2,1,0:T(8,128)(2,1)}, u32[]{:S(2)}, u32[]{:S(2)}) %collective-permute-start.14) | collective-permute-done | bytes 393248 | tf_op jit(solution)/shard_map/ppermute | solution.py:262
  97.2 5.8 %collective-permute-start.15 = (bf16[4,192,256]{2,1,0:T(8,128)(2,1)}, bf16[4,192,256]{2,1,0:T(8,128)(2,1)S(1)}, u32[]{:S(2)}, u32[]{:S(2)}) collective-permute-start(bf16[4,192,256]{2,1,0:T(8,128)(2,1)} %collective-permute-done.14.refs_3_), channel_id=1, source_target_pairs={{0,120},{8,0},{16,8},{24,16},{32,24},{40,32},{48,40},{56,48},{64,5... | collective-permute-start | bytes 1179656 | tf_op jit(solution)/shard_map/ppermute | solution.py:262
  103.0 1.9 %collective-permute-start.7 = (bf16[4,192,256]{2,1,0:T(8,128)(2,1)}, bf16[4,192,256]{2,1,0:T(8,128)(2,1)S(1)}, u32[]{:S(2)}, u32[]{:S(2)}) collective-permute-start(bf16[4,192,256]{2,1,0:T(8,128)(2,1)} %collective-permute-done.6.refs_2_), channel_id=1, source_target_pairs={{0,8},{8,16},{16,24},{24,32},{32,40},{40,48},{48,56},{56,64},{64,7... | collective-permute-start | bytes 1179656 | tf_op jit(solution)/shard_map/ppermute | solution.py:261
  104.9 1.1 fusion.10
  106.0 9.9 %attend.5 = (f32[768,128]{1,0:T(8,128)S(1)}, f32[768,128]{1,0:T(8,128)S(1)}, f32[768,128]{1,0:T(8,128)S(1)}) custom-call(s32[2]{0:T(128)S(1)} %compare_select_fusion.3.par_ref, s32[64]{0:T(128)S(1)} %fusion.6.pos_ref, bf16[192,512]{1,0:T(8,128)(2,1)S(1)} %get-tuple-element.33.refs_0_, bf16[192,512]{1,0:T(8,128)(2,1)S(1)} %get-tuple-element.32.refs_1_, ...), custom_call_target="tpu_custom_call" | custom-call | flops 905969664 | bytes 3538944 | tf_op jit(solution)/shard_map/attend/pallas_call | solution.py:160
  115.9 10.8 %attend.6 = (f32[768,128]{1,0:T(8,128)S(1)}, f32[768,128]{1,0:T(8,128)S(1)}, f32[768,128]{1,0:T(8,128)S(1)}) custom-call(s32[2]{0:T(128)S(1)} %compare_select_fusion.3.par_ref, s32[64]{0:T(128)S(1)} %fusion.6.pos_ref, bf16[192,512]{1,0:T(8,128)(2,1)S(1)} %get-tuple-element.33.refs_0_, bf16[192,512]{1,0:T(8,128)(2,1)S(1)} %get-tuple-element.32.refs_1_, ...), custom_call_target="tpu_custom_call" | custom-call | flops 1207959552 | bytes 3932160 | tf_op jit(solution)/shard_map/attend/pallas_call | solution.py:160
  126.7 1.9 %collective-permute-start.16 = (bf16[2,192,256]{2,1,0:T(8,128)(2,1)S(1)}, bf16[2,192,256]{2,1,0:T(8,128)(2,1)S(1)}, u32[]{:S(2)}, u32[]{:S(2)}) collective-permute-start(bf16[2,192,256]{2,1,0:T(8,128)(2,1)S(1)} %slice.39), channel_id=1, source_target_pairs={{0,120},{8,0},{16,8},{24,16},{32,24},{40,32},{48,40},{56,48},{64,5... | collective-permute-start | bytes 589832 | tf_op jit(solution)/shard_map/ppermute | solution.py:262
  128.7 3.9 %collective-permute-start.8 = (bf16[2,192,256]{2,1,0:T(8,128)(2,1)S(1)}, bf16[2,192,256]{2,1,0:T(8,128)(2,1)S(1)}, u32[]{:S(2)}, u32[]{:S(2)}) collective-permute-start(bf16[2,192,256]{2,1,0:T(8,128)(2,1)S(1)} %slice.38), channel_id=1, source_target_pairs={{0,8},{8,16},{16,24},{24,32},{32,40},{40,48},{48,56},{56,64},{64,7... | collective-permute-start | bytes 589832 | tf_op jit(solution)/shard_map/ppermute | solution.py:261
  132.6 11.5 %attend.7 = (f32[768,128]{1,0:T(8,128)S(1)}, f32[768,128]{1,0:T(8,128)S(1)}, f32[768,128]{1,0:T(8,128)S(1)}) custom-call(s32[2]{0:T(128)S(1)} %compare_select_fusion.3.par_ref, s32[64]{0:T(128)S(1)} %fusion.6.pos_ref, bf16[192,512]{1,0:T(8,128)(2,1)S(1)} %get-tuple-element.33.refs_0_, bf16[192,512]{1,0:T(8,128)(2,1)S(1)} %get-tuple-element.32.refs_1_, ...), custom_call_target="tpu_custom_call" | custom-call | flops 1207959552 | bytes 3932160 | tf_op jit(solution)/shard_map/attend/pallas_call | solution.py:160
  144.1 11.5 %attend.8 = (f32[768,128]{1,0:T(8,128)S(1)}, f32[768,128]{1,0:T(8,128)S(1)}, f32[768,128]{1,0:T(8,128)S(1)}) custom-call(s32[2]{0:T(128)S(1)} %compare_select_fusion.3.par_ref, s32[64]{0:T(128)S(1)} %fusion.6.pos_ref, bf16[192,512]{1,0:T(8,128)(2,1)S(1)} %get-tuple-element.33.refs_0_, bf16[192,512]{1,0:T(8,128)(2,1)S(1)} %get-tuple-element.32.refs_1_, ...), custom_call_target="tpu_custom_call" | custom-call | flops 1207959552 | bytes 3932160 | tf_op jit(solution)/shard_map/attend/pallas_call | solution.py:160
  155.7 5.4 %attend.9.gq_ref = bf16[192,512]{1,0:T(8,128)(2,1)S(1)} custom-call(s32[2]{0:T(128)S(1)} %compare_select_fusion.3.par_ref, s32[64]{0:T(128)S(1)} %fusion.6.pos_ref, bf16[192,512]{1,0:T(8,128)(2,1)S(1)} %get-tuple-element.33.refs_0_, bf16[192,512]{1,0:T(8,128)(2,1)S(1)} %get-tuple-element.32.refs_1_, bf16[2,192,256]{2,1,0:T(8,128)(2,1)S(1)} %collective-permute-done.8.refs_2_, ...), custom_call_target="tpu_custom_call" | custom-call | flops 301989888 | bytes 2752512 | tf_op jit(solution)/shard_map/attend/pallas_call | solution.py:160
  161.1 1.4 project.3
  162.5 1.9 %collective-permute-start.17 = (bf16[4,192,512]{2,1,0:T(8,128)(2,1)S(1)}, bf16[4,192,512]{2,1,0:T(8,128)(2,1)S(1)}, u32[]{:S(2)}, u32[]{:S(2)}) collective-permute-start(bf16[4,192,512]{2,1,0:T(8,128)(2,1)S(1)} %project.3), channel_id=1, source_target_pairs={{0,1},{1,0},{2,3},{3,2},{4,5},{5,4},{6,7},{7,6},{8,9},{9,8},{10,11... | collective-permute-start | bytes 2359304 | tf_op jit(solution)/shard_map/ppermute | solution.py:211
  164.4 1.4 project.2
  165.8 0.8 collective-permute-done.17
  166.9 5.0 %collective-permute-start.18 = (bf16[192,512]{1,0:T(8,128)(2,1)S(1)}, bf16[192,512]{1,0:T(8,128)(2,1)S(1)}, u32[]{:S(2)}, u32[]{:S(2)}) collective-permute-start(bf16[192,512]{1,0:T(8,128)(2,1)S(1)} %get-tuple-element.29), channel_id=1, source_target_pairs={{0,4},{2,6},{4,0},{6,2},{1,5},{3,7},{5,1},{7,3},{8,12},{10,14},{12... | collective-permute-start | bytes 589832 | tf_op jit(solution)/shard_map/ppermute | solution.py:211
  171.9 2.1 %collective-permute-start.19 = (bf16[192,512]{1,0:T(8,128)(2,1)S(1)}, bf16[192,512]{1,0:T(8,128)(2,1)S(1)}, u32[]{:S(2)}, u32[]{:S(2)}) collective-permute-start(bf16[192,512]{1,0:T(8,128)(2,1)S(1)} %get-tuple-element.31), channel_id=1, source_target_pairs={{0,2},{2,0},{4,6},{6,4},{1,3},{3,1},{5,7},{7,5},{8,10},{10,8},{12,... | collective-permute-start | bytes 589832 | tf_op jit(solution)/shard_map/ppermute | solution.py:211
  174.0 2.9 %collective-permute-start.20 = (bf16[192,512]{1,0:T(8,128)(2,1)S(1)}, bf16[192,512]{1,0:T(8,128)(2,1)S(1)}, u32[]{:S(2)}, u32[]{:S(2)}) collective-permute-start(bf16[192,512]{1,0:T(8,128)(2,1)S(1)} %get-tuple-element.30), channel_id=1, source_target_pairs={{0,6},{2,4},{4,2},{6,0},{1,7},{3,5},{5,3},{7,1},{8,14},{10,12},{12... | collective-permute-start | bytes 589832 | tf_op jit(solution)/shard_map/ppermute | solution.py:211
  176.9 0.8 collective-permute-done.18
  177.7 3.5 %collective-permute-done.19 = bf16[192,512]{1,0:T(8,128)(2,1)S(1)} collective-permute-done((bf16[192,512]{1,0:T(8,128)(2,1)S(1)}, bf16[192,512]{1,0:T(8,128)(2,1)S(1)}, u32[]{:S(2)}, u32[]{:S(2)}) %collective-permute-start.19) | collective-permute-done | bytes 196640 | tf_op jit(solution)/shard_map/ppermute | solution.py:211
  181.2 2.4 %collective-permute-done.20 = bf16[192,512]{1,0:T(8,128)(2,1)S(1)} collective-permute-done((bf16[192,512]{1,0:T(8,128)(2,1)S(1)}, bf16[192,512]{1,0:T(8,128)(2,1)S(1)}, u32[]{:S(2)}, u32[]{:S(2)}) %collective-permute-start.20) | collective-permute-done | bytes 196640 | tf_op jit(solution)/shard_map/ppermute | solution.py:211
  183.6 1.7 fusion.3
  (23 shorter events, 0.7 us)
Async XLA Ops:
  0.0 89.8 %copy-start.3 = (s32[64]{0:T(128)S(1)}, s32[64]{0:T(128)}, u32[]{:S(2)}) copy-start(s32[64]{0:T(128)} %param.13) | copy-start | bytes 772
  15.7 14.8 %collective-permute-start.9 = (bf16[4,192,256]{2,1,0:T(8,128)(2,1)S(1)}, bf16[4,192,256]{2,1,0:T(8,128)(2,1)S(1)}, u32[]{:S(2)}, u32[]{:S(2)}) collective-permute-start(bf16[4,192,256]{2,1,0:T(8,128)(2,1)S(1)} %bitcast.13), channel_id=1, source_target_pairs={{0,120},{8,0},{16,8},{24,16},{32,24},{40,32},{48,40},{56,48},{64,5... | collective-permute-start | bytes 1179656 | tf_op jit(solution)/shard_map/ppermute | solution.py:262
  25.2 10.9 %collective-permute-start.1 = (bf16[4,192,256]{2,1,0:T(8,128)(2,1)S(1)}, bf16[4,192,256]{2,1,0:T(8,128)(2,1)S(1)}, u32[]{:S(2)}, u32[]{:S(2)}) collective-permute-start(bf16[4,192,256]{2,1,0:T(8,128)(2,1)S(1)} %bitcast.14), channel_id=1, source_target_pairs={{0,8},{8,16},{16,24},{24,32},{32,40},{40,48},{48,56},{56,64},{64,7... | collective-permute-start | bytes 1179656 | tf_op jit(solution)/shard_map/ppermute | solution.py:261
  30.5 11.0 %collective-permute-start.10 = (bf16[4,192,256]{2,1,0:T(8,128)(2,1)S(1)}, bf16[4,192,256]{2,1,0:T(8,128)(2,1)S(1)}, u32[]{:S(2)}, u32[]{:S(2)}) collective-permute-start(bf16[4,192,256]{2,1,0:T(8,128)(2,1)S(1)} %collective-permute-done.9.refs_4_), channel_id=1, source_target_pairs={{0,120},{8,0},{16,8},{24,16},{32,24},{40,32},{48,40},{56,48},{64,5... | collective-permute-start | bytes 1179656 | tf_op jit(solution)/shard_map/ppermute | solution.py:262
  36.1 11.3 %collective-permute-start.2 = (bf16[4,192,256]{2,1,0:T(8,128)(2,1)S(1)}, bf16[4,192,256]{2,1,0:T(8,128)(2,1)S(1)}, u32[]{:S(2)}, u32[]{:S(2)}) collective-permute-start(bf16[4,192,256]{2,1,0:T(8,128)(2,1)S(1)} %collective-permute-done.1.refs_3_), channel_id=1, source_target_pairs={{0,8},{8,16},{16,24},{24,32},{32,40},{40,48},{48,56},{56,64},{64,7... | collective-permute-start | bytes 1179656 | tf_op jit(solution)/shard_map/ppermute | solution.py:261
  41.5 12.1 %collective-permute-start.11 = (bf16[4,192,256]{2,1,0:T(8,128)(2,1)S(1)}, bf16[4,192,256]{2,1,0:T(8,128)(2,1)S(1)}, u32[]{:S(2)}, u32[]{:S(2)}) collective-permute-start(bf16[4,192,256]{2,1,0:T(8,128)(2,1)S(1)} %collective-permute-done.10.refs_3_), channel_id=1, source_target_pairs={{0,120},{8,0},{16,8},{24,16},{32,24},{40,32},{48,40},{56,48},{64,5... | collective-permute-start | bytes 1179656 | tf_op jit(solution)/shard_map/ppermute | solution.py:262
  47.4 12.4 %collective-permute-start.3 = (bf16[4,192,256]{2,1,0:T(8,128)(2,1)S(1)}, bf16[4,192,256]{2,1,0:T(8,128)(2,1)S(1)}, u32[]{:S(2)}, u32[]{:S(2)}) collective-permute-start(bf16[4,192,256]{2,1,0:T(8,128)(2,1)S(1)} %collective-permute-done.2.refs_2_), channel_id=1, source_target_pairs={{0,8},{8,16},{16,24},{24,32},{32,40},{40,48},{48,56},{56,64},{64,7... | collective-permute-start | bytes 1179656 | tf_op jit(solution)/shard_map/ppermute | solution.py:261
  53.6 13.3 %collective-permute-start.12 = (bf16[4,192,256]{2,1,0:T(8,128)(2,1)S(1)}, bf16[4,192,256]{2,1,0:T(8,128)(2,1)S(1)}, u32[]{:S(2)}, u32[]{:S(2)}) collective-permute-start(bf16[4,192,256]{2,1,0:T(8,128)(2,1)S(1)} %collective-permute-done.11.refs_5_), channel_id=1, source_target_pairs={{0,120},{8,0},{16,8},{24,16},{32,24},{40,32},{48,40},{56,48},{64,5... | collective-permute-start | bytes 1179656 | tf_op jit(solution)/shard_map/ppermute | solution.py:262
  59.8 13.6 %collective-permute-start.4 = (bf16[4,192,256]{2,1,0:T(8,128)(2,1)S(1)}, bf16[4,192,256]{2,1,0:T(8,128)(2,1)S(1)}, u32[]{:S(2)}, u32[]{:S(2)}) collective-permute-start(bf16[4,192,256]{2,1,0:T(8,128)(2,1)S(1)} %collective-permute-done.3.refs_4_), channel_id=1, source_target_pairs={{0,8},{8,16},{16,24},{24,32},{32,40},{40,48},{48,56},{56,64},{64,7... | collective-permute-start | bytes 1179656 | tf_op jit(solution)/shard_map/ppermute | solution.py:261
  61.7 0.8 copy-start.1
  66.9 15.1 %collective-permute-start.13 = (bf16[4,192,256]{2,1,0:T(8,128)(2,1)S(1)}, bf16[4,192,256]{2,1,0:T(8,128)(2,1)S(1)}, u32[]{:S(2)}, u32[]{:S(2)}) collective-permute-start(bf16[4,192,256]{2,1,0:T(8,128)(2,1)S(1)} %collective-permute-done.12.refs_3_), channel_id=1, source_target_pairs={{0,120},{8,0},{16,8},{24,16},{32,24},{40,32},{48,40},{56,48},{64,5... | collective-permute-start | bytes 1179656 | tf_op jit(solution)/shard_map/ppermute | solution.py:262
  73.4 14.5 %collective-permute-start.5 = (bf16[4,192,256]{2,1,0:T(8,128)(2,1)S(1)}, bf16[4,192,256]{2,1,0:T(8,128)(2,1)}, u32[]{:S(2)}, u32[]{:S(2)}) collective-permute-start(bf16[4,192,256]{2,1,0:T(8,128)(2,1)S(1)} %collective-permute-done.4.refs_2_), channel_id=1, source_target_pairs={{0,8},{8,16},{16,24},{24,32},{32,40},{40,48},{48,56},{56,64},{64,7... | collective-permute-start | bytes 1179656 | tf_op jit(solution)/shard_map/ppermute | solution.py:261
  77.3 27.6 %collective-permute-start = (bf16[192,1536]{1,0:T(8,128)(2,1)}, bf16[192,1536]{1,0:T(8,128)(2,1)}, u32[]{:S(2)}, u32[]{:S(2)}) collective-permute-start(bf16[192,1536]{1,0:T(8,128)(2,1)} %pad_maximum_fusion), channel_id=1, source_target_pairs={{8,0},{16,8},{24,16},{32,24},{40,32},{48,40},{56,48},{64,56},{72,6... | collective-permute-start | bytes 1769480 | tf_op jit(solution)/shard_map/ppermute | solution.py:241
  82.0 15.2 %collective-permute-start.14 = (bf16[4,192,256]{2,1,0:T(8,128)(2,1)S(1)}, bf16[4,192,256]{2,1,0:T(8,128)(2,1)}, u32[]{:S(2)}, u32[]{:S(2)}) collective-permute-start(bf16[4,192,256]{2,1,0:T(8,128)(2,1)S(1)} %collective-permute-done.13.refs_5_), channel_id=1, source_target_pairs={{0,120},{8,0},{16,8},{24,16},{32,24},{40,32},{48,40},{56,48},{64,5... | collective-permute-start | bytes 1179656 | tf_op jit(solution)/shard_map/ppermute | solution.py:262
  87.9 15.1 %collective-permute-start.6 = (bf16[4,192,256]{2,1,0:T(8,128)(2,1)}, bf16[4,192,256]{2,1,0:T(8,128)(2,1)}, u32[]{:S(2)}, u32[]{:S(2)}) collective-permute-start(bf16[4,192,256]{2,1,0:T(8,128)(2,1)} %collective-permute-done.5.refs_4_), channel_id=1, source_target_pairs={{0,8},{8,16},{16,24},{24,32},{32,40},{40,48},{48,56},{56,64},{64,7... | collective-permute-start | bytes 1179656 | tf_op jit(solution)/shard_map/ppermute | solution.py:261
  97.2 29.5 %collective-permute-start.15 = (bf16[4,192,256]{2,1,0:T(8,128)(2,1)}, bf16[4,192,256]{2,1,0:T(8,128)(2,1)S(1)}, u32[]{:S(2)}, u32[]{:S(2)}) collective-permute-start(bf16[4,192,256]{2,1,0:T(8,128)(2,1)} %collective-permute-done.14.refs_3_), channel_id=1, source_target_pairs={{0,120},{8,0},{16,8},{24,16},{32,24},{40,32},{48,40},{56,48},{64,5... | collective-permute-start | bytes 1179656 | tf_op jit(solution)/shard_map/ppermute | solution.py:262
  103.0 25.7 %collective-permute-start.7 = (bf16[4,192,256]{2,1,0:T(8,128)(2,1)}, bf16[4,192,256]{2,1,0:T(8,128)(2,1)S(1)}, u32[]{:S(2)}, u32[]{:S(2)}) collective-permute-start(bf16[4,192,256]{2,1,0:T(8,128)(2,1)} %collective-permute-done.6.refs_2_), channel_id=1, source_target_pairs={{0,8},{8,16},{16,24},{24,32},{32,40},{40,48},{48,56},{56,64},{64,7... | collective-permute-start | bytes 1179656 | tf_op jit(solution)/shard_map/ppermute | solution.py:261
  106.0 9.9 %copy-start.2 = (bf16[4,192,256]{2,1,0:T(8,128)(2,1)S(1)}, bf16[4,192,256]{2,1,0:T(8,128)(2,1)}, u32[]{:S(2)}) copy-start(bf16[4,192,256]{2,1,0:T(8,128)(2,1)} %copy-done.1) | copy-start | bytes 1179652
  126.7 29.0 %collective-permute-start.16 = (bf16[2,192,256]{2,1,0:T(8,128)(2,1)S(1)}, bf16[2,192,256]{2,1,0:T(8,128)(2,1)S(1)}, u32[]{:S(2)}, u32[]{:S(2)}) collective-permute-start(bf16[2,192,256]{2,1,0:T(8,128)(2,1)S(1)} %slice.39), channel_id=1, source_target_pairs={{0,120},{8,0},{16,8},{24,16},{32,24},{40,32},{48,40},{56,48},{64,5... | collective-permute-start | bytes 589832 | tf_op jit(solution)/shard_map/ppermute | solution.py:262
  128.7 27.0 %collective-permute-start.8 = (bf16[2,192,256]{2,1,0:T(8,128)(2,1)S(1)}, bf16[2,192,256]{2,1,0:T(8,128)(2,1)S(1)}, u32[]{:S(2)}, u32[]{:S(2)}) collective-permute-start(bf16[2,192,256]{2,1,0:T(8,128)(2,1)S(1)} %slice.38), channel_id=1, source_target_pairs={{0,8},{8,16},{16,24},{24,32},{32,40},{40,48},{48,56},{56,64},{64,7... | collective-permute-start | bytes 589832 | tf_op jit(solution)/shard_map/ppermute | solution.py:261
  144.1 17.0 %copy-start = (bf16[4096,512]{1,0:T(8,128)(2,1)S(1)}, bf16[4096,512]{1,0:T(8,128)(2,1)}, u32[]{:S(2)}) copy-start(bf16[4096,512]{1,0:T(8,128)(2,1)} %w_ref.3) | copy-start | bytes 12582916
  162.5 4.2 %collective-permute-start.17 = (bf16[4,192,512]{2,1,0:T(8,128)(2,1)S(1)}, bf16[4,192,512]{2,1,0:T(8,128)(2,1)S(1)}, u32[]{:S(2)}, u32[]{:S(2)}) collective-permute-start(bf16[4,192,512]{2,1,0:T(8,128)(2,1)S(1)} %project.3), channel_id=1, source_target_pairs={{0,1},{1,0},{2,3},{3,2},{4,5},{5,4},{6,7},{7,6},{8,9},{9,8},{10,11... | collective-permute-start | bytes 2359304 | tf_op jit(solution)/shard_map/ppermute | solution.py:211
  166.9 10.8 %collective-permute-start.18 = (bf16[192,512]{1,0:T(8,128)(2,1)S(1)}, bf16[192,512]{1,0:T(8,128)(2,1)S(1)}, u32[]{:S(2)}, u32[]{:S(2)}) collective-permute-start(bf16[192,512]{1,0:T(8,128)(2,1)S(1)} %get-tuple-element.29), channel_id=1, source_target_pairs={{0,4},{2,6},{4,0},{6,2},{1,5},{3,7},{5,1},{7,3},{8,12},{10,14},{12... | collective-permute-start | bytes 589832 | tf_op jit(solution)/shard_map/ppermute | solution.py:211
  171.9 9.3 %collective-permute-start.19 = (bf16[192,512]{1,0:T(8,128)(2,1)S(1)}, bf16[192,512]{1,0:T(8,128)(2,1)S(1)}, u32[]{:S(2)}, u32[]{:S(2)}) collective-permute-start(bf16[192,512]{1,0:T(8,128)(2,1)S(1)} %get-tuple-element.31), channel_id=1, source_target_pairs={{0,2},{2,0},{4,6},{6,4},{1,3},{3,1},{5,7},{7,5},{8,10},{10,8},{12,... | collective-permute-start | bytes 589832 | tf_op jit(solution)/shard_map/ppermute | solution.py:211
  174.0 9.6 %collective-permute-start.20 = (bf16[192,512]{1,0:T(8,128)(2,1)S(1)}, bf16[192,512]{1,0:T(8,128)(2,1)S(1)}, u32[]{:S(2)}, u32[]{:S(2)}) collective-permute-start(bf16[192,512]{1,0:T(8,128)(2,1)S(1)} %get-tuple-element.30), channel_id=1, source_target_pairs={{0,6},{2,4},{4,2},{6,0},{1,7},{3,5},{5,3},{7,1},{8,14},{10,12},{12... | collective-permute-start | bytes 589832 | tf_op jit(solution)/shard_map/ppermute | solution.py:211

commit v2 on v1

--- a/solution.py
+++ b/solution.py
@@ -231,16 +231,11 @@
 def shards(queries, keys, values, d_attn, d_out, w_query, prefix_len):
     y_id = lax.axis_index("y")
     z_id = lax.axis_index("z")
-    owner = y_id * Z + z_id + 1
-    base = owner * ROWS
-    reach = prefix_len[jnp.minimum(owner, Y * Z - 1)]
-    lo = jnp.where(owner < Y * Z, jnp.maximum(base - reach, 0), 1 << 28)
+    section = y_id * Z + z_id
+    base = section * ROWS
+    lo = jnp.maximum(base - prefix_len[section], 0)
     par = jnp.where(jnp.arange(2) == 0, base, lo).astype(jnp.int32)
-
-    own = jnp.concatenate([queries, d_attn, d_out], axis=1)
-    own = lax.ppermute(own, ("y", "z"), [(i + 1, i) for i in range(Y * Z - 1)])
-    width = queries.shape[1]
-    q, g, d_out = own[:, :width], own[:, width : 2 * width], own[:, 2 * width :]
+    q, g = queries, d_attn
 
     mine = lax.all_gather(jnp.concatenate([keys, values], axis=1), "y", axis=0)
 
@@ -260,13 +255,14 @@
         last = step == half
         below = lax.ppermute(below[: Y // 2] if last else below, "z", up)
         above = lax.ppermute(above[Y // 2 :] if last else above, "z", down)
-        if step % 2 == 0:
+        if step % 2 == 0 or step == half - 1:
             state = attention(par, pos, done, q, g, arrays, state, False)
             done += sum(a.shape[0] for a in arrays)
             arrays = []
         arrays += [below, above]
     state = attention(par, pos, done, q, g, arrays, state, True)
-    return reduce_heads(state, w_query, d_out)
+    hidden = reduce_heads(state, w_query, d_out)
+    return lax.ppermute(hidden, ("y", "z"), [(i + 1, i) for i in range(Y * Z - 1)])
 
 
 def solution(mesh):

time: 186 us -> 195 us (1.048)
  waiting for transfers between devices: 34 us -> 41.9 us
  starting transfers between devices: 76.2 us -> 80.2 us
  other arithmetic: 4.81 us -> 1.23 us
  local copies, waits for them, and re-layouts: 2.49 us -> 5.36 us
  Pallas kernels: 51.9 us -> 49.5 us
    ppermute x1, waiting for transfers between devices: 0.01 us -> 5.47 us  [shards(): lax.ppermute(hidden, ('y', 'z'), [(i + 1, i) for i in range(Y * Z - 1)])]
    ppermute x1, starting transfers between devices: 1.91 us -> 6.21 us  [shards(): lax.ppermute(hidden, ('y', 'z'), [(i + 1, i) for i in range(Y * Z - 1)])]
    unnamed x8 -> x17, local copies, waits for them, and re-layouts: 0.78 us -> 4.05 us
    pallas_call x5 -> x6, Pallas kernels: 49.1 us -> 46.7 us  [attention(): pl.pallas_call(functools.partial(attend, counts, group, offset, first, la...]
    ppermute x8, waiting for transfers between devices: 2.05 us -> 4.34 us  [shards(): below = lax.ppermute(below[:Y // 2] if last else below, 'z', up)]
    concatenate x1 -> x0, other arithmetic: 1.98 us -> none  [shards(): own = jnp.concatenate([queries, d_attn, d_out], axis=1)]
  transfers between devices with their start and end apart: 21 -> 21, of which waited for: 14 -> 15; matrix products, arithmetic and copies ran while one was open for 2% -> 1% of each run, Pallas kernels for 24% -> 22%
where the time goes in v2:
time: 195 us; the launch traced here: 194 us
  starting transfers between devices  80.2 us (41%)
  Pallas kernels  49.5 us (25%)
  waiting for transfers between devices  41.9 us (21%)
  blocking collectives  14.9 us (8%)
  local copies, waits for them, and re-layouts  5.36 us (3%)
    pallas_call x6, Pallas kernels, attention(): pl.pallas_call(functools.partial(attend, counts, group, offset, first, la...  46.7 us
    ppermute x8, starting transfers between devices, shards(): above = lax.ppermute(above[Y // 2:] if last else above, 'z', down)  45.7 us
    ppermute x8, waiting for transfers between devices, shards(): above = lax.ppermute(above[Y // 2:] if last else above, 'z', down)  24.6 us
    ppermute x8, starting transfers between devices, shards(): below = lax.ppermute(below[:Y // 2] if last else below, 'z', up)  16.6 us
    all_gather x1, blocking collectives, shards(): mine = lax.all_gather(jnp.concatenate([keys, values], axis=1), 'y', axis=0)  14.9 us
    ppermute x4, starting transfers between devices, exchange(): return lax.ppermute(value, axis, [(i, i ^ mask) for i in range(count)])  11.7 us
    ppermute x4, waiting for transfers between devices, exchange(): return lax.ppermute(value, axis, [(i, i ^ mask) for i in range(count)])  7.51 us
    ppermute x1, starting transfers between devices, shards(): lax.ppermute(hidden, ('y', 'z'), [(i + 1, i) for i in range(Y * Z - 1)])  6.21 us
  transfers between devices with their start and end apart: 21, of which 15 were waited for; matrix products, arithmetic and copies ran while one was open for 1% of the time, Pallas kernels for 22%

profile of v2, /device:TPU:24, one launch (start us, length us, event | category | flops | bytes accessed | tf_op | source)
XLA Modules:
  0.0 194.2 jit_solution(9512484343178322227)
XLA Ops:
  0.0 0.8 pad_maximum_fusion
  0.8 14.9 %all-gather = bf16[768,256]{1,0:T(8,128)(2,1)S(1)} all-gather(bf16[192,256]{1,0:T(8,128)(2,1)S(1)} %pad_maximum_fusion), channel_id=2, replica_groups=mesh['y'=4,'z'=16,'x'=4,'core'=2] {'y'}, dimensions={0}, use_global_device_ids=true | all-gather | bytes 491520 | tf_op jit(solution)/shard_map/all_gather | solution.py:240
  15.7 9.5 %collective-permute-start.8 = (bf16[4,192,256]{2,1,0:T(8,128)(2,1)S(1)}, bf16[4,192,256]{2,1,0:T(8,128)(2,1)S(1)}, u32[]{:S(2)}, u32[]{:S(2)}) collective-permute-start(bf16[4,192,256]{2,1,0:T(8,128)(2,1)S(1)} %bitcast.13), channel_id=1, source_target_pairs={{0,120},{8,0},{16,8},{24,16},{32,24},{40,32},{48,40},{56,48},{64,5... | collective-permute-start | bytes 1179656 | tf_op jit(solution)/shard_map/ppermute | solution.py:257
  25.2 1.9 collective-permute-start
  27.1 3.3 %collective-permute-done.8.refs_4_ = bf16[4,192,256]{2,1,0:T(8,128)(2,1)S(1)} collective-permute-done((bf16[4,192,256]{2,1,0:T(8,128)(2,1)S(1)}, bf16[4,192,256]{2,1,0:T(8,128)(2,1)S(1)}, u32[]{:S(2)}, u32[]{:S(2)}) %collective-permute-start.8) | collective-permute-done | bytes 393248 | tf_op jit(solution)/shard_map/ppermute | solution.py:257
  30.5 5.6 %collective-permute-start.9 = (bf16[4,192,256]{2,1,0:T(8,128)(2,1)S(1)}, bf16[4,192,256]{2,1,0:T(8,128)(2,1)S(1)}, u32[]{:S(2)}, u32[]{:S(2)}) collective-permute-start(bf16[4,192,256]{2,1,0:T(8,128)(2,1)S(1)} %collective-permute-done.8.refs_4_), channel_id=1, source_target_pairs={{0,120},{8,0},{16,8},{24,16},{32,24},{40,32},{48,40},{56,48},{64,5... | collective-permute-start | bytes 1179656 | tf_op jit(solution)/shard_map/ppermute | solution.py:257
  36.1 1.9 collective-permute-start.1
  38.0 3.5 %collective-permute-done.9.refs_3_ = bf16[4,192,256]{2,1,0:T(8,128)(2,1)S(1)} collective-permute-done((bf16[4,192,256]{2,1,0:T(8,128)(2,1)S(1)}, bf16[4,192,256]{2,1,0:T(8,128)(2,1)S(1)}, u32[]{:S(2)}, u32[]{:S(2)}) %collective-permute-start.9) | collective-permute-done | bytes 393248 | tf_op jit(solution)/shard_map/ppermute | solution.py:257
  41.5 5.6 %collective-permute-start.10 = (bf16[4,192,256]{2,1,0:T(8,128)(2,1)S(1)}, bf16[4,192,256]{2,1,0:T(8,128)(2,1)S(1)}, u32[]{:S(2)}, u32[]{:S(2)}) collective-permute-start(bf16[4,192,256]{2,1,0:T(8,128)(2,1)S(1)} %collective-permute-done.9.refs_3_), channel_id=1, source_target_pairs={{0,120},{8,0},{16,8},{24,16},{32,24},{40,32},{48,40},{56,48},{64,5... | collective-permute-start | bytes 1179656 | tf_op jit(solution)/shard_map/ppermute | solution.py:257
  47.4 1.9 collective-permute-start.2
  49.3 4.3 %collective-permute-done.10.refs_5_ = bf16[4,192,256]{2,1,0:T(8,128)(2,1)S(1)} collective-permute-done((bf16[4,192,256]{2,1,0:T(8,128)(2,1)S(1)}, bf16[4,192,256]{2,1,0:T(8,128)(2,1)S(1)}, u32[]{:S(2)}, u32[]{:S(2)}) %collective-permute-start.10) | collective-permute-done | bytes 393248 | tf_op jit(solution)/shard_map/ppermute | solution.py:257
  53.6 5.6 %collective-permute-start.11 = (bf16[4,192,256]{2,1,0:T(8,128)(2,1)S(1)}, bf16[4,192,256]{2,1,0:T(8,128)(2,1)S(1)}, u32[]{:S(2)}, u32[]{:S(2)}) collective-permute-start(bf16[4,192,256]{2,1,0:T(8,128)(2,1)S(1)} %collective-permute-done.10.refs_5_), channel_id=1, source_target_pairs={{0,120},{8,0},{16,8},{24,16},{32,24},{40,32},{48,40},{56,48},{64,5... | collective-permute-start | bytes 1179656 | tf_op jit(solution)/shard_map/ppermute | solution.py:257
  60.0 1.9 collective-permute-start.3
  62.7 4.2 %collective-permute-done.11.refs_3_ = bf16[4,192,256]{2,1,0:T(8,128)(2,1)S(1)} collective-permute-done((bf16[4,192,256]{2,1,0:T(8,128)(2,1)S(1)}, bf16[4,192,256]{2,1,0:T(8,128)(2,1)S(1)}, u32[]{:S(2)}, u32[]{:S(2)}) %collective-permute-start.11) | collective-permute-done | bytes 393248 | tf_op jit(solution)/shard_map/ppermute | solution.py:257
  66.9 5.6 %collective-permute-start.12 = (bf16[4,192,256]{2,1,0:T(8,128)(2,1)S(1)}, bf16[4,192,256]{2,1,0:T(8,128)(2,1)}, u32[]{:S(2)}, u32[]{:S(2)}) collective-permute-start(bf16[4,192,256]{2,1,0:T(8,128)(2,1)S(1)} %collective-permute-done.11.refs_3_), channel_id=1, source_target_pairs={{0,120},{8,0},{16,8},{24,16},{32,24},{40,32},{48,40},{56,48},{64,5... | collective-permute-start | bytes 1179656 | tf_op jit(solution)/shard_map/ppermute | solution.py:257
  72.5 1.2 collective-permute-done.3.refs_2_
  73.7 1.9 collective-permute-start.4
  75.6 5.4 %collective-permute-done.12.refs_5_ = bf16[4,192,256]{2,1,0:T(8,128)(2,1)} collective-permute-done((bf16[4,192,256]{2,1,0:T(8,128)(2,1)S(1)}, bf16[4,192,256]{2,1,0:T(8,128)(2,1)}, u32[]{:S(2)}, u32[]{:S(2)}) %collective-permute-start.12) | collective-permute-done | bytes 393248 | tf_op jit(solution)/shard_map/ppermute | solution.py:257
  81.0 5.7 %collective-permute-start.13 = (bf16[4,192,256]{2,1,0:T(8,128)(2,1)}, bf16[4,192,256]{2,1,0:T(8,128)(2,1)S(1)}, u32[]{:S(2)}, u32[]{:S(2)}) collective-permute-start(bf16[4,192,256]{2,1,0:T(8,128)(2,1)} %collective-permute-done.12.refs_5_), channel_id=1, source_target_pairs={{0,120},{8,0},{16,8},{24,16},{32,24},{40,32},{48,40},{56,48},{64,5... | collective-permute-start | bytes 1179656 | tf_op jit(solution)/shard_map/ppermute | solution.py:257
  86.7 1.6 collective-permute-done.4.refs_4_
  88.4 1.9 collective-permute-start.5
  90.3 1.2 dynamic_slice.3
  92.2 3.8 %collective-permute-done.13.refs_3_ = bf16[4,192,256]{2,1,0:T(8,128)(2,1)S(1)} collective-permute-done((bf16[4,192,256]{2,1,0:T(8,128)(2,1)}, bf16[4,192,256]{2,1,0:T(8,128)(2,1)S(1)}, u32[]{:S(2)}, u32[]{:S(2)}) %collective-permute-start.13) | collective-permute-done | bytes 393248 | tf_op jit(solution)/shard_map/ppermute | solution.py:257
  96.0 5.5 %collective-permute-start.14 = (bf16[4,192,256]{2,1,0:T(8,128)(2,1)S(1)}, bf16[4,192,256]{2,1,0:T(8,128)(2,1)S(1)}, u32[]{:S(2)}, u32[]{:S(2)}) collective-permute-start(bf16[4,192,256]{2,1,0:T(8,128)(2,1)S(1)} %collective-permute-done.13.refs_3_), channel_id=1, source_target_pairs={{0,120},{8,0},{16,8},{24,16},{32,24},{40,32},{48,40},{56,48},{64,5... | collective-permute-start | bytes 1179656 | tf_op jit(solution)/shard_map/ppermute | solution.py:257
  101.5 1.2 collective-permute-done.5.refs_2_
  102.7 1.9 collective-permute-start.6
  104.7 0.9 copy-done.1
  105.6 0.9 copy-done.2
  106.5 9.9 %attend.6 = (f32[768,128]{1,0:T(8,128)S(1)}, f32[768,128]{1,0:T(8,128)S(1)}, f32[768,128]{1,0:T(8,128)S(1)}) custom-call(s32[2]{0:T(128)S(1)} %compare_select_fusion.3.par_ref, s32[64]{0:T(128)S(1)} %fusion.6.pos_ref, bf16[192,512]{1,0:T(8,128)(2,1)S(1)} %copy-done.1, bf16[192,512]{1,0:T(8,128)(2,1)S(1)} %copy-done.2, bf16[4,192,256]{2,1,0:T(8,128)(2,1)S(1)} %bitcast.15, ...), custom_call_target="tpu_custom_call" | custom-call | flops 905969664 | bytes 3538944 | tf_op jit(solution)/shard_map/attend/pallas_call | solution.py:160
  116.5 10.8 %attend.7 = (f32[768,128]{1,0:T(8,128)S(1)}, f32[768,128]{1,0:T(8,128)S(1)}, f32[768,128]{1,0:T(8,128)S(1)}) custom-call(s32[2]{0:T(128)S(1)} %compare_select_fusion.3.par_ref, s32[64]{0:T(128)S(1)} %fusion.6.pos_ref, bf16[192,512]{1,0:T(8,128)(2,1)S(1)} %copy-done.1, bf16[192,512]{1,0:T(8,128)(2,1)S(1)} %copy-done.2, ...), custom_call_target="tpu_custom_call" | custom-call | flops 1207959552 | bytes 3932160 | tf_op jit(solution)/shard_map/attend/pallas_call | solution.py:160
  127.3 2.7 %collective-permute-start.15 = (bf16[2,192,256]{2,1,0:T(8,128)(2,1)S(1)}, bf16[2,192,256]{2,1,0:T(8,128)(2,1)S(1)}, u32[]{:S(2)}, u32[]{:S(2)}) collective-permute-start(bf16[2,192,256]{2,1,0:T(8,128)(2,1)S(1)} %slice.25), channel_id=1, source_target_pairs={{0,120},{8,0},{16,8},{24,16},{32,24},{40,32},{48,40},{56,48},{64,5... | collective-permute-start | bytes 589832 | tf_op jit(solution)/shard_map/ppermute | solution.py:257
  130.0 3.2 %collective-permute-start.7 = (bf16[2,192,256]{2,1,0:T(8,128)(2,1)S(1)}, bf16[2,192,256]{2,1,0:T(8,128)(2,1)S(1)}, u32[]{:S(2)}, u32[]{:S(2)}) collective-permute-start(bf16[2,192,256]{2,1,0:T(8,128)(2,1)S(1)} %slice.24), channel_id=1, source_target_pairs={{0,8},{8,16},{16,24},{24,32},{32,40},{40,48},{48,56},{56,64},{64,7... | collective-permute-start | bytes 589832 | tf_op jit(solution)/shard_map/ppermute | solution.py:256
  133.2 5.8 %attend.8 = (f32[768,128]{1,0:T(8,128)S(1)}, f32[768,128]{1,0:T(8,128)S(1)}, f32[768,128]{1,0:T(8,128)S(1)}) custom-call(s32[2]{0:T(128)S(1)} %compare_select_fusion.3.par_ref, s32[64]{0:T(128)S(1)} %fusion.6.pos_ref, bf16[192,512]{1,0:T(8,128)(2,1)S(1)} %copy-done.1, bf16[192,512]{1,0:T(8,128)(2,1)S(1)} %copy-done.2, ...), custom_call_target="tpu_custom_call" | custom-call | flops 1207959552 | bytes 3932160 | tf_op jit(solution)/shard_map/attend/pallas_call | solution.py:160
  139.0 7.3 %attend.9 = (f32[768,128]{1,0:T(8,128)S(1)}, f32[768,128]{1,0:T(8,128)S(1)}, f32[768,128]{1,0:T(8,128)S(1)}) custom-call(s32[2]{0:T(128)S(1)} %compare_select_fusion.3.par_ref, s32[64]{0:T(128)S(1)} %fusion.6.pos_ref, bf16[192,512]{1,0:T(8,128)(2,1)S(1)} %copy-done.1, bf16[192,512]{1,0:T(8,128)(2,1)S(1)} %copy-done.2, ...), custom_call_target="tpu_custom_call" | custom-call | flops 603979776 | bytes 3145728 | tf_op jit(solution)/shard_map/attend/pallas_call | solution.py:160
  146.3 7.6 %attend.10 = (f32[768,128]{1,0:T(8,128)S(1)}, f32[768,128]{1,0:T(8,128)S(1)}, f32[768,128]{1,0:T(8,128)S(1)}) custom-call(s32[2]{0:T(128)S(1)} %compare_select_fusion.3.par_ref, s32[64]{0:T(128)S(1)} %fusion.6.pos_ref, bf16[192,512]{1,0:T(8,128)(2,1)S(1)} %copy-done.1, bf16[192,512]{1,0:T(8,128)(2,1)S(1)} %copy-done.2, ...), custom_call_target="tpu_custom_call" | custom-call | flops 603979776 | bytes 3145728 | tf_op jit(solution)/shard_map/attend/pallas_call | solution.py:160
  153.9 5.4 %attend.11.gq_ref = bf16[192,512]{1,0:T(8,128)(2,1)S(1)} custom-call(s32[2]{0:T(128)S(1)} %compare_select_fusion.3.par_ref, s32[64]{0:T(128)S(1)} %fusion.6.pos_ref, bf16[192,512]{1,0:T(8,128)(2,1)S(1)} %copy-done.1, bf16[192,512]{1,0:T(8,128)(2,1)S(1)} %copy-done.2, bf16[2,192,256]{2,1,0:T(8,128)(2,1)S(1)} %collective-permute-done.7.refs_2_, ...), custom_call_target="tpu_custom_call" | custom-call | flops 301989888 | bytes 2752512 | tf_op jit(solution)/shard_map/attend/pallas_call | solution.py:160
  159.3 1.4 project.3
  160.7 1.9 collective-permute-start.16
  162.7 1.4 project.2
  164.1 0.8 collective-permute-done.16
  165.2 4.6 %collective-permute-start.17 = (bf16[192,512]{1,0:T(8,128)(2,1)S(1)}, bf16[192,512]{1,0:T(8,128)(2,1)S(1)}, u32[]{:S(2)}, u32[]{:S(2)}) collective-permute-start(bf16[192,512]{1,0:T(8,128)(2,1)S(1)} %get-tuple-element.35), channel_id=1, source_target_pairs={{0,4},{2,6},{4,0},{6,2},{1,5},{3,7},{5,1},{7,3},{8,12},{10,14},{12... | collective-permute-start | bytes 589832 | tf_op jit(solution)/shard_map/ppermute | solution.py:211
  169.8 2.4 %collective-permute-start.18 = (bf16[192,512]{1,0:T(8,128)(2,1)S(1)}, bf16[192,512]{1,0:T(8,128)(2,1)S(1)}, u32[]{:S(2)}, u32[]{:S(2)}) collective-permute-start(bf16[192,512]{1,0:T(8,128)(2,1)S(1)} %get-tuple-element.37), channel_id=1, source_target_pairs={{0,2},{2,0},{4,6},{6,4},{1,3},{3,1},{5,7},{7,5},{8,10},{10,8},{12,... | collective-permute-start | bytes 589832 | tf_op jit(solution)/shard_map/ppermute | solution.py:211
  172.2 2.8 %collective-permute-start.19 = (bf16[192,512]{1,0:T(8,128)(2,1)S(1)}, bf16[192,512]{1,0:T(8,128)(2,1)S(1)}, u32[]{:S(2)}, u32[]{:S(2)}) collective-permute-start(bf16[192,512]{1,0:T(8,128)(2,1)S(1)} %get-tuple-element.36), channel_id=1, source_target_pairs={{0,6},{2,4},{4,2},{6,0},{1,7},{3,5},{5,3},{7,1},{8,14},{10,12},{12... | collective-permute-start | bytes 589832 | tf_op jit(solution)/shard_map/ppermute | solution.py:211
  175.0 1.3 collective-permute-done.17
  176.3 3.1 %collective-permute-done.18 = bf16[192,512]{1,0:T(8,128)(2,1)S(1)} collective-permute-done((bf16[192,512]{1,0:T(8,128)(2,1)S(1)}, bf16[192,512]{1,0:T(8,128)(2,1)S(1)}, u32[]{:S(2)}, u32[]{:S(2)}) %collective-permute-start.18) | collective-permute-done | bytes 196640 | tf_op jit(solution)/shard_map/ppermute | solution.py:211
  179.4 2.3 %collective-permute-done.19 = bf16[192,512]{1,0:T(8,128)(2,1)S(1)} collective-permute-done((bf16[192,512]{1,0:T(8,128)(2,1)S(1)}, bf16[192,512]{1,0:T(8,128)(2,1)S(1)}, u32[]{:S(2)}, u32[]{:S(2)}) %collective-permute-start.19) | collective-permute-done | bytes 196640 | tf_op jit(solution)/shard_map/ppermute | solution.py:211
  181.8 6.2 %collective-permute-start.20 = (bf16[192,512]{1,0:T(8,128)(2,1)S(1)}, bf16[192,512]{1,0:T(8,128)(2,1)S(1)}, u32[]{:S(2)}, u32[]{:S(2)}) collective-permute-start(bf16[192,512]{1,0:T(8,128)(2,1)S(1)} %fusion.3), channel_id=1, source_target_pairs={{8,0},{16,8},{24,16},{32,24},{40,32},{48,40},{56,48},{64,56},{72,6... | collective-permute-start | bytes 589832 | tf_op jit(solution)/shard_map/ppermute | solution.py:265
  188.1 5.5 %collective-permute-done.20 = bf16[192,512]{1,0:T(8,128)(2,1)S(1)} collective-permute-done((bf16[192,512]{1,0:T(8,128)(2,1)S(1)}, bf16[192,512]{1,0:T(8,128)(2,1)S(1)}, u32[]{:S(2)}, u32[]{:S(2)}) %collective-permute-start.20) | collective-permute-done | bytes 196640 | tf_op jit(solution)/shard_map/ppermute | solution.py:265
  (31 shorter events, 3.0 us)
Async XLA Ops:
  15.7 14.8 %collective-permute-start.8 = (bf16[4,192,256]{2,1,0:T(8,128)(2,1)S(1)}, bf16[4,192,256]{2,1,0:T(8,128)(2,1)S(1)}, u32[]{:S(2)}, u32[]{:S(2)}) collective-permute-start(bf16[4,192,256]{2,1,0:T(8,128)(2,1)S(1)} %bitcast.13), channel_id=1, source_target_pairs={{0,120},{8,0},{16,8},{24,16},{32,24},{40,32},{48,40},{56,48},{64,5... | collective-permute-start | bytes 1179656 | tf_op jit(solution)/shard_map/ppermute | solution.py:257
  25.2 10.9 %collective-permute-start = (bf16[4,192,256]{2,1,0:T(8,128)(2,1)S(1)}, bf16[4,192,256]{2,1,0:T(8,128)(2,1)S(1)}, u32[]{:S(2)}, u32[]{:S(2)}) collective-permute-start(bf16[4,192,256]{2,1,0:T(8,128)(2,1)S(1)} %bitcast.14), channel_id=1, source_target_pairs={{0,8},{8,16},{16,24},{24,32},{32,40},{40,48},{48,56},{56,64},{64,7... | collective-permute-start | bytes 1179656 | tf_op jit(solution)/shard_map/ppermute | solution.py:256
  30.5 11.0 %collective-permute-start.9 = (bf16[4,192,256]{2,1,0:T(8,128)(2,1)S(1)}, bf16[4,192,256]{2,1,0:T(8,128)(2,1)S(1)}, u32[]{:S(2)}, u32[]{:S(2)}) collective-permute-start(bf16[4,192,256]{2,1,0:T(8,128)(2,1)S(1)} %collective-permute-done.8.refs_4_), channel_id=1, source_target_pairs={{0,120},{8,0},{16,8},{24,16},{32,24},{40,32},{48,40},{56,48},{64,5... | collective-permute-start | bytes 1179656 | tf_op jit(solution)/shard_map/ppermute | solution.py:257
  36.1 11.3 %collective-permute-start.1 = (bf16[4,192,256]{2,1,0:T(8,128)(2,1)S(1)}, bf16[4,192,256]{2,1,0:T(8,128)(2,1)S(1)}, u32[]{:S(2)}, u32[]{:S(2)}) collective-permute-start(bf16[4,192,256]{2,1,0:T(8,128)(2,1)S(1)} %collective-permute-done.refs_3_), channel_id=1, source_target_pairs={{0,8},{8,16},{16,24},{24,32},{32,40},{40,48},{48,56},{56,64},{64,7... | collective-permute-start | bytes 1179656 | tf_op jit(solution)/shard_map/ppermute | solution.py:256
  41.5 12.1 %collective-permute-start.10 = (bf16[4,192,256]{2,1,0:T(8,128)(2,1)S(1)}, bf16[4,192,256]{2,1,0:T(8,128)(2,1)S(1)}, u32[]{:S(2)}, u32[]{:S(2)}) collective-permute-start(bf16[4,192,256]{2,1,0:T(8,128)(2,1)S(1)} %collective-permute-done.9.refs_3_), channel_id=1, source_target_pairs={{0,120},{8,0},{16,8},{24,16},{32,24},{40,32},{48,40},{56,48},{64,5... | collective-permute-start | bytes 1179656 | tf_op jit(solution)/shard_map/ppermute | solution.py:257
  47.4 12.6 %collective-permute-start.2 = (bf16[4,192,256]{2,1,0:T(8,128)(2,1)S(1)}, bf16[4,192,256]{2,1,0:T(8,128)(2,1)S(1)}, u32[]{:S(2)}, u32[]{:S(2)}) collective-permute-start(bf16[4,192,256]{2,1,0:T(8,128)(2,1)S(1)} %collective-permute-done.1.refs_2_), channel_id=1, source_target_pairs={{0,8},{8,16},{16,24},{24,32},{32,40},{40,48},{48,56},{56,64},{64,7... | collective-permute-start | bytes 1179656 | tf_op jit(solution)/shard_map/ppermute | solution.py:256
  53.6 13.3 %collective-permute-start.11 = (bf16[4,192,256]{2,1,0:T(8,128)(2,1)S(1)}, bf16[4,192,256]{2,1,0:T(8,128)(2,1)S(1)}, u32[]{:S(2)}, u32[]{:S(2)}) collective-permute-start(bf16[4,192,256]{2,1,0:T(8,128)(2,1)S(1)} %collective-permute-done.10.refs_5_), channel_id=1, source_target_pairs={{0,120},{8,0},{16,8},{24,16},{32,24},{40,32},{48,40},{56,48},{64,5... | collective-permute-start | bytes 1179656 | tf_op jit(solution)/shard_map/ppermute | solution.py:257
  59.2 0.7 copy-start.3
  60.0 13.7 %collective-permute-start.3 = (bf16[4,192,256]{2,1,0:T(8,128)(2,1)S(1)}, bf16[4,192,256]{2,1,0:T(8,128)(2,1)S(1)}, u32[]{:S(2)}, u32[]{:S(2)}) collective-permute-start(bf16[4,192,256]{2,1,0:T(8,128)(2,1)S(1)} %collective-permute-done.2.refs_4_), channel_id=1, source_target_pairs={{0,8},{8,16},{16,24},{24,32},{32,40},{40,48},{48,56},{56,64},{64,7... | collective-permute-start | bytes 1179656 | tf_op jit(solution)/shard_map/ppermute | solution.py:256
  61.9 0.8 copy-start.5
  66.9 14.1 %collective-permute-start.12 = (bf16[4,192,256]{2,1,0:T(8,128)(2,1)S(1)}, bf16[4,192,256]{2,1,0:T(8,128)(2,1)}, u32[]{:S(2)}, u32[]{:S(2)}) collective-permute-start(bf16[4,192,256]{2,1,0:T(8,128)(2,1)S(1)} %collective-permute-done.11.refs_3_), channel_id=1, source_target_pairs={{0,120},{8,0},{16,8},{24,16},{32,24},{40,32},{48,40},{56,48},{64,5... | collective-permute-start | bytes 1179656 | tf_op jit(solution)/shard_map/ppermute | solution.py:257
  73.7 14.7 %collective-permute-start.4 = (bf16[4,192,256]{2,1,0:T(8,128)(2,1)S(1)}, bf16[4,192,256]{2,1,0:T(8,128)(2,1)}, u32[]{:S(2)}, u32[]{:S(2)}) collective-permute-start(bf16[4,192,256]{2,1,0:T(8,128)(2,1)S(1)} %collective-permute-done.3.refs_2_), channel_id=1, source_target_pairs={{0,8},{8,16},{16,24},{24,32},{32,40},{40,48},{48,56},{56,64},{64,7... | collective-permute-start | bytes 1179656 | tf_op jit(solution)/shard_map/ppermute | solution.py:256
  81.0 15.0 %collective-permute-start.13 = (bf16[4,192,256]{2,1,0:T(8,128)(2,1)}, bf16[4,192,256]{2,1,0:T(8,128)(2,1)S(1)}, u32[]{:S(2)}, u32[]{:S(2)}) collective-permute-start(bf16[4,192,256]{2,1,0:T(8,128)(2,1)} %collective-permute-done.12.refs_5_), channel_id=1, source_target_pairs={{0,120},{8,0},{16,8},{24,16},{32,24},{40,32},{48,40},{56,48},{64,5... | collective-permute-start | bytes 1179656 | tf_op jit(solution)/shard_map/ppermute | solution.py:257
  88.4 14.3 %collective-permute-start.5 = (bf16[4,192,256]{2,1,0:T(8,128)(2,1)}, bf16[4,192,256]{2,1,0:T(8,128)(2,1)S(1)}, u32[]{:S(2)}, u32[]{:S(2)}) collective-permute-start(bf16[4,192,256]{2,1,0:T(8,128)(2,1)} %collective-permute-done.4.refs_4_), channel_id=1, source_target_pairs={{0,8},{8,16},{16,24},{24,32},{32,40},{40,48},{48,56},{56,64},{64,7... | collective-permute-start | bytes 1179656 | tf_op jit(solution)/shard_map/ppermute | solution.py:256
  96.0 31.2 %collective-permute-start.14 = (bf16[4,192,256]{2,1,0:T(8,128)(2,1)S(1)}, bf16[4,192,256]{2,1,0:T(8,128)(2,1)S(1)}, u32[]{:S(2)}, u32[]{:S(2)}) collective-permute-start(bf16[4,192,256]{2,1,0:T(8,128)(2,1)S(1)} %collective-permute-done.13.refs_3_), channel_id=1, source_target_pairs={{0,120},{8,0},{16,8},{24,16},{32,24},{40,32},{48,40},{56,48},{64,5... | collective-permute-start | bytes 1179656 | tf_op jit(solution)/shard_map/ppermute | solution.py:257
  102.7 27.2 %collective-permute-start.6 = (bf16[4,192,256]{2,1,0:T(8,128)(2,1)S(1)}, bf16[4,192,256]{2,1,0:T(8,128)(2,1)S(1)}, u32[]{:S(2)}, u32[]{:S(2)}) collective-permute-start(bf16[4,192,256]{2,1,0:T(8,128)(2,1)S(1)} %collective-permute-done.5.refs_2_), channel_id=1, source_target_pairs={{0,8},{8,16},{16,24},{24,32},{32,40},{40,48},{48,56},{56,64},{64,7... | collective-permute-start | bytes 1179656 | tf_op jit(solution)/shard_map/ppermute | solution.py:256
  104.7 0.9 copy-start.1
  105.6 0.9 copy-start.2
  106.5 9.9 %copy-start.4 = (bf16[4,192,256]{2,1,0:T(8,128)(2,1)S(1)}, bf16[4,192,256]{2,1,0:T(8,128)(2,1)}, u32[]{:S(2)}) copy-start(bf16[4,192,256]{2,1,0:T(8,128)(2,1)} %copy-done.3) | copy-start | bytes 1179652
  106.5 9.9 %copy-start.6 = (bf16[4,192,256]{2,1,0:T(8,128)(2,1)S(1)}, bf16[4,192,256]{2,1,0:T(8,128)(2,1)}, u32[]{:S(2)}) copy-start(bf16[4,192,256]{2,1,0:T(8,128)(2,1)} %copy-done.5) | copy-start | bytes 1179652
  127.3 26.6 %collective-permute-start.15 = (bf16[2,192,256]{2,1,0:T(8,128)(2,1)S(1)}, bf16[2,192,256]{2,1,0:T(8,128)(2,1)S(1)}, u32[]{:S(2)}, u32[]{:S(2)}) collective-permute-start(bf16[2,192,256]{2,1,0:T(8,128)(2,1)S(1)} %slice.25), channel_id=1, source_target_pairs={{0,120},{8,0},{16,8},{24,16},{32,24},{40,32},{48,40},{56,48},{64,5... | collective-permute-start | bytes 589832 | tf_op jit(solution)/shard_map/ppermute | solution.py:257
  130.0 23.9 %collective-permute-start.7 = (bf16[2,192,256]{2,1,0:T(8,128)(2,1)S(1)}, bf16[2,192,256]{2,1,0:T(8,128)(2,1)S(1)}, u32[]{:S(2)}, u32[]{:S(2)}) collective-permute-start(bf16[2,192,256]{2,1,0:T(8,128)(2,1)S(1)} %slice.24), channel_id=1, source_target_pairs={{0,8},{8,16},{16,24},{24,32},{32,40},{40,48},{48,56},{56,64},{64,7... | collective-permute-start | bytes 589832 | tf_op jit(solution)/shard_map/ppermute | solution.py:256
  146.3 13.1 %copy-start = (bf16[4096,512]{1,0:T(8,128)(2,1)S(1)}, bf16[4096,512]{1,0:T(8,128)(2,1)}, u32[]{:S(2)}) copy-start(bf16[4096,512]{1,0:T(8,128)(2,1)} %w_ref.3) | copy-start | bytes 12582916
  160.7 4.2 %collective-permute-start.16 = (bf16[4,192,512]{2,1,0:T(8,128)(2,1)S(1)}, bf16[4,192,512]{2,1,0:T(8,128)(2,1)S(1)}, u32[]{:S(2)}, u32[]{:S(2)}) collective-permute-start(bf16[4,192,512]{2,1,0:T(8,128)(2,1)S(1)} %project.3), channel_id=1, source_target_pairs={{0,1},{1,0},{2,3},{3,2},{4,5},{5,4},{6,7},{7,6},{8,9},{9,8},{10,11... | collective-permute-start | bytes 2359304 | tf_op jit(solution)/shard_map/ppermute | solution.py:211
  164.1 17.6 %copy-start.7 = (bf16[192,512]{1,0:T(8,128)(2,1)S(1)}, bf16[192,512]{1,0:T(8,128)(2,1)}, u32[]{:S(2)}) copy-start(bf16[192,512]{1,0:T(8,128)(2,1)} %param.11) | copy-start | bytes 589828
  165.2 11.1 %collective-permute-start.17 = (bf16[192,512]{1,0:T(8,128)(2,1)S(1)}, bf16[192,512]{1,0:T(8,128)(2,1)S(1)}, u32[]{:S(2)}, u32[]{:S(2)}) collective-permute-start(bf16[192,512]{1,0:T(8,128)(2,1)S(1)} %get-tuple-element.35), channel_id=1, source_target_pairs={{0,4},{2,6},{4,0},{6,2},{1,5},{3,7},{5,1},{7,3},{8,12},{10,14},{12... | collective-permute-start | bytes 589832 | tf_op jit(solution)/shard_map/ppermute | solution.py:211
  169.8 9.6 %collective-permute-start.18 = (bf16[192,512]{1,0:T(8,128)(2,1)S(1)}, bf16[192,512]{1,0:T(8,128)(2,1)S(1)}, u32[]{:S(2)}, u32[]{:S(2)}) collective-permute-start(bf16[192,512]{1,0:T(8,128)(2,1)S(1)} %get-tuple-element.37), channel_id=1, source_target_pairs={{0,2},{2,0},{4,6},{6,4},{1,3},{3,1},{5,7},{7,5},{8,10},{10,8},{12,... | collective-permute-start | bytes 589832 | tf_op jit(solution)/shard_map/ppermute | solution.py:211
  172.2 9.5 %collective-permute-start.19 = (bf16[192,512]{1,0:T(8,128)(2,1)S(1)}, bf16[192,512]{1,0:T(8,128)(2,1)S(1)}, u32[]{:S(2)}, u32[]{:S(2)}) collective-permute-start(bf16[192,512]{1,0:T(8,128)(2,1)S(1)} %get-tuple-element.36), channel_id=1, source_target_pairs={{0,6},{2,4},{4,2},{6,0},{1,7},{3,5},{5,3},{7,1},{8,14},{10,12},{12... | collective-permute-start | bytes 589832 | tf_op jit(solution)/shard_map/ppermute | solution.py:211
  181.8 11.7 %collective-permute-start.20 = (bf16[192,512]{1,0:T(8,128)(2,1)S(1)}, bf16[192,512]{1,0:T(8,128)(2,1)S(1)}, u32[]{:S(2)}, u32[]{:S(2)}) collective-permute-start(bf16[192,512]{1,0:T(8,128)(2,1)S(1)} %fusion.3), channel_id=1, source_target_pairs={{8,0},{16,8},{24,16},{32,24},{40,32},{48,40},{56,48},{64,56},{72,6... | collective-permute-start | bytes 589832 | tf_op jit(solution)/shard_map/ppermute | solution.py:265

commit v3 on v2

--- a/solution.py
+++ b/solution.py
@@ -10,6 +10,8 @@
 
 
 ROWS = 192
+SEG = 96
+PAIR = 2
 WIDTH = 128
 HEADS = 4
 SLOTS = HEADS * ROWS
@@ -21,38 +23,105 @@
 
 def attend(counts, group, offset, first, last, par_ref, pos_ref, *refs):
     refs = list(refs)
-    q_ref, g_ref = refs[:2]
+    qg_refs = refs[:2]
     kv_refs = refs[2 : 2 + len(counts)]
     refs = refs[2 + len(counts) :]
     if not first:
         sw_in, sp_in, st_in = refs[:3]
         refs = refs[3:]
-    outs = refs[: 1 if last else 3]
-    slot_pos, buf, q_s, g_s, m_s, w_s, p_s = refs[1 if last else 3 :]
-    base = par_ref[0]
-    lo = par_ref[1]
-
+    outs = refs[:3]
+    slot_pos, buf, q_s, g_s, m_s, w_s, p_s = refs[3:]
+
+    for t, qg_ref in enumerate(qg_refs):
+        for h in range(HEADS):
+            rows = pl.ds(h * ROWS, ROWS)
+            scaled = qg_ref[:, pl.ds(h * WIDTH, WIDTH)].astype(jnp.float32) * (
+                SCALE * math.log2(math.e)
+            )
+            high = scaled.astype(jnp.bfloat16)
+            q_s[t, rows, :WIDTH] = high
+            q_s[t, rows, WIDTH:] = (scaled - high.astype(jnp.float32)).astype(jnp.bfloat16)
+            g_s[t, rows, :] = qg_ref[:, pl.ds((HEADS + h) * WIDTH, WIDTH)]
+        if first:
+            m_s[t] = jnp.full((SLOTS, WIDTH), LOW, jnp.float32)
+            w_s[t] = jnp.zeros((SLOTS, 2 * WIDTH), jnp.float32)
+            p_s[t] = jnp.zeros((SLOTS, 2 * WIDTH), jnp.float32)
+        else:
+            st = st_in[t]
+            shape = (SLOTS, WIDTH)
+            m_s[t] = jnp.broadcast_to(st[:, 0:1], shape)
+            p_s[t, :, :WIDTH] = sp_in[t]
+            p_s[t, :, WIDTH:] = jnp.broadcast_to(st[:, 64:65], shape)
+            w_s[t, :, :WIDTH] = sw_in[t]
+            w_s[t, :, WIDTH:] = jnp.broadcast_to(st[:, 127:128], shape)
+
+    @pl.loop(0, PAIR)
+    def _(t):
+        sweep(
+            counts, group, offset, par_ref[2 * t], par_ref[2 * t + 1], pos_ref, kv_refs,
+            slot_pos, buf, q_s.at[t], g_s.at[t], m_s.at[t], w_s.at[t], p_s.at[t],
+        )
+
+    lane = lax.broadcasted_iota(jnp.int32, (SLOTS, WIDTH), 1)
+    for t in range(PAIR):
+        if not last:
+            sw_out, sp_out, st_out = outs
+            sw_out[t] = w_s[t, :, :WIDTH]
+            sp_out[t] = p_s[t, :, :WIDTH]
+            st_out[t] = jnp.where(
+                lane < 43, m_s[t], jnp.where(lane < 86, p_s[t, :, WIDTH:], w_s[t, :, WIDTH:])
+            )
+            continue
+        kept, sent, sent_stats = outs
+        l = p_s[t, :, WIDTH:]
+        some = l > 0.0
+        l = jnp.where(some, l, 1.0)
+        delta = w_s[t, :, WIDTH:] / l
+        key_mean = p_s[t, :, :WIDTH] / l
+        centred = w_s[t, :, :WIDTH] / l - delta * key_mean
+        weight = jnp.where(some, m_s[t] + jnp.log2(l), LOW)
+        if t == 0:
+            kept[0], kept[1], kept[2], kept[3] = centred, key_mean, weight, delta
+        else:
+            sent[0] = centred.astype(jnp.bfloat16)
+            sent[1] = key_mean.astype(jnp.bfloat16)
+            row = lax.broadcasted_iota(jnp.int32, (8, SLOTS), 0)
+            sent_stats[...] = jnp.where(row < 4, weight.T[:8], delta.T[:8])
+
+
+def merge_body(kept, came, came_stats, out_ref):
+    stats = jnp.concatenate([came_stats[...]] * (WIDTH // 8), axis=0).T
+    weight_b, delta_b = stats[:, 0:1], stats[:, 4:5]
+    weight_a, delta_a = kept[2], kept[3]
+    top = jnp.maximum(weight_a, weight_b)
+    a = jnp.exp2(weight_a - top)
+    b = jnp.exp2(weight_b - top)
+    total = a + b
+    a = a / total
+    b = b / total
+    delta = a * delta_a + b * delta_b
+    grad = a * (kept[0] + (delta_a - delta) * kept[1])
+    grad += b * (came[0].astype(jnp.float32) + (delta_b - delta) * came[1].astype(jnp.float32))
+    grad = grad * SCALE
     for h in range(HEADS):
-        rows = pl.ds(h * ROWS, ROWS)
-        cols = pl.ds(h * WIDTH, WIDTH)
-        scaled = q_ref[:, cols].astype(jnp.float32) * (SCALE * math.log2(math.e))
-        high = scaled.astype(jnp.bfloat16)
-        q_s[rows, :WIDTH] = high
-        q_s[rows, WIDTH:] = (scaled - high.astype(jnp.float32)).astype(jnp.bfloat16)
-        g_s[rows, :] = g_ref[:, cols]
-    if first:
-        m_s[...] = jnp.full((SLOTS, WIDTH), LOW, jnp.float32)
-        w_s[...] = jnp.zeros((SLOTS, 2 * WIDTH), jnp.float32)
-        p_s[...] = jnp.zeros((SLOTS, 2 * WIDTH), jnp.float32)
-    else:
-        st = st_in[...]
-        shape = (SLOTS, WIDTH)
-        m_s[...] = jnp.broadcast_to(st[:, 0:1], shape)
-        p_s[:, :WIDTH] = sp_in[...]
-        p_s[:, WIDTH:] = jnp.broadcast_to(st[:, 64:65], shape)
-        w_s[:, :WIDTH] = sw_in[...]
-        w_s[:, WIDTH:] = jnp.broadcast_to(st[:, 127:128], shape)
-
+        out_ref[:, pl.ds(h * WIDTH, WIDTH)] = grad[h * ROWS : (h + 1) * ROWS].astype(jnp.bfloat16)
+
+
+def merge(kept, came, came_stats):
+    vmem = pl.BlockSpec(memory_space=pltpu.VMEM)
+    return pl.pallas_call(
+        merge_body,
+        in_specs=[vmem] * 3,
+        out_specs=vmem,
+        out_shape=jax.ShapeDtypeStruct((ROWS, HEADS * WIDTH), jnp.bfloat16),
+        compiler_params=pltpu.CompilerParams(vmem_limit_bytes=16 << 20),
+        name="merge",
+    )(kept, came, came_stats)
+
+
+def sweep(
+    counts, group, offset, base, lo, pos_ref, kv_refs, slot_pos, buf, q_s, g_s, m_s, w_s, p_s
+):
     def collect(used, chosen_of):
         at = offset
         for ref, n in zip(kv_refs, counts):
@@ -74,14 +143,14 @@
 
     full = collect(jnp.int32(0), lambda p: (p >= lo) & (p < base))
     used = collect(
-        full, lambda p: (p + ROWS > lo) & (p <= base) & ((p < lo) | (p == base))
+        full, lambda p: (p + SEG > lo) & (p < base + ROWS) & ((p < lo) | (p >= base))
     )
     groups = (used + group - 1) // group
     for j in range(group - 1):
 
         @pl.when(used + j < groups * group)
         def _():
-            buf[used + j] = jnp.zeros((ROWS, 2 * WIDTH), jnp.bfloat16)
+            buf[used + j] = jnp.zeros((SEG, 2 * WIDTH), jnp.bfloat16)
             slot_pos[used + j] = jnp.int32(1 << 30)
 
     contract = (((1,), (1,)), ((), ()))
@@ -94,9 +163,9 @@
         k1 = jnp.concatenate([k, jnp.ones_like(k)], axis=1)
         s = lax.dot_general(q_s[rows, :], kk, contract, preferred_element_type=jnp.float32)
         if masked:
-            lane = lax.broadcasted_iota(jnp.int32, (1, ROWS), 1)
+            lane = lax.broadcasted_iota(jnp.int32, (1, SEG), 1)
             key_at = jnp.concatenate([lane + slot_pos[start + j] for j in range(group)], axis=1)
-            row = lax.broadcasted_iota(jnp.int32, (ROWS, group * ROWS), 0) + base
+            row = lax.broadcasted_iota(jnp.int32, (ROWS, group * SEG), 0) + base
             inside = (key_at >= lo) & (key_at <= row)
             s = jnp.where(inside, s, LOW)
         top = jnp.max(s, axis=1, keepdims=True)
@@ -130,52 +199,42 @@
             def _(h):
                 visit(g, pl.ds(pl.multiple_of(h * ROWS, ROWS), ROWS), True)
 
-    if last:
-        l = p_s[:, WIDTH:]
-        l = jnp.where(l > 0.0, l, 1.0)
-        delta = w_s[:, WIDTH:] / l
-        grad = (w_s[:, :WIDTH] - delta * p_s[:, :WIDTH]) / l * SCALE
-        for h in range(HEADS):
-            outs[0][:, pl.ds(h * WIDTH, WIDTH)] = grad[h * ROWS : (h + 1) * ROWS].astype(jnp.bfloat16)
-    else:
-        sw_out, sp_out, st_out = outs
-        sw_out[...] = w_s[:, :WIDTH]
-        sp_out[...] = p_s[:, :WIDTH]
-        lane = lax.broadcasted_iota(jnp.int32, (SLOTS, WIDTH), 1)
-        st_out[...] = jnp.where(
-            lane < 43, m_s[...], jnp.where(lane < 86, p_s[:, WIDTH:], w_s[:, WIDTH:])
-        )
-
-
-def attention(par, pos, offset, q, g, arrays, state, last):
+
+def attention(par, pos, offset, qg, arrays, state, last):
     counts = tuple(a.shape[0] for a in arrays)
     first = state is None
     total = sum(counts)
     group = {4: 4, 12: 6}.get(total, 8)
-    shape = jax.ShapeDtypeStruct((SLOTS, WIDTH), jnp.float32)
-    out_shape = jax.ShapeDtypeStruct((ROWS, HEADS * WIDTH), jnp.bfloat16) if last else [shape] * 3
-    operands = [q, g, *arrays] + ([] if first else list(state))
+    shape = jax.ShapeDtypeStruct((PAIR, SLOTS, WIDTH), jnp.float32)
+    out_shape = [shape] * 3
+    if last:
+        out_shape = [
+            jax.ShapeDtypeStruct((4, SLOTS, WIDTH), jnp.float32),
+            jax.ShapeDtypeStruct((2, SLOTS, WIDTH), jnp.bfloat16),
+            jax.ShapeDtypeStruct((8, SLOTS), jnp.float32),
+        ]
+    operands = [*qg, *arrays] + ([] if first else list(state))
     vmem = pl.BlockSpec(memory_space=pltpu.VMEM)
     smem = pl.BlockSpec(memory_space=pltpu.SMEM)
     return pl.pallas_call(
         functools.partial(attend, counts, group, offset, first, last),
         in_specs=[smem, smem] + [vmem] * len(operands),
-        out_specs=vmem if last else [vmem] * 3,
+        out_specs=[vmem] * 3,
         out_shape=out_shape,
         scratch_shapes=[
             pltpu.SMEM((total + group,), jnp.int32),
-            pltpu.VMEM((total + group, ROWS, 2 * WIDTH), jnp.bfloat16),
-            pltpu.VMEM((SLOTS, 2 * WIDTH), jnp.bfloat16),
-            pltpu.VMEM((SLOTS, WIDTH), jnp.bfloat16),
-            pltpu.VMEM((SLOTS, WIDTH), jnp.float32),
-            pltpu.VMEM((SLOTS, 2 * WIDTH), jnp.float32),
-            pltpu.VMEM((SLOTS, 2 * WIDTH), jnp.float32),
+            pltpu.VMEM((total + group, SEG, 2 * WIDTH), jnp.bfloat16),
+            pltpu.VMEM((PAIR, SLOTS, 2 * WIDTH), jnp.bfloat16),
+            pltpu.VMEM((PAIR, SLOTS, WIDTH), jnp.bfloat16),
+            pltpu.VMEM((PAIR, SLOTS, WIDTH), jnp.float32),
+            pltpu.VMEM((PAIR, SLOTS, 2 * WIDTH), jnp.float32),
+            pltpu.VMEM((PAIR, SLOTS, 2 * WIDTH), jnp.float32),
         ],
-        compiler_params=pltpu.CompilerParams(vmem_limit_bytes=24 << 20),
+        compiler_params=pltpu.CompilerParams(vmem_limit_bytes=20 << 20),
         cost_estimate=pl.CostEstimate(
-            flops=8 * total * ROWS * SLOTS * WIDTH // 2,
-            transcendentals=total * ROWS * SLOTS // 2,
-            bytes_accessed=total * ROWS * 2 * WIDTH * 2 + 3 * SLOTS * WIDTH * 8,
+            flops=8 * total * SEG * SLOTS * WIDTH,
+            transcendentals=total * SEG * SLOTS,
+            bytes_accessed=total * SEG * 2 * WIDTH * 2 + 6 * SLOTS * WIDTH * 8,
         ),
         name="attend",
     )(par, pos, *operands)
@@ -231,13 +290,21 @@
 def shards(queries, keys, values, d_attn, d_out, w_query, prefix_len):
     y_id = lax.axis_index("y")
     z_id = lax.axis_index("z")
-    section = y_id * Z + z_id
-    base = section * ROWS
-    lo = jnp.maximum(base - prefix_len[section], 0)
-    par = jnp.where(jnp.arange(2) == 0, base, lo).astype(jnp.int32)
-    q, g = queries, d_attn
+    base = (y_id * Z + z_id) * ROWS
+    other = ((Y - 1 - y_id) * Z + z_id) * ROWS
+    low = jnp.maximum(base - prefix_len[base // ROWS], 0)
+    other_low = jnp.maximum(other - prefix_len[other // ROWS], 0)
+    entry = jnp.arange(2 * PAIR)
+    par = jnp.where(entry < 2, jnp.where(entry == 0, base, low), jnp.where(entry == 2, other, other_low))
+    par = par.astype(jnp.int32)
+    part = (y_id >= Y // 2).astype(jnp.int32) * SEG
+
+    qg = jnp.concatenate([queries, d_attn], axis=1)
+    mirror = [(y, Y - 1 - y) for y in range(Y)]
+    qg = (qg, lax.ppermute(qg, "y", mirror))
 
     mine = lax.all_gather(jnp.concatenate([keys, values], axis=1), "y", axis=0)
+    mine = lax.dynamic_slice_in_dim(mine, part, SEG, axis=1)
 
     up = [(z, (z + 1) % Z) for z in range(Z)]
     down = [(z, (z - 1) % Z) for z in range(Z)]
@@ -245,7 +312,7 @@
     turn = jnp.arange(Z * Y, dtype=jnp.int32)
     hop = turn // Y
     hop = jnp.where(hop % 2 == 1, (hop + 1) // 2, Z - hop // 2)
-    pos = ((z_id + Z - hop) % Z + turn % Y * Z) * ROWS
+    pos = ((z_id + Z - hop) % Z + turn % Y * Z) * ROWS + part
 
     half = Z // 2
     below = above = mine
@@ -256,12 +323,14 @@
         below = lax.ppermute(below[: Y // 2] if last else below, "z", up)
         above = lax.ppermute(above[Y // 2 :] if last else above, "z", down)
         if step % 2 == 0 or step == half - 1:
-            state = attention(par, pos, done, q, g, arrays, state, False)
+            state = attention(par, pos, done, qg, arrays, state, False)
             done += sum(a.shape[0] for a in arrays)
             arrays = []
         arrays += [below, above]
-    state = attention(par, pos, done, q, g, arrays, state, True)
-    hidden = reduce_heads(state, w_query, d_out)
+    kept, sent, stats = attention(par, pos, done, qg, arrays, state, True)
+    came = lax.ppermute(sent, "y", mirror)
+    came_stats = lax.ppermute(stats, "y", mirror)
+    hidden = reduce_heads(merge(kept, came, came_stats), w_query, d_out)
     return lax.ppermute(hidden, ("y", "z"), [(i + 1, i) for i in range(Y * Z - 1)])
 
 

time: 195 us -> 207 us (1.062)
  starting transfers between devices: 80.2 us -> 112 us
  waiting for transfers between devices: 41.9 us -> 21.6 us
    ppermute x8, waiting for transfers between devices: 24.6 us -> 3.92 us  [shards(): above = lax.ppermute(above[Y // 2:] if last else above, 'z', down)]
    ppermute x1, starting transfers between devices: 6.21 us -> 18.7 us  [shards(): lax.ppermute(hidden, ('y', 'z'), [(i + 1, i) for i in range(Y * Z - 1)])]
    ppermute x8, starting transfers between devices: 45.7 us -> 56.2 us  [shards(): above = lax.ppermute(above[Y // 2:] if last else above, 'z', down)]
    ppermute x0 -> x3, starting transfers between devices: none -> 9.23 us  [the longest x1 4.77 us: shards(): came_stats = lax.ppermute(stats, 'y', mirror)]
    ppermute x0 -> x3, waiting for transfers between devices: none -> 3.8 us  [the longest x1 3.8 us: shards(): came_stats = lax.ppermute(stats, 'y', mirror)]
    ppermute x1, waiting for transfers between devices: 5.47 us -> 3.17 us  [shards(): lax.ppermute(hidden, ('y', 'z'), [(i + 1, i) for i in range(Y * Z - 1)])]
  transfers between devices with their start and end apart: 21 -> 24, of which waited for: 15 -> 13; matrix products, arithmetic and copies ran while one was open for 1% -> 1% of each run, Pallas kernels for 22% -> 20%
where the time goes in v3:
time: 207 us; the launch traced here: 206 us
  starting transfers between devices  112 us (54%)
  Pallas kernels  49.7 us (24%)
  waiting for transfers between devices  21.6 us (10%)
  blocking collectives  14.9 us (7%)
  local copies, waits for them, and re-layouts  4.56 us (2%)
    ppermute x8, starting transfers between devices, shards(): above = lax.ppermute(above[Y // 2:] if last else above, 'z', down)  56.2 us
    pallas_call x6, Pallas kernels, attention(): pl.pallas_call(functools.partial(attend, counts, group, offset, first, la...  46.4 us
    ppermute x1, starting transfers between devices, shards(): lax.ppermute(hidden, ('y', 'z'), [(i + 1, i) for i in range(Y * Z - 1)])  18.7 us
    ppermute x8, starting transfers between devices, shards(): below = lax.ppermute(below[:Y // 2] if last else below, 'z', up)  15.7 us
    all_gather x1, blocking collectives, shards(): mine = lax.all_gather(jnp.concatenate([keys, values], axis=1), 'y', axis=0)  14.9 us
    ppermute x4, starting transfers between devices, exchange(): return lax.ppermute(value, axis, [(i, i ^ mask) for i in range(count)])  11.7 us
    ppermute x4, waiting for transfers between devices, exchange(): return lax.ppermute(value, axis, [(i, i ^ mask) for i in range(count)])  7.8 us
    ppermute x1, starting transfers between devices, shards(): came_stats = lax.ppermute(stats, 'y', mirror)  4.77 us
  transfers between devices with their start and end apart: 24, of which 13 were waited for; matrix products, arithmetic and copies ran while one was open for 1% of the time, Pallas kernels for 20%

profile of v3, /device:TPU:24, one launch (start us, length us, event | category | flops | bytes accessed | tf_op | source)
XLA Modules:
  0.0 205.6 jit_solution(13771375572986064618)
XLA Ops:
  0.0 0.9 pad_maximum_fusion
  0.9 14.9 %all-gather = bf16[768,256]{1,0:T(8,128)(2,1)S(1)} all-gather(bf16[192,256]{1,0:T(8,128)(2,1)S(1)} %pad_maximum_fusion), channel_id=2, replica_groups=mesh['y'=4,'z'=16,'x'=4,'core'=2] {'y'}, dimensions={0}, use_global_device_ids=true | all-gather | bytes 491520 | tf_op jit(solution)/shard_map/all_gather | solution.py:306
  15.8 9.5 %collective-permute-start.9 = (bf16[4,96,256]{2,1,0:T(8,128)(2,1)S(1)}, bf16[4,96,256]{2,1,0:T(8,128)(2,1)S(1)}, u32[]{:S(2)}, u32[]{:S(2)}) collective-permute-start(bf16[4,96,256]{2,1,0:T(8,128)(2,1)S(1)} %constant_dynamic-slice_fusion.refs_2_), channel_id=1, source_target_pairs={{0,120},{8,0},{16,8},{24,16},{32,24},{40,32},{48,40},{56,48},{64,5... | collective-permute-start | bytes 589832 | tf_op jit(solution)/shard_map/ppermute | solution.py:324
  25.3 1.9 collective-permute-start.1
  27.2 1.2 collective-permute-done.9.refs_4_
  28.5 5.6 %collective-permute-start.10 = (bf16[4,96,256]{2,1,0:T(8,128)(2,1)S(1)}, bf16[4,96,256]{2,1,0:T(8,128)(2,1)S(1)}, u32[]{:S(2)}, u32[]{:S(2)}) collective-permute-start(bf16[4,96,256]{2,1,0:T(8,128)(2,1)S(1)} %collective-permute-done.9.refs_4_), channel_id=1, source_target_pairs={{0,120},{8,0},{16,8},{24,16},{32,24},{40,32},{48,40},{56,48},{64,5... | collective-permute-start | bytes 589832 | tf_op jit(solution)/shard_map/ppermute | solution.py:324
  34.1 1.9 collective-permute-start.2
  36.0 1.4 collective-permute-done.10.refs_3_
  37.3 5.6 %collective-permute-start.11 = (bf16[4,96,256]{2,1,0:T(8,128)(2,1)S(1)}, bf16[4,96,256]{2,1,0:T(8,128)(2,1)S(1)}, u32[]{:S(2)}, u32[]{:S(2)}) collective-permute-start(bf16[4,96,256]{2,1,0:T(8,128)(2,1)S(1)} %collective-permute-done.10.refs_3_), channel_id=1, source_target_pairs={{0,120},{8,0},{16,8},{24,16},{32,24},{40,32},{48,40},{56,48},{64,5... | collective-permute-start | bytes 589832 | tf_op jit(solution)/shard_map/ppermute | solution.py:324
  43.2 1.9 collective-permute-start.3
  45.2 0.9 constant_dynamic-update-slice_fusion.1
  46.1 1.3 collective-permute-done.11.refs_5_
  47.4 5.6 %collective-permute-start.12 = (bf16[4,96,256]{2,1,0:T(8,128)(2,1)S(1)}, bf16[4,96,256]{2,1,0:T(8,128)(2,1)S(1)}, u32[]{:S(2)}, u32[]{:S(2)}) collective-permute-start(bf16[4,96,256]{2,1,0:T(8,128)(2,1)S(1)} %collective-permute-done.11.refs_5_), channel_id=1, source_target_pairs={{0,120},{8,0},{16,8},{24,16},{32,24},{40,32},{48,40},{56,48},{64,5... | collective-permute-start | bytes 589832 | tf_op jit(solution)/shard_map/ppermute | solution.py:324
  53.6 1.9 collective-permute-start.4
  55.5 1.9 collective-permute-start
  57.5 5.6 %collective-permute-start.13 = (bf16[4,96,256]{2,1,0:T(8,128)(2,1)S(1)}, bf16[4,96,256]{2,1,0:T(8,128)(2,1)S(1)}, u32[]{:S(2)}, u32[]{:S(2)}) collective-permute-start(bf16[4,96,256]{2,1,0:T(8,128)(2,1)S(1)} %collective-permute-done.12.refs_3_), channel_id=1, source_target_pairs={{0,120},{8,0},{16,8},{24,16},{32,24},{40,32},{48,40},{56,48},{64,5... | collective-permute-start | bytes 589832 | tf_op jit(solution)/shard_map/ppermute | solution.py:324
  63.1 1.3 collective-permute-done.4.refs_2_
  64.4 1.9 collective-permute-start.5
  68.4 5.2 %collective-permute-start.14 = (bf16[4,96,256]{2,1,0:T(8,128)(2,1)S(1)}, bf16[4,96,256]{2,1,0:T(8,128)(2,1)S(1)}, u32[]{:S(2)}, u32[]{:S(2)}) collective-permute-start(bf16[4,96,256]{2,1,0:T(8,128)(2,1)S(1)} %collective-permute-done.13.refs_5_), channel_id=1, source_target_pairs={{0,120},{8,0},{16,8},{24,16},{32,24},{40,32},{48,40},{56,48},{64,5... | collective-permute-start | bytes 589832 | tf_op jit(solution)/shard_map/ppermute | solution.py:324
  73.6 0.7 collective-permute-done.5.refs_4_
  74.3 1.9 collective-permute-start.6
  76.2 12.8 %attend.6 = (f32[2,768,128]{2,1,0:T(8,128)S(1)}, f32[2,768,128]{2,1,0:T(8,128)S(1)}, f32[2,768,128]{2,1,0:T(8,128)S(1)}) custom-call(s32[4]{0:T(128)S(1)} %compare_select_fusion.5.par_ref, s32[64]{0:T(128)S(1)} %fusion.7.pos_ref, bf16[192,1024]{1,0:T(8,128)(2,1)S(1)} %constant_dynamic-update-slice_fusion.refs_0_, ...), custom_call_target="tpu_custom_call" | custom-call | flops 905969664 | bytes 5308416 | tf_op jit(solution)/shard_map/attend/pallas_call | solution.py:219
  89.0 5.1 %collective-permute-start.15 = (bf16[4,96,256]{2,1,0:T(8,128)(2,1)S(1)}, bf16[4,96,256]{2,1,0:T(8,128)(2,1)S(1)}, u32[]{:S(2)}, u32[]{:S(2)}) collective-permute-start(bf16[4,96,256]{2,1,0:T(8,128)(2,1)S(1)} %collective-permute-done.14.refs_3_), channel_id=1, source_target_pairs={{0,120},{8,0},{16,8},{24,16},{32,24},{40,32},{48,40},{56,48},{64,5... | collective-permute-start | bytes 589832 | tf_op jit(solution)/shard_map/ppermute | solution.py:324
  94.2 2.1 %collective-permute-start.7 = (bf16[4,96,256]{2,1,0:T(8,128)(2,1)S(1)}, bf16[4,96,256]{2,1,0:T(8,128)(2,1)S(1)}, u32[]{:S(2)}, u32[]{:S(2)}) collective-permute-start(bf16[4,96,256]{2,1,0:T(8,128)(2,1)S(1)} %collective-permute-done.6.refs_2_), channel_id=1, source_target_pairs={{0,8},{8,16},{16,24},{24,32},{32,40},{40,48},{48,56},{56,64},{64,7... | collective-permute-start | bytes 589832 | tf_op jit(solution)/shard_map/ppermute | solution.py:323
  96.3 9.5 %attend.7 = (f32[2,768,128]{2,1,0:T(8,128)S(1)}, f32[2,768,128]{2,1,0:T(8,128)S(1)}, f32[2,768,128]{2,1,0:T(8,128)S(1)}) custom-call(s32[4]{0:T(128)S(1)} %compare_select_fusion.5.par_ref, s32[64]{0:T(128)S(1)} %fusion.7.pos_ref, bf16[192,1024]{1,0:T(8,128)(2,1)S(1)} %constant_dynamic-update-slice_fusion.refs_0_, ...), custom_call_target="tpu_custom_call" | custom-call | flops 1207959552 | bytes 5505024 | tf_op jit(solution)/shard_map/attend/pallas_call | solution.py:219
  105.8 5.1 %attend.8 = (f32[2,768,128]{2,1,0:T(8,128)S(1)}, f32[2,768,128]{2,1,0:T(8,128)S(1)}, f32[2,768,128]{2,1,0:T(8,128)S(1)}) custom-call(s32[4]{0:T(128)S(1)} %compare_select_fusion.5.par_ref, s32[64]{0:T(128)S(1)} %fusion.7.pos_ref, bf16[192,1024]{1,0:T(8,128)(2,1)S(1)} %constant_dynamic-update-slice_fusion.refs_0_, ...), custom_call_target="tpu_custom_call" | custom-call | flops 1207959552 | bytes 5505024 | tf_op jit(solution)/shard_map/attend/pallas_call | solution.py:219
  110.9 14.0 %collective-permute-start.16 = (bf16[2,96,256]{2,1,0:T(8,128)(2,1)S(1)}, bf16[2,96,256]{2,1,0:T(8,128)(2,1)S(1)}, u32[]{:S(2)}, u32[]{:S(2)}) collective-permute-start(bf16[2,96,256]{2,1,0:T(8,128)(2,1)S(1)} %slice.25), channel_id=1, source_target_pairs={{0,120},{8,0},{16,8},{24,16},{32,24},{40,32},{48,40},{56,48},{64,5... | collective-permute-start | bytes 294920 | tf_op jit(solution)/shard_map/ppermute | solution.py:324
  125.0 2.1 %collective-permute-start.8 = (bf16[2,96,256]{2,1,0:T(8,128)(2,1)S(1)}, bf16[2,96,256]{2,1,0:T(8,128)(2,1)S(1)}, u32[]{:S(2)}, u32[]{:S(2)}) collective-permute-start(bf16[2,96,256]{2,1,0:T(8,128)(2,1)S(1)} %slice.24), channel_id=1, source_target_pairs={{0,8},{8,16},{16,24},{24,32},{32,40},{40,48},{48,56},{56,64},{64,7... | collective-permute-start | bytes 294920 | tf_op jit(solution)/shard_map/ppermute | solution.py:323
  127.1 6.7 %attend.9 = (f32[2,768,128]{2,1,0:T(8,128)S(1)}, f32[2,768,128]{2,1,0:T(8,128)S(1)}, f32[2,768,128]{2,1,0:T(8,128)S(1)}) custom-call(s32[4]{0:T(128)S(1)} %compare_select_fusion.5.par_ref, s32[64]{0:T(128)S(1)} %fusion.7.pos_ref, bf16[192,1024]{1,0:T(8,128)(2,1)S(1)} %constant_dynamic-update-slice_fusion.refs_0_, ...), custom_call_target="tpu_custom_call" | custom-call | flops 603979776 | bytes 5111808 | tf_op jit(solution)/shard_map/attend/pallas_call | solution.py:219
  133.9 6.5 %attend.10 = (f32[2,768,128]{2,1,0:T(8,128)S(1)}, f32[2,768,128]{2,1,0:T(8,128)S(1)}, f32[2,768,128]{2,1,0:T(8,128)S(1)}) custom-call(s32[4]{0:T(128)S(1)} %compare_select_fusion.5.par_ref, s32[64]{0:T(128)S(1)} %fusion.7.pos_ref, bf16[192,1024]{1,0:T(8,128)(2,1)S(1)} %constant_dynamic-update-slice_fusion.refs_0_, ...), custom_call_target="tpu_custom_call" | custom-call | flops 603979776 | bytes 5111808 | tf_op jit(solution)/shard_map/attend/pallas_call | solution.py:219
  140.4 5.8 %attend.11 = (f32[4,768,128]{2,1,0:T(8,128)S(1)}, bf16[2,768,128]{2,1,0:T(8,128)(2,1)S(1)}, f32[8,768]{1,0:T(8,128)S(1)}) custom-call(s32[4]{0:T(128)S(1)} %compare_select_fusion.5.par_ref, s32[64]{0:T(128)S(1)} %fusion.7.pos_ref, bf16[192,1024]{1,0:T(8,128)(2,1)S(1)} %constant_dynamic-update-slice_fusion.refs_0_, ...), custom_call_target="tpu_custom_call" | custom-call | flops 301989888 | bytes 4915200 | tf_op jit(solution)/shard_map/attend/pallas_call | solution.py:219
  146.3 2.5 %collective-permute-start.17 = (bf16[2,768,128]{2,1,0:T(8,128)(2,1)S(1)}, bf16[2,768,128]{2,1,0:T(8,128)(2,1)S(1)}, u32[]{:S(2)}, u32[]{:S(2)}) collective-permute-start(bf16[2,768,128]{2,1,0:T(8,128)(2,1)S(1)} %get-tuple-element.39), channel_id=1, source_target_pairs={{0,384},{128,256},{256,128},{384,0},{1,385},{129,257},{257,129},{3... | collective-permute-start | bytes 1179656 | tf_op jit(solution)/shard_map/ppermute | solution.py:331
  148.8 4.8 %collective-permute-start.18 = (f32[8,768]{1,0:T(8,128)S(1)}, f32[8,768]{1,0:T(8,128)S(1)}, u32[]{:S(2)}, u32[]{:S(2)}) collective-permute-start(f32[8,768]{1,0:T(8,128)S(1)} %get-tuple-element.40), channel_id=1, source_target_pairs={{0,384},{128,256},{256,128},{384,0},{1,385},{129,257},{257,129},{3... | collective-permute-start | bytes 73736 | tf_op jit(solution)/shard_map/ppermute | solution.py:332
  153.6 3.8 %collective-permute-done.18.came_stats = f32[8,768]{1,0:T(8,128)S(1)} collective-permute-done((f32[8,768]{1,0:T(8,128)S(1)}, f32[8,768]{1,0:T(8,128)S(1)}, u32[]{:S(2)}, u32[]{:S(2)}) %collective-permute-start.18) | collective-permute-done | bytes 24608 | tf_op jit(solution)/shard_map/ppermute | solution.py:332
  158.0 2.2 %copy-done = bf16[4096,512]{1,0:T(8,128)(2,1)S(1)} copy-done((bf16[4096,512]{1,0:T(8,128)(2,1)S(1)}, bf16[4096,512]{1,0:T(8,128)(2,1)}, u32[]{:S(2)}) %copy-start) | copy-done | bytes 4194328
  160.2 1.4 project.3
  161.5 1.9 collective-permute-start.19
  163.5 1.4 project.2
  164.9 0.8 collective-permute-done.19
  166.0 5.1 %collective-permute-start.20 = (bf16[192,512]{1,0:T(8,128)(2,1)S(1)}, bf16[192,512]{1,0:T(8,128)(2,1)S(1)}, u32[]{:S(2)}, u32[]{:S(2)}) collective-permute-start(bf16[192,512]{1,0:T(8,128)(2,1)S(1)} %get-tuple-element.41), channel_id=1, source_target_pairs={{0,4},{2,6},{4,0},{6,2},{1,5},{3,7},{5,1},{7,3},{8,12},{10,14},{12... | collective-permute-start | bytes 589832 | tf_op jit(solution)/shard_map/ppermute | solution.py:270
  171.1 2.1 %collective-permute-start.21 = (bf16[192,512]{1,0:T(8,128)(2,1)S(1)}, bf16[192,512]{1,0:T(8,128)(2,1)S(1)}, u32[]{:S(2)}, u32[]{:S(2)}) collective-permute-start(bf16[192,512]{1,0:T(8,128)(2,1)S(1)} %get-tuple-element.43), channel_id=1, source_target_pairs={{0,2},{2,0},{4,6},{6,4},{1,3},{3,1},{5,7},{7,5},{8,10},{10,8},{12,... | collective-permute-start | bytes 589832 | tf_op jit(solution)/shard_map/ppermute | solution.py:270
  173.2 2.6 %collective-permute-start.22 = (bf16[192,512]{1,0:T(8,128)(2,1)S(1)}, bf16[192,512]{1,0:T(8,128)(2,1)S(1)}, u32[]{:S(2)}, u32[]{:S(2)}) collective-permute-start(bf16[192,512]{1,0:T(8,128)(2,1)S(1)} %get-tuple-element.42), channel_id=1, source_target_pairs={{0,6},{2,4},{4,2},{6,0},{1,7},{3,5},{5,3},{7,1},{8,14},{10,12},{12... | collective-permute-start | bytes 589832 | tf_op jit(solution)/shard_map/ppermute | solution.py:270
  175.8 1.1 collective-permute-done.20
  176.9 3.5 %collective-permute-done.21 = bf16[192,512]{1,0:T(8,128)(2,1)S(1)} collective-permute-done((bf16[192,512]{1,0:T(8,128)(2,1)S(1)}, bf16[192,512]{1,0:T(8,128)(2,1)S(1)}, u32[]{:S(2)}, u32[]{:S(2)}) %collective-permute-start.21) | collective-permute-done | bytes 196640 | tf_op jit(solution)/shard_map/ppermute | solution.py:270
  180.4 2.4 %collective-permute-done.22 = bf16[192,512]{1,0:T(8,128)(2,1)S(1)} collective-permute-done((bf16[192,512]{1,0:T(8,128)(2,1)S(1)}, bf16[192,512]{1,0:T(8,128)(2,1)S(1)}, u32[]{:S(2)}, u32[]{:S(2)}) %collective-permute-start.22) | collective-permute-done | bytes 196640 | tf_op jit(solution)/shard_map/ppermute | solution.py:270
  183.0 18.7 %collective-permute-start.23 = (bf16[192,512]{1,0:T(8,128)(2,1)S(1)}, bf16[192,512]{1,0:T(8,128)(2,1)S(1)}, u32[]{:S(2)}, u32[]{:S(2)}) collective-permute-start(bf16[192,512]{1,0:T(8,128)(2,1)S(1)} %fusion.3), channel_id=1, source_target_pairs={{8,0},{16,8},{24,16},{32,24},{40,32},{48,40},{56,48},{64,56},{72,6... | collective-permute-start | bytes 589832 | tf_op jit(solution)/shard_map/ppermute | solution.py:334
  201.7 3.2 %collective-permute-done.23 = bf16[192,512]{1,0:T(8,128)(2,1)S(1)} collective-permute-done((bf16[192,512]{1,0:T(8,128)(2,1)S(1)}, bf16[192,512]{1,0:T(8,128)(2,1)S(1)}, u32[]{:S(2)}, u32[]{:S(2)}) %collective-permute-start.23) | collective-permute-done | bytes 196640 | tf_op jit(solution)/shard_map/ppermute | solution.py:334
  204.9 0.7 copy.10
  (35 shorter events, 2.7 us)
Async XLA Ops:
  0.0 55.5 %copy-start.3 = (bf16[192,512]{1,0:T(8,128)(2,1)S(1)}, bf16[192,512]{1,0:T(8,128)(2,1)}, u32[]{:S(2)}) copy-start(bf16[192,512]{1,0:T(8,128)(2,1)} %param.10) | copy-start | bytes 589828
  0.0 66.3 %copy-start.4 = (s32[64]{0:T(128)S(1)}, s32[64]{0:T(128)}, u32[]{:S(2)}) copy-start(s32[64]{0:T(128)} %param.13) | copy-start | bytes 772
  15.8 12.7 %collective-permute-start.9 = (bf16[4,96,256]{2,1,0:T(8,128)(2,1)S(1)}, bf16[4,96,256]{2,1,0:T(8,128)(2,1)S(1)}, u32[]{:S(2)}, u32[]{:S(2)}) collective-permute-start(bf16[4,96,256]{2,1,0:T(8,128)(2,1)S(1)} %constant_dynamic-slice_fusion.refs_2_), channel_id=1, source_target_pairs={{0,120},{8,0},{16,8},{24,16},{32,24},{40,32},{48,40},{56,48},{64,5... | collective-permute-start | bytes 589832 | tf_op jit(solution)/shard_map/ppermute | solution.py:324
  25.3 8.8 %collective-permute-start.1 = (bf16[4,96,256]{2,1,0:T(8,128)(2,1)S(1)}, bf16[4,96,256]{2,1,0:T(8,128)(2,1)S(1)}, u32[]{:S(2)}, u32[]{:S(2)}) collective-permute-start(bf16[4,96,256]{2,1,0:T(8,128)(2,1)S(1)} %constant_dynamic-slice_fusion.refs_2_), channel_id=1, source_target_pairs={{0,8},{8,16},{16,24},{24,32},{32,40},{40,48},{48,56},{56,64},{64,7... | collective-permute-start | bytes 589832 | tf_op jit(solution)/shard_map/ppermute | solution.py:323
  28.5 8.9 %collective-permute-start.10 = (bf16[4,96,256]{2,1,0:T(8,128)(2,1)S(1)}, bf16[4,96,256]{2,1,0:T(8,128)(2,1)S(1)}, u32[]{:S(2)}, u32[]{:S(2)}) collective-permute-start(bf16[4,96,256]{2,1,0:T(8,128)(2,1)S(1)} %collective-permute-done.9.refs_4_), channel_id=1, source_target_pairs={{0,120},{8,0},{16,8},{24,16},{32,24},{40,32},{48,40},{56,48},{64,5... | collective-permute-start | bytes 589832 | tf_op jit(solution)/shard_map/ppermute | solution.py:324
  34.1 9.2 %collective-permute-start.2 = (bf16[4,96,256]{2,1,0:T(8,128)(2,1)S(1)}, bf16[4,96,256]{2,1,0:T(8,128)(2,1)S(1)}, u32[]{:S(2)}, u32[]{:S(2)}) collective-permute-start(bf16[4,96,256]{2,1,0:T(8,128)(2,1)S(1)} %collective-permute-done.1.refs_3_), channel_id=1, source_target_pairs={{0,8},{8,16},{16,24},{24,32},{32,40},{40,48},{48,56},{56,64},{64,7... | collective-permute-start | bytes 589832 | tf_op jit(solution)/shard_map/ppermute | solution.py:323
  37.3 10.0 %collective-permute-start.11 = (bf16[4,96,256]{2,1,0:T(8,128)(2,1)S(1)}, bf16[4,96,256]{2,1,0:T(8,128)(2,1)S(1)}, u32[]{:S(2)}, u32[]{:S(2)}) collective-permute-start(bf16[4,96,256]{2,1,0:T(8,128)(2,1)S(1)} %collective-permute-done.10.refs_3_), channel_id=1, source_target_pairs={{0,120},{8,0},{16,8},{24,16},{32,24},{40,32},{48,40},{56,48},{64,5... | collective-permute-start | bytes 589832 | tf_op jit(solution)/shard_map/ppermute | solution.py:324
  43.2 10.3 %collective-permute-start.3 = (bf16[4,96,256]{2,1,0:T(8,128)(2,1)S(1)}, bf16[4,96,256]{2,1,0:T(8,128)(2,1)S(1)}, u32[]{:S(2)}, u32[]{:S(2)}) collective-permute-start(bf16[4,96,256]{2,1,0:T(8,128)(2,1)S(1)} %collective-permute-done.2.refs_2_), channel_id=1, source_target_pairs={{0,8},{8,16},{16,24},{24,32},{32,40},{40,48},{48,56},{56,64},{64,7... | collective-permute-start | bytes 589832 | tf_op jit(solution)/shard_map/ppermute | solution.py:323
  47.4 10.1 %collective-permute-start.12 = (bf16[4,96,256]{2,1,0:T(8,128)(2,1)S(1)}, bf16[4,96,256]{2,1,0:T(8,128)(2,1)S(1)}, u32[]{:S(2)}, u32[]{:S(2)}) collective-permute-start(bf16[4,96,256]{2,1,0:T(8,128)(2,1)S(1)} %collective-permute-done.11.refs_5_), channel_id=1, source_target_pairs={{0,120},{8,0},{16,8},{24,16},{32,24},{40,32},{48,40},{56,48},{64,5... | collective-permute-start | bytes 589832 | tf_op jit(solution)/shard_map/ppermute | solution.py:324
  53.6 10.8 %collective-permute-start.4 = (bf16[4,96,256]{2,1,0:T(8,128)(2,1)S(1)}, bf16[4,96,256]{2,1,0:T(8,128)(2,1)S(1)}, u32[]{:S(2)}, u32[]{:S(2)}) collective-permute-start(bf16[4,96,256]{2,1,0:T(8,128)(2,1)S(1)} %collective-permute-done.3.refs_4_), channel_id=1, source_target_pairs={{0,8},{8,16},{16,24},{24,32},{32,40},{40,48},{48,56},{56,64},{64,7... | collective-permute-start | bytes 589832 | tf_op jit(solution)/shard_map/ppermute | solution.py:323
  55.5 20.7 %collective-permute-start = (bf16[192,1024]{1,0:T(8,128)(2,1)S(1)}, bf16[192,1024]{1,0:T(8,128)(2,1)S(1)}, u32[]{:S(2)}, u32[]{:S(2)}) collective-permute-start(bf16[192,1024]{1,0:T(8,128)(2,1)S(1)} %constant_dynamic-update-slice_fusion.refs_0_), channel_id=1, source_target_pairs={{0,384},{128,256},{256,128},{384,0},{1,385},{129,257},{257,129},{3... | collective-permute-start | bytes 1179656 | tf_op jit(solution)/shard_map/ppermute | solution.py:304
  57.5 10.9 %collective-permute-start.13 = (bf16[4,96,256]{2,1,0:T(8,128)(2,1)S(1)}, bf16[4,96,256]{2,1,0:T(8,128)(2,1)S(1)}, u32[]{:S(2)}, u32[]{:S(2)}) collective-permute-start(bf16[4,96,256]{2,1,0:T(8,128)(2,1)S(1)} %collective-permute-done.12.refs_3_), channel_id=1, source_target_pairs={{0,120},{8,0},{16,8},{24,16},{32,24},{40,32},{48,40},{56,48},{64,5... | collective-permute-start | bytes 589832 | tf_op jit(solution)/shard_map/ppermute | solution.py:324
  64.4 9.9 %collective-permute-start.5 = (bf16[4,96,256]{2,1,0:T(8,128)(2,1)S(1)}, bf16[4,96,256]{2,1,0:T(8,128)(2,1)S(1)}, u32[]{:S(2)}, u32[]{:S(2)}) collective-permute-start(bf16[4,96,256]{2,1,0:T(8,128)(2,1)S(1)} %collective-permute-done.4.refs_2_), channel_id=1, source_target_pairs={{0,8},{8,16},{16,24},{24,32},{32,40},{40,48},{48,56},{56,64},{64,7... | collective-permute-start | bytes 589832 | tf_op jit(solution)/shard_map/ppermute | solution.py:323
  68.4 20.6 %collective-permute-start.14 = (bf16[4,96,256]{2,1,0:T(8,128)(2,1)S(1)}, bf16[4,96,256]{2,1,0:T(8,128)(2,1)S(1)}, u32[]{:S(2)}, u32[]{:S(2)}) collective-permute-start(bf16[4,96,256]{2,1,0:T(8,128)(2,1)S(1)} %collective-permute-done.13.refs_5_), channel_id=1, source_target_pairs={{0,120},{8,0},{16,8},{24,16},{32,24},{40,32},{48,40},{56,48},{64,5... | collective-permute-start | bytes 589832 | tf_op jit(solution)/shard_map/ppermute | solution.py:324
  74.3 19.9 %collective-permute-start.6 = (bf16[4,96,256]{2,1,0:T(8,128)(2,1)S(1)}, bf16[4,96,256]{2,1,0:T(8,128)(2,1)S(1)}, u32[]{:S(2)}, u32[]{:S(2)}) collective-permute-start(bf16[4,96,256]{2,1,0:T(8,128)(2,1)S(1)} %collective-permute-done.5.refs_4_), channel_id=1, source_target_pairs={{0,8},{8,16},{16,24},{24,32},{32,40},{40,48},{48,56},{56,64},{64,7... | collective-permute-start | bytes 589832 | tf_op jit(solution)/shard_map/ppermute | solution.py:323
  89.0 21.9 %collective-permute-start.15 = (bf16[4,96,256]{2,1,0:T(8,128)(2,1)S(1)}, bf16[4,96,256]{2,1,0:T(8,128)(2,1)S(1)}, u32[]{:S(2)}, u32[]{:S(2)}) collective-permute-start(bf16[4,96,256]{2,1,0:T(8,128)(2,1)S(1)} %collective-permute-done.14.refs_3_), channel_id=1, source_target_pairs={{0,120},{8,0},{16,8},{24,16},{32,24},{40,32},{48,40},{56,48},{64,5... | collective-permute-start | bytes 589832 | tf_op jit(solution)/shard_map/ppermute | solution.py:324
  94.2 30.8 %collective-permute-start.7 = (bf16[4,96,256]{2,1,0:T(8,128)(2,1)S(1)}, bf16[4,96,256]{2,1,0:T(8,128)(2,1)S(1)}, u32[]{:S(2)}, u32[]{:S(2)}) collective-permute-start(bf16[4,96,256]{2,1,0:T(8,128)(2,1)S(1)} %collective-permute-done.6.refs_2_), channel_id=1, source_target_pairs={{0,8},{8,16},{16,24},{24,32},{32,40},{40,48},{48,56},{56,64},{64,7... | collective-permute-start | bytes 589832 | tf_op jit(solution)/shard_map/ppermute | solution.py:323
  110.9 29.5 %collective-permute-start.16 = (bf16[2,96,256]{2,1,0:T(8,128)(2,1)S(1)}, bf16[2,96,256]{2,1,0:T(8,128)(2,1)S(1)}, u32[]{:S(2)}, u32[]{:S(2)}) collective-permute-start(bf16[2,96,256]{2,1,0:T(8,128)(2,1)S(1)} %slice.25), channel_id=1, source_target_pairs={{0,120},{8,0},{16,8},{24,16},{32,24},{40,32},{48,40},{56,48},{64,5... | collective-permute-start | bytes 294920 | tf_op jit(solution)/shard_map/ppermute | solution.py:324
  125.0 15.4 %collective-permute-start.8 = (bf16[2,96,256]{2,1,0:T(8,128)(2,1)S(1)}, bf16[2,96,256]{2,1,0:T(8,128)(2,1)S(1)}, u32[]{:S(2)}, u32[]{:S(2)}) collective-permute-start(bf16[2,96,256]{2,1,0:T(8,128)(2,1)S(1)} %slice.24), channel_id=1, source_target_pairs={{0,8},{8,16},{16,24},{24,32},{32,40},{40,48},{48,56},{56,64},{64,7... | collective-permute-start | bytes 294920 | tf_op jit(solution)/shard_map/ppermute | solution.py:323
  146.3 11.1 %collective-permute-start.17 = (bf16[2,768,128]{2,1,0:T(8,128)(2,1)S(1)}, bf16[2,768,128]{2,1,0:T(8,128)(2,1)S(1)}, u32[]{:S(2)}, u32[]{:S(2)}) collective-permute-start(bf16[2,768,128]{2,1,0:T(8,128)(2,1)S(1)} %get-tuple-element.39), channel_id=1, source_target_pairs={{0,384},{128,256},{256,128},{384,0},{1,385},{129,257},{257,129},{3... | collective-permute-start | bytes 1179656 | tf_op jit(solution)/shard_map/ppermute | solution.py:331
  148.8 8.6 %collective-permute-start.18 = (f32[8,768]{1,0:T(8,128)S(1)}, f32[8,768]{1,0:T(8,128)S(1)}, u32[]{:S(2)}, u32[]{:S(2)}) collective-permute-start(f32[8,768]{1,0:T(8,128)S(1)} %get-tuple-element.40), channel_id=1, source_target_pairs={{0,384},{128,256},{256,128},{384,0},{1,385},{129,257},{257,129},{3... | collective-permute-start | bytes 73736 | tf_op jit(solution)/shard_map/ppermute | solution.py:332
  158.0 2.2 %copy-start = (bf16[4096,512]{1,0:T(8,128)(2,1)S(1)}, bf16[4096,512]{1,0:T(8,128)(2,1)}, u32[]{:S(2)}) copy-start(bf16[4096,512]{1,0:T(8,128)(2,1)} %w_ref.3) | copy-start | bytes 12582916
  160.1 3.3 %copy-start.1 = (bf16[4096,512]{1,0:T(8,128)(2,1)S(1)}, bf16[4096,512]{1,0:T(8,128)(2,1)}, u32[]{:S(2)}) copy-start(bf16[4096,512]{1,0:T(8,128)(2,1)} %w_ref.3) | copy-start | bytes 12582916
  161.5 4.2 %collective-permute-start.19 = (bf16[4,192,512]{2,1,0:T(8,128)(2,1)S(1)}, bf16[4,192,512]{2,1,0:T(8,128)(2,1)S(1)}, u32[]{:S(2)}, u32[]{:S(2)}) collective-permute-start(bf16[4,192,512]{2,1,0:T(8,128)(2,1)S(1)} %project.3), channel_id=1, source_target_pairs={{0,1},{1,0},{2,3},{3,2},{4,5},{5,4},{6,7},{7,6},{8,9},{9,8},{10,11... | collective-permute-start | bytes 2359304 | tf_op jit(solution)/shard_map/ppermute | solution.py:270
  164.9 17.9 %copy-start.2 = (bf16[192,512]{1,0:T(8,128)(2,1)S(1)}, bf16[192,512]{1,0:T(8,128)(2,1)}, u32[]{:S(2)}) copy-start(bf16[192,512]{1,0:T(8,128)(2,1)} %param.11) | copy-start | bytes 589828
  166.0 10.9 %collective-permute-start.20 = (bf16[192,512]{1,0:T(8,128)(2,1)S(1)}, bf16[192,512]{1,0:T(8,128)(2,1)S(1)}, u32[]{:S(2)}, u32[]{:S(2)}) collective-permute-start(bf16[192,512]{1,0:T(8,128)(2,1)S(1)} %get-tuple-element.41), channel_id=1, source_target_pairs={{0,4},{2,6},{4,0},{6,2},{1,5},{3,7},{5,1},{7,3},{8,12},{10,14},{12... | collective-permute-start | bytes 589832 | tf_op jit(solution)/shard_map/ppermute | solution.py:270
  171.1 9.3 %collective-permute-start.21 = (bf16[192,512]{1,0:T(8,128)(2,1)S(1)}, bf16[192,512]{1,0:T(8,128)(2,1)S(1)}, u32[]{:S(2)}, u32[]{:S(2)}) collective-permute-start(bf16[192,512]{1,0:T(8,128)(2,1)S(1)} %get-tuple-element.43), channel_id=1, source_target_pairs={{0,2},{2,0},{4,6},{6,4},{1,3},{3,1},{5,7},{7,5},{8,10},{10,8},{12,... | collective-permute-start | bytes 589832 | tf_op jit(solution)/shard_map/ppermute | solution.py:270
  173.2 9.6 %collective-permute-start.22 = (bf16[192,512]{1,0:T(8,128)(2,1)S(1)}, bf16[192,512]{1,0:T(8,128)(2,1)S(1)}, u32[]{:S(2)}, u32[]{:S(2)}) collective-permute-start(bf16[192,512]{1,0:T(8,128)(2,1)S(1)} %get-tuple-element.42), channel_id=1, source_target_pairs={{0,6},{2,4},{4,2},{6,0},{1,7},{3,5},{5,3},{7,1},{8,14},{10,12},{12... | collective-permute-start | bytes 589832 | tf_op jit(solution)/shard_map/ppermute | solution.py:270
  183.0 21.9 %collective-permute-start.23 = (bf16[192,512]{1,0:T(8,128)(2,1)S(1)}, bf16[192,512]{1,0:T(8,128)(2,1)S(1)}, u32[]{:S(2)}, u32[]{:S(2)}) collective-permute-start(bf16[192,512]{1,0:T(8,128)(2,1)S(1)} %fusion.3), channel_id=1, source_target_pairs={{8,0},{16,8},{24,16},{32,24},{40,32},{48,40},{56,48},{64,56},{72,6... | collective-permute-start | bytes 589832 | tf_op jit(solution)/shard_map/ppermute | solution.py:334

commit v4 on v2

--- a/solution.py
+++ b/solution.py
@@ -15,6 +15,7 @@
 SLOTS = HEADS * ROWS
 LOW = -1e30
 SLACK = 8.0
+REST = 4
 SCALE = WIDTH ** -0.5
 Y, Z, X, C = 4, 16, 4, 2
 
@@ -76,27 +77,28 @@
     used = collect(
         full, lambda p: (p + ROWS > lo) & (p <= base) & ((p < lo) | (p == base))
     )
-    groups = (used + group - 1) // group
-    for j in range(group - 1):
-
-        @pl.when(used + j < groups * group)
+    wholes = full // group
+    head = wholes * group
+    rests = (used - head + REST - 1) // REST
+    for j in range(REST - 1):
+
+        @pl.when(used + j < head + rests * REST)
         def _():
             buf[used + j] = jnp.zeros((ROWS, 2 * WIDTH), jnp.bfloat16)
             slot_pos[used + j] = jnp.int32(1 << 30)
 
     contract = (((1,), (1,)), ((), ()))
 
-    def visit(g, rows, masked):
-        start = g * group
-        kv = jnp.concatenate([buf[start + j] for j in range(group)], axis=0)
+    def visit(start, size, rows, masked):
+        kv = jnp.concatenate([buf[start + j] for j in range(size)], axis=0)
         k, v = kv[:, :WIDTH], kv[:, WIDTH:]
         kk = jnp.concatenate([k, k], axis=1)
         k1 = jnp.concatenate([k, jnp.ones_like(k)], axis=1)
         s = lax.dot_general(q_s[rows, :], kk, contract, preferred_element_type=jnp.float32)
         if masked:
             lane = lax.broadcasted_iota(jnp.int32, (1, ROWS), 1)
-            key_at = jnp.concatenate([lane + slot_pos[start + j] for j in range(group)], axis=1)
-            row = lax.broadcasted_iota(jnp.int32, (ROWS, group * ROWS), 0) + base
+            key_at = jnp.concatenate([lane + slot_pos[start + j] for j in range(size)], axis=1)
+            row = lax.broadcasted_iota(jnp.int32, (ROWS, size * ROWS), 0) + base
             inside = (key_at >= lo) & (key_at <= row)
             s = jnp.where(inside, s, LOW)
         top = jnp.max(s, axis=1, keepdims=True)
@@ -119,16 +121,15 @@
         )
         p_s[rows, :] += jnp.dot(prob.astype(jnp.bfloat16), k1, preferred_element_type=jnp.float32)
 
-    @pl.loop(0, groups)
-    def _(g):
-        whole = (g + 1) * group <= full
-        pl.when(whole)(lambda: visit(g, pl.ds(0, SLOTS), False))
-
-        @pl.when(jnp.logical_not(whole))
-        def _():
-            @pl.loop(0, HEADS)
-            def _(h):
-                visit(g, pl.ds(pl.multiple_of(h * ROWS, ROWS), ROWS), True)
+    @pl.loop(0, wholes * 2)
+    def _(i):
+        rows = pl.ds(pl.multiple_of(i % 2 * (SLOTS // 2), SLOTS // 2), SLOTS // 2)
+        visit(i // 2 * group, group, rows, False)
+
+    @pl.loop(0, rests * HEADS)
+    def _(i):
+        rows = pl.ds(pl.multiple_of(i % HEADS * ROWS, ROWS), ROWS)
+        visit(head + i // HEADS * REST, REST, rows, True)
 
     if last:
         l = p_s[:, WIDTH:]
@@ -151,7 +152,7 @@
     counts = tuple(a.shape[0] for a in arrays)
     first = state is None
     total = sum(counts)
-    group = {4: 4, 12: 6}.get(total, 8)
+    group = min(total, 8)
     shape = jax.ShapeDtypeStruct((SLOTS, WIDTH), jnp.float32)
     out_shape = jax.ShapeDtypeStruct((ROWS, HEADS * WIDTH), jnp.bfloat16) if last else [shape] * 3
     operands = [q, g, *arrays] + ([] if first else list(state))
@@ -255,10 +256,9 @@
         last = step == half
         below = lax.ppermute(below[: Y // 2] if last else below, "z", up)
         above = lax.ppermute(above[Y // 2 :] if last else above, "z", down)
-        if step % 2 == 0 or step == half - 1:
-            state = attention(par, pos, done, q, g, arrays, state, False)
-            done += sum(a.shape[0] for a in arrays)
-            arrays = []
+        state = attention(par, pos, done, q, g, arrays, state, False)
+        done += sum(a.shape[0] for a in arrays)
+        arrays = []
         arrays += [below, above]
     state = attention(par, pos, done, q, g, arrays, state, True)
     hidden = reduce_heads(state, w_query, d_out)

time: 195 us -> 224 us (1.15)
  starting transfers between devices: 80.2 us -> 94.2 us
  Pallas kernels: 49.5 us -> 63.2 us
    pallas_call x6 -> x9, Pallas kernels: 46.7 us -> 60.5 us  [attention(): pl.pallas_call(functools.partial(attend, counts, group, offset, first, la...]
    ppermute x1, starting transfers between devices: 6.21 us -> 18.7 us  [shards(): lax.ppermute(hidden, ('y', 'z'), [(i + 1, i) for i in range(Y * Z - 1)])]
    unnamed x17 -> x21, local copies, waits for them, and re-layouts: 4.05 us -> 4.78 us
  transfers between devices with their start and end apart: 21 -> 21, of which waited for: 15 -> 15; matrix products, arithmetic and copies ran while one was open for 1% -> 1% of each run, Pallas kernels for 22% -> 25%
where the time goes in v4:
time: 224 us; the launch traced here: 223 us
  starting transfers between devices  94.2 us (42%)
  Pallas kernels  63.2 us (28%)
  waiting for transfers between devices  42.3 us (19%)
  blocking collectives  14.9 us (7%)
  local copies, waits for them, and re-layouts  6.09 us (3%)
    pallas_call x9, Pallas kernels, attention(): pl.pallas_call(functools.partial(attend, counts, group, offset, first, la...  60.5 us
    ppermute x8, starting transfers between devices, shards(): above = lax.ppermute(above[Y // 2:] if last else above, 'z', down)  45 us
    ppermute x8, waiting for transfers between devices, shards(): above = lax.ppermute(above[Y // 2:] if last else above, 'z', down)  23.8 us
    ppermute x8, starting transfers between devices, shards(): below = lax.ppermute(below[:Y // 2] if last else below, 'z', up)  18.8 us
    ppermute x1, starting transfers between devices, shards(): lax.ppermute(hidden, ('y', 'z'), [(i + 1, i) for i in range(Y * Z - 1)])  18.7 us
    all_gather x1, blocking collectives, shards(): mine = lax.all_gather(jnp.concatenate([keys, values], axis=1), 'y', axis=0)  14.9 us
    ppermute x4, starting transfers between devices, exchange(): return lax.ppermute(value, axis, [(i, i ^ mask) for i in range(count)])  11.7 us
    ppermute x4, waiting for transfers between devices, exchange(): return lax.ppermute(value, axis, [(i, i ^ mask) for i in range(count)])  7.71 us
  transfers between devices with their start and end apart: 21, of which 15 were waited for; matrix products, arithmetic and copies ran while one was open for 1% of the time, Pallas kernels for 25%

profile of v4, /device:TPU:24, one launch (start us, length us, event | category | flops | bytes accessed | tf_op | source)
XLA Modules:
  0.0 223.1 jit_solution(1763571955383811522)
XLA Ops:
  0.8 14.9 %all-gather = bf16[768,256]{1,0:T(8,128)(2,1)S(1)} all-gather(bf16[192,256]{1,0:T(8,128)(2,1)S(1)} %pad_maximum_fusion), channel_id=2, replica_groups=mesh['y'=4,'z'=16,'x'=4,'core'=2] {'y'}, dimensions={0}, use_global_device_ids=true | all-gather | bytes 491520 | tf_op jit(solution)/shard_map/all_gather | solution.py:241
  15.7 9.5 %collective-permute-start.8 = (bf16[4,192,256]{2,1,0:T(8,128)(2,1)S(1)}, bf16[4,192,256]{2,1,0:T(8,128)(2,1)S(1)}, u32[]{:S(2)}, u32[]{:S(2)}) collective-permute-start(bf16[4,192,256]{2,1,0:T(8,128)(2,1)S(1)} %bitcast.13), channel_id=1, source_target_pairs={{0,120},{8,0},{16,8},{24,16},{32,24},{40,32},{48,40},{56,48},{64,5... | collective-permute-start | bytes 1179656 | tf_op jit(solution)/shard_map/ppermute | solution.py:258
  25.2 1.9 collective-permute-start
  27.1 3.3 %collective-permute-done.8.refs_3_ = bf16[4,192,256]{2,1,0:T(8,128)(2,1)S(1)} collective-permute-done((bf16[4,192,256]{2,1,0:T(8,128)(2,1)S(1)}, bf16[4,192,256]{2,1,0:T(8,128)(2,1)S(1)}, u32[]{:S(2)}, u32[]{:S(2)}) %collective-permute-start.8) | collective-permute-done | bytes 393248 | tf_op jit(solution)/shard_map/ppermute | solution.py:258
  30.5 5.6 %collective-permute-start.9 = (bf16[4,192,256]{2,1,0:T(8,128)(2,1)S(1)}, bf16[4,192,256]{2,1,0:T(8,128)(2,1)S(1)}, u32[]{:S(2)}, u32[]{:S(2)}) collective-permute-start(bf16[4,192,256]{2,1,0:T(8,128)(2,1)S(1)} %collective-permute-done.8.refs_3_), channel_id=1, source_target_pairs={{0,120},{8,0},{16,8},{24,16},{32,24},{40,32},{48,40},{56,48},{64,5... | collective-permute-start | bytes 1179656 | tf_op jit(solution)/shard_map/ppermute | solution.py:258
  36.1 1.9 collective-permute-start.1
  38.0 3.5 %collective-permute-done.9.refs_3_ = bf16[4,192,256]{2,1,0:T(8,128)(2,1)S(1)} collective-permute-done((bf16[4,192,256]{2,1,0:T(8,128)(2,1)S(1)}, bf16[4,192,256]{2,1,0:T(8,128)(2,1)S(1)}, u32[]{:S(2)}, u32[]{:S(2)}) %collective-permute-start.9) | collective-permute-done | bytes 393248 | tf_op jit(solution)/shard_map/ppermute | solution.py:258
  41.5 5.6 %collective-permute-start.10 = (bf16[4,192,256]{2,1,0:T(8,128)(2,1)S(1)}, bf16[4,192,256]{2,1,0:T(8,128)(2,1)S(1)}, u32[]{:S(2)}, u32[]{:S(2)}) collective-permute-start(bf16[4,192,256]{2,1,0:T(8,128)(2,1)S(1)} %collective-permute-done.9.refs_3_), channel_id=1, source_target_pairs={{0,120},{8,0},{16,8},{24,16},{32,24},{40,32},{48,40},{56,48},{64,5... | collective-permute-start | bytes 1179656 | tf_op jit(solution)/shard_map/ppermute | solution.py:258
  47.4 1.9 collective-permute-start.2
  50.0 3.6 %collective-permute-done.10.refs_3_ = bf16[4,192,256]{2,1,0:T(8,128)(2,1)S(1)} collective-permute-done((bf16[4,192,256]{2,1,0:T(8,128)(2,1)S(1)}, bf16[4,192,256]{2,1,0:T(8,128)(2,1)S(1)}, u32[]{:S(2)}, u32[]{:S(2)}) %collective-permute-start.10) | collective-permute-done | bytes 393248 | tf_op jit(solution)/shard_map/ppermute | solution.py:258
  53.6 5.6 %collective-permute-start.11 = (bf16[4,192,256]{2,1,0:T(8,128)(2,1)S(1)}, bf16[4,192,256]{2,1,0:T(8,128)(2,1)S(1)}, u32[]{:S(2)}, u32[]{:S(2)}) collective-permute-start(bf16[4,192,256]{2,1,0:T(8,128)(2,1)S(1)} %collective-permute-done.10.refs_3_), channel_id=1, source_target_pairs={{0,120},{8,0},{16,8},{24,16},{32,24},{40,32},{48,40},{56,48},{64,5... | collective-permute-start | bytes 1179656 | tf_op jit(solution)/shard_map/ppermute | solution.py:258
  60.0 1.9 collective-permute-start.3
  62.7 4.3 %collective-permute-done.11.refs_3_ = bf16[4,192,256]{2,1,0:T(8,128)(2,1)S(1)} collective-permute-done((bf16[4,192,256]{2,1,0:T(8,128)(2,1)S(1)}, bf16[4,192,256]{2,1,0:T(8,128)(2,1)S(1)}, u32[]{:S(2)}, u32[]{:S(2)}) %collective-permute-start.11) | collective-permute-done | bytes 393248 | tf_op jit(solution)/shard_map/ppermute | solution.py:258
  66.9 5.6 %collective-permute-start.12 = (bf16[4,192,256]{2,1,0:T(8,128)(2,1)S(1)}, bf16[4,192,256]{2,1,0:T(8,128)(2,1)S(1)}, u32[]{:S(2)}, u32[]{:S(2)}) collective-permute-start(bf16[4,192,256]{2,1,0:T(8,128)(2,1)S(1)} %collective-permute-done.11.refs_3_), channel_id=1, source_target_pairs={{0,120},{8,0},{16,8},{24,16},{32,24},{40,32},{48,40},{56,48},{64,5... | collective-permute-start | bytes 1179656 | tf_op jit(solution)/shard_map/ppermute | solution.py:258
  72.5 1.2 collective-permute-done.3.refs_2_
  73.8 1.9 collective-permute-start.4
  75.7 5.7 %collective-permute-done.12.refs_3_ = bf16[4,192,256]{2,1,0:T(8,128)(2,1)S(1)} collective-permute-done((bf16[4,192,256]{2,1,0:T(8,128)(2,1)S(1)}, bf16[4,192,256]{2,1,0:T(8,128)(2,1)S(1)}, u32[]{:S(2)}, u32[]{:S(2)}) %collective-permute-start.12) | collective-permute-done | bytes 393248 | tf_op jit(solution)/shard_map/ppermute | solution.py:258
  81.4 5.6 %collective-permute-start.13 = (bf16[4,192,256]{2,1,0:T(8,128)(2,1)S(1)}, bf16[4,192,256]{2,1,0:T(8,128)(2,1)S(1)}, u32[]{:S(2)}, u32[]{:S(2)}) collective-permute-start(bf16[4,192,256]{2,1,0:T(8,128)(2,1)S(1)} %collective-permute-done.12.refs_3_), channel_id=1, source_target_pairs={{0,120},{8,0},{16,8},{24,16},{32,24},{40,32},{48,40},{56,48},{64,5... | collective-permute-start | bytes 1179656 | tf_op jit(solution)/shard_map/ppermute | solution.py:258
  87.0 1.7 collective-permute-done.4.refs_2_
  88.7 1.9 collective-permute-start.5
  90.6 1.2 dynamic_slice.3
  92.5 3.4 %collective-permute-done.13.refs_3_ = bf16[4,192,256]{2,1,0:T(8,128)(2,1)S(1)} collective-permute-done((bf16[4,192,256]{2,1,0:T(8,128)(2,1)S(1)}, bf16[4,192,256]{2,1,0:T(8,128)(2,1)S(1)}, u32[]{:S(2)}, u32[]{:S(2)}) %collective-permute-start.13) | collective-permute-done | bytes 393248 | tf_op jit(solution)/shard_map/ppermute | solution.py:258
  95.9 5.6 %collective-permute-start.14 = (bf16[4,192,256]{2,1,0:T(8,128)(2,1)S(1)}, bf16[4,192,256]{2,1,0:T(8,128)(2,1)S(1)}, u32[]{:S(2)}, u32[]{:S(2)}) collective-permute-start(bf16[4,192,256]{2,1,0:T(8,128)(2,1)S(1)} %collective-permute-done.13.refs_3_), channel_id=1, source_target_pairs={{0,120},{8,0},{16,8},{24,16},{32,24},{40,32},{48,40},{56,48},{64,5... | collective-permute-start | bytes 1179656 | tf_op jit(solution)/shard_map/ppermute | solution.py:258
  101.5 1.7 collective-permute-done.5.refs_2_
  103.2 1.9 collective-permute-start.6
  106.1 0.9 copy-done.2
  107.0 5.5 %attend.9 = (f32[768,128]{1,0:T(8,128)S(1)}, f32[768,128]{1,0:T(8,128)S(1)}, f32[768,128]{1,0:T(8,128)S(1)}) custom-call(s32[2]{0:T(128)S(1)} %compare_select_fusion.3.par_ref, s32[64]{0:T(128)S(1)} %fusion.6.pos_ref, bf16[192,512]{1,0:T(8,128)(2,1)S(1)} %copy-done.1, bf16[192,512]{1,0:T(8,128)(2,1)S(1)} %copy-done.2, bf16[4,192,256]{2,1,0:T(8,128)(2,1)S(1)} %bitcast.15), custom_call_target="tpu_custom_call" | custom-call | flops 301989888 | bytes 2752512 | tf_op jit(solution)/shard_map/attend/pallas_call | solution.py:161
  112.5 10.1 %attend.10 = (f32[768,128]{1,0:T(8,128)S(1)}, f32[768,128]{1,0:T(8,128)S(1)}, f32[768,128]{1,0:T(8,128)S(1)}) custom-call(s32[2]{0:T(128)S(1)} %compare_select_fusion.3.par_ref, s32[64]{0:T(128)S(1)} %fusion.6.pos_ref, bf16[192,512]{1,0:T(8,128)(2,1)S(1)} %copy-done.1, bf16[192,512]{1,0:T(8,128)(2,1)S(1)} %copy-done.2, ...), custom_call_target="tpu_custom_call" | custom-call | flops 603979776 | bytes 3145728 | tf_op jit(solution)/shard_map/attend/pallas_call | solution.py:161
  122.6 10.1 %attend.11 = (f32[768,128]{1,0:T(8,128)S(1)}, f32[768,128]{1,0:T(8,128)S(1)}, f32[768,128]{1,0:T(8,128)S(1)}) custom-call(s32[2]{0:T(128)S(1)} %compare_select_fusion.3.par_ref, s32[64]{0:T(128)S(1)} %fusion.6.pos_ref, bf16[192,512]{1,0:T(8,128)(2,1)S(1)} %copy-done.1, bf16[192,512]{1,0:T(8,128)(2,1)S(1)} %copy-done.2, bf16[4,192,256]{2,1,0:T(8,128)(2,1)S(1)} %copy-done.6, ...), custom_call_target="tpu_custom_call" | custom-call | flops 603979776 | bytes 3145728 | tf_op jit(solution)/shard_map/attend/pallas_call | solution.py:161
  132.7 5.9 %attend.12 = (f32[768,128]{1,0:T(8,128)S(1)}, f32[768,128]{1,0:T(8,128)S(1)}, f32[768,128]{1,0:T(8,128)S(1)}) custom-call(s32[2]{0:T(128)S(1)} %compare_select_fusion.3.par_ref, s32[64]{0:T(128)S(1)} %fusion.6.pos_ref, bf16[192,512]{1,0:T(8,128)(2,1)S(1)} %copy-done.1, bf16[192,512]{1,0:T(8,128)(2,1)S(1)} %copy-done.2, bf16[4,192,256]{2,1,0:T(8,128)(2,1)S(1)} %copy-done.8, ...), custom_call_target="tpu_custom_call" | custom-call | flops 603979776 | bytes 3145728 | tf_op jit(solution)/shard_map/attend/pallas_call | solution.py:161
  138.7 1.9 collective-permute-start.15
  140.6 5.4 %collective-permute-start.7 = (bf16[2,192,256]{2,1,0:T(8,128)(2,1)S(1)}, bf16[2,192,256]{2,1,0:T(8,128)(2,1)S(1)}, u32[]{:S(2)}, u32[]{:S(2)}) collective-permute-start(bf16[2,192,256]{2,1,0:T(8,128)(2,1)S(1)} %slice.24), channel_id=1, source_target_pairs={{0,8},{8,16},{16,24},{24,32},{32,40},{40,48},{48,56},{56,64},{64,7... | collective-permute-start | bytes 589832 | tf_op jit(solution)/shard_map/ppermute | solution.py:257
  146.0 5.5 %attend.13 = (f32[768,128]{1,0:T(8,128)S(1)}, f32[768,128]{1,0:T(8,128)S(1)}, f32[768,128]{1,0:T(8,128)S(1)}) custom-call(s32[2]{0:T(128)S(1)} %compare_select_fusion.3.par_ref, s32[64]{0:T(128)S(1)} %fusion.6.pos_ref, bf16[192,512]{1,0:T(8,128)(2,1)S(1)} %copy-done.1, bf16[192,512]{1,0:T(8,128)(2,1)S(1)} %copy-done.2, ...), custom_call_target="tpu_custom_call" | custom-call | flops 603979776 | bytes 3145728 | tf_op jit(solution)/shard_map/attend/pallas_call | solution.py:161
  151.6 5.7 %attend.14 = (f32[768,128]{1,0:T(8,128)S(1)}, f32[768,128]{1,0:T(8,128)S(1)}, f32[768,128]{1,0:T(8,128)S(1)}) custom-call(s32[2]{0:T(128)S(1)} %compare_select_fusion.3.par_ref, s32[64]{0:T(128)S(1)} %fusion.6.pos_ref, bf16[192,512]{1,0:T(8,128)(2,1)S(1)} %copy-done.1, bf16[192,512]{1,0:T(8,128)(2,1)S(1)} %copy-done.2, ...), custom_call_target="tpu_custom_call" | custom-call | flops 603979776 | bytes 3145728 | tf_op jit(solution)/shard_map/attend/pallas_call | solution.py:161
  157.3 6.2 %attend.15 = (f32[768,128]{1,0:T(8,128)S(1)}, f32[768,128]{1,0:T(8,128)S(1)}, f32[768,128]{1,0:T(8,128)S(1)}) custom-call(s32[2]{0:T(128)S(1)} %compare_select_fusion.3.par_ref, s32[64]{0:T(128)S(1)} %fusion.6.pos_ref, bf16[192,512]{1,0:T(8,128)(2,1)S(1)} %copy-done.1, bf16[192,512]{1,0:T(8,128)(2,1)S(1)} %copy-done.2, ...), custom_call_target="tpu_custom_call" | custom-call | flops 603979776 | bytes 3145728 | tf_op jit(solution)/shard_map/attend/pallas_call | solution.py:161
  163.6 6.1 %attend.16 = (f32[768,128]{1,0:T(8,128)S(1)}, f32[768,128]{1,0:T(8,128)S(1)}, f32[768,128]{1,0:T(8,128)S(1)}) custom-call(s32[2]{0:T(128)S(1)} %compare_select_fusion.3.par_ref, s32[64]{0:T(128)S(1)} %fusion.6.pos_ref, bf16[192,512]{1,0:T(8,128)(2,1)S(1)} %copy-done.1, bf16[192,512]{1,0:T(8,128)(2,1)S(1)} %copy-done.2, ...), custom_call_target="tpu_custom_call" | custom-call | flops 603979776 | bytes 3145728 | tf_op jit(solution)/shard_map/attend/pallas_call | solution.py:161
  169.6 5.4 %attend.17.gq_ref = bf16[192,512]{1,0:T(8,128)(2,1)S(1)} custom-call(s32[2]{0:T(128)S(1)} %compare_select_fusion.3.par_ref, s32[64]{0:T(128)S(1)} %fusion.6.pos_ref, bf16[192,512]{1,0:T(8,128)(2,1)S(1)} %copy-done.1, bf16[192,512]{1,0:T(8,128)(2,1)S(1)} %copy-done.2, bf16[2,192,256]{2,1,0:T(8,128)(2,1)S(1)} %collective-permute-done.7.refs_2_, ...), custom_call_target="tpu_custom_call" | custom-call | flops 301989888 | bytes 2752512 | tf_op jit(solution)/shard_map/attend/pallas_call | solution.py:161
  175.1 1.4 project.3
  176.4 1.9 collective-permute-start.16
  178.4 1.4 project.2
  180.9 4.2 %collective-permute-start.17 = (bf16[192,512]{1,0:T(8,128)(2,1)S(1)}, bf16[192,512]{1,0:T(8,128)(2,1)S(1)}, u32[]{:S(2)}, u32[]{:S(2)}) collective-permute-start(bf16[192,512]{1,0:T(8,128)(2,1)S(1)} %get-tuple-element.53), channel_id=1, source_target_pairs={{0,4},{2,6},{4,0},{6,2},{1,5},{3,7},{5,1},{7,3},{8,12},{10,14},{12... | collective-permute-start | bytes 589832 | tf_op jit(solution)/shard_map/ppermute | solution.py:212
  185.2 3.0 %collective-permute-start.18 = (bf16[192,512]{1,0:T(8,128)(2,1)S(1)}, bf16[192,512]{1,0:T(8,128)(2,1)S(1)}, u32[]{:S(2)}, u32[]{:S(2)}) collective-permute-start(bf16[192,512]{1,0:T(8,128)(2,1)S(1)} %get-tuple-element.55), channel_id=1, source_target_pairs={{0,2},{2,0},{4,6},{6,4},{1,3},{3,1},{5,7},{7,5},{8,10},{10,8},{12,... | collective-permute-start | bytes 589832 | tf_op jit(solution)/shard_map/ppermute | solution.py:212
  188.1 2.6 %collective-permute-start.19 = (bf16[192,512]{1,0:T(8,128)(2,1)S(1)}, bf16[192,512]{1,0:T(8,128)(2,1)S(1)}, u32[]{:S(2)}, u32[]{:S(2)}) collective-permute-start(bf16[192,512]{1,0:T(8,128)(2,1)S(1)} %get-tuple-element.54), channel_id=1, source_target_pairs={{0,6},{2,4},{4,2},{6,0},{1,7},{3,5},{5,3},{7,1},{8,14},{10,12},{12... | collective-permute-start | bytes 589832 | tf_op jit(solution)/shard_map/ppermute | solution.py:212
  190.7 1.3 collective-permute-done.17
  192.1 3.3 %collective-permute-done.18 = bf16[192,512]{1,0:T(8,128)(2,1)S(1)} collective-permute-done((bf16[192,512]{1,0:T(8,128)(2,1)S(1)}, bf16[192,512]{1,0:T(8,128)(2,1)S(1)}, u32[]{:S(2)}, u32[]{:S(2)}) %collective-permute-start.18) | collective-permute-done | bytes 196640 | tf_op jit(solution)/shard_map/ppermute | solution.py:212
  195.3 2.3 %collective-permute-done.19 = bf16[192,512]{1,0:T(8,128)(2,1)S(1)} collective-permute-done((bf16[192,512]{1,0:T(8,128)(2,1)S(1)}, bf16[192,512]{1,0:T(8,128)(2,1)S(1)}, u32[]{:S(2)}, u32[]{:S(2)}) %collective-permute-start.19) | collective-permute-done | bytes 196640 | tf_op jit(solution)/shard_map/ppermute | solution.py:212
  197.8 18.7 %collective-permute-start.20 = (bf16[192,512]{1,0:T(8,128)(2,1)S(1)}, bf16[192,512]{1,0:T(8,128)(2,1)S(1)}, u32[]{:S(2)}, u32[]{:S(2)}) collective-permute-start(bf16[192,512]{1,0:T(8,128)(2,1)S(1)} %fusion.3), channel_id=1, source_target_pairs={{8,0},{16,8},{24,16},{32,24},{40,32},{48,40},{56,48},{64,56},{72,6... | collective-permute-start | bytes 589832 | tf_op jit(solution)/shard_map/ppermute | solution.py:265
  216.5 5.9 %collective-permute-done.20 = bf16[192,512]{1,0:T(8,128)(2,1)S(1)} collective-permute-done((bf16[192,512]{1,0:T(8,128)(2,1)S(1)}, bf16[192,512]{1,0:T(8,128)(2,1)S(1)}, u32[]{:S(2)}, u32[]{:S(2)}) %collective-permute-start.20) | collective-permute-done | bytes 196640 | tf_op jit(solution)/shard_map/ppermute | solution.py:265
  (38 shorter events, 6.3 us)
Async XLA Ops:
  15.7 14.8 %collective-permute-start.8 = (bf16[4,192,256]{2,1,0:T(8,128)(2,1)S(1)}, bf16[4,192,256]{2,1,0:T(8,128)(2,1)S(1)}, u32[]{:S(2)}, u32[]{:S(2)}) collective-permute-start(bf16[4,192,256]{2,1,0:T(8,128)(2,1)S(1)} %bitcast.13), channel_id=1, source_target_pairs={{0,120},{8,0},{16,8},{24,16},{32,24},{40,32},{48,40},{56,48},{64,5... | collective-permute-start | bytes 1179656 | tf_op jit(solution)/shard_map/ppermute | solution.py:258
  25.2 10.9 %collective-permute-start = (bf16[4,192,256]{2,1,0:T(8,128)(2,1)S(1)}, bf16[4,192,256]{2,1,0:T(8,128)(2,1)S(1)}, u32[]{:S(2)}, u32[]{:S(2)}) collective-permute-start(bf16[4,192,256]{2,1,0:T(8,128)(2,1)S(1)} %bitcast.14), channel_id=1, source_target_pairs={{0,8},{8,16},{16,24},{24,32},{32,40},{40,48},{48,56},{56,64},{64,7... | collective-permute-start | bytes 1179656 | tf_op jit(solution)/shard_map/ppermute | solution.py:257
  30.5 11.0 %collective-permute-start.9 = (bf16[4,192,256]{2,1,0:T(8,128)(2,1)S(1)}, bf16[4,192,256]{2,1,0:T(8,128)(2,1)S(1)}, u32[]{:S(2)}, u32[]{:S(2)}) collective-permute-start(bf16[4,192,256]{2,1,0:T(8,128)(2,1)S(1)} %collective-permute-done.8.refs_3_), channel_id=1, source_target_pairs={{0,120},{8,0},{16,8},{24,16},{32,24},{40,32},{48,40},{56,48},{64,5... | collective-permute-start | bytes 1179656 | tf_op jit(solution)/shard_map/ppermute | solution.py:258
  36.1 11.3 %collective-permute-start.1 = (bf16[4,192,256]{2,1,0:T(8,128)(2,1)S(1)}, bf16[4,192,256]{2,1,0:T(8,128)(2,1)S(1)}, u32[]{:S(2)}, u32[]{:S(2)}) collective-permute-start(bf16[4,192,256]{2,1,0:T(8,128)(2,1)S(1)} %collective-permute-done.refs_2_), channel_id=1, source_target_pairs={{0,8},{8,16},{16,24},{24,32},{32,40},{40,48},{48,56},{56,64},{64,7... | collective-permute-start | bytes 1179656 | tf_op jit(solution)/shard_map/ppermute | solution.py:257
  41.5 12.1 %collective-permute-start.10 = (bf16[4,192,256]{2,1,0:T(8,128)(2,1)S(1)}, bf16[4,192,256]{2,1,0:T(8,128)(2,1)S(1)}, u32[]{:S(2)}, u32[]{:S(2)}) collective-permute-start(bf16[4,192,256]{2,1,0:T(8,128)(2,1)S(1)} %collective-permute-done.9.refs_3_), channel_id=1, source_target_pairs={{0,120},{8,0},{16,8},{24,16},{32,24},{40,32},{48,40},{56,48},{64,5... | collective-permute-start | bytes 1179656 | tf_op jit(solution)/shard_map/ppermute | solution.py:258
  47.4 12.6 %collective-permute-start.2 = (bf16[4,192,256]{2,1,0:T(8,128)(2,1)S(1)}, bf16[4,192,256]{2,1,0:T(8,128)(2,1)S(1)}, u32[]{:S(2)}, u32[]{:S(2)}) collective-permute-start(bf16[4,192,256]{2,1,0:T(8,128)(2,1)S(1)} %collective-permute-done.1.refs_2_), channel_id=1, source_target_pairs={{0,8},{8,16},{16,24},{24,32},{32,40},{40,48},{48,56},{56,64},{64,7... | collective-permute-start | bytes 1179656 | tf_op jit(solution)/shard_map/ppermute | solution.py:257
  49.3 0.7 copy-start.5
  53.6 13.3 %collective-permute-start.11 = (bf16[4,192,256]{2,1,0:T(8,128)(2,1)S(1)}, bf16[4,192,256]{2,1,0:T(8,128)(2,1)S(1)}, u32[]{:S(2)}, u32[]{:S(2)}) collective-permute-start(bf16[4,192,256]{2,1,0:T(8,128)(2,1)S(1)} %collective-permute-done.10.refs_3_), channel_id=1, source_target_pairs={{0,120},{8,0},{16,8},{24,16},{32,24},{40,32},{48,40},{56,48},{64,5... | collective-permute-start | bytes 1179656 | tf_op jit(solution)/shard_map/ppermute | solution.py:258
  59.2 0.8 copy-start.3
  60.0 13.8 %collective-permute-start.3 = (bf16[4,192,256]{2,1,0:T(8,128)(2,1)S(1)}, bf16[4,192,256]{2,1,0:T(8,128)(2,1)S(1)}, u32[]{:S(2)}, u32[]{:S(2)}) collective-permute-start(bf16[4,192,256]{2,1,0:T(8,128)(2,1)S(1)} %collective-permute-done.2.refs_2_), channel_id=1, source_target_pairs={{0,8},{8,16},{16,24},{24,32},{32,40},{40,48},{48,56},{56,64},{64,7... | collective-permute-start | bytes 1179656 | tf_op jit(solution)/shard_map/ppermute | solution.py:257
  61.9 0.7 copy-start.7
  66.9 14.4 %collective-permute-start.12 = (bf16[4,192,256]{2,1,0:T(8,128)(2,1)S(1)}, bf16[4,192,256]{2,1,0:T(8,128)(2,1)S(1)}, u32[]{:S(2)}, u32[]{:S(2)}) collective-permute-start(bf16[4,192,256]{2,1,0:T(8,128)(2,1)S(1)} %collective-permute-done.11.refs_3_), channel_id=1, source_target_pairs={{0,120},{8,0},{16,8},{24,16},{32,24},{40,32},{48,40},{56,48},{64,5... | collective-permute-start | bytes 1179656 | tf_op jit(solution)/shard_map/ppermute | solution.py:258
  73.8 14.9 %collective-permute-start.4 = (bf16[4,192,256]{2,1,0:T(8,128)(2,1)S(1)}, bf16[4,192,256]{2,1,0:T(8,128)(2,1)S(1)}, u32[]{:S(2)}, u32[]{:S(2)}) collective-permute-start(bf16[4,192,256]{2,1,0:T(8,128)(2,1)S(1)} %collective-permute-done.3.refs_2_), channel_id=1, source_target_pairs={{0,8},{8,16},{16,24},{24,32},{32,40},{40,48},{48,56},{56,64},{64,7... | collective-permute-start | bytes 1179656 | tf_op jit(solution)/shard_map/ppermute | solution.py:257
  81.4 14.6 %collective-permute-start.13 = (bf16[4,192,256]{2,1,0:T(8,128)(2,1)S(1)}, bf16[4,192,256]{2,1,0:T(8,128)(2,1)S(1)}, u32[]{:S(2)}, u32[]{:S(2)}) collective-permute-start(bf16[4,192,256]{2,1,0:T(8,128)(2,1)S(1)} %collective-permute-done.12.refs_3_), channel_id=1, source_target_pairs={{0,120},{8,0},{16,8},{24,16},{32,24},{40,32},{48,40},{56,48},{64,5... | collective-permute-start | bytes 1179656 | tf_op jit(solution)/shard_map/ppermute | solution.py:258
  88.7 14.5 %collective-permute-start.5 = (bf16[4,192,256]{2,1,0:T(8,128)(2,1)S(1)}, bf16[4,192,256]{2,1,0:T(8,128)(2,1)}, u32[]{:S(2)}, u32[]{:S(2)}) collective-permute-start(bf16[4,192,256]{2,1,0:T(8,128)(2,1)S(1)} %collective-permute-done.4.refs_2_), channel_id=1, source_target_pairs={{0,8},{8,16},{16,24},{24,32},{32,40},{40,48},{48,56},{56,64},{64,7... | collective-permute-start | bytes 1179656 | tf_op jit(solution)/shard_map/ppermute | solution.py:257
  95.9 42.7 %collective-permute-start.14 = (bf16[4,192,256]{2,1,0:T(8,128)(2,1)S(1)}, bf16[4,192,256]{2,1,0:T(8,128)(2,1)S(1)}, u32[]{:S(2)}, u32[]{:S(2)}) collective-permute-start(bf16[4,192,256]{2,1,0:T(8,128)(2,1)S(1)} %collective-permute-done.13.refs_3_), channel_id=1, source_target_pairs={{0,120},{8,0},{16,8},{24,16},{32,24},{40,32},{48,40},{56,48},{64,5... | collective-permute-start | bytes 1179656 | tf_op jit(solution)/shard_map/ppermute | solution.py:258
  103.2 37.4 %collective-permute-start.6 = (bf16[4,192,256]{2,1,0:T(8,128)(2,1)}, bf16[4,192,256]{2,1,0:T(8,128)(2,1)S(1)}, u32[]{:S(2)}, u32[]{:S(2)}) collective-permute-start(bf16[4,192,256]{2,1,0:T(8,128)(2,1)} %collective-permute-done.5.refs_2_), channel_id=1, source_target_pairs={{0,8},{8,16},{16,24},{24,32},{32,40},{40,48},{48,56},{56,64},{64,7... | collective-permute-start | bytes 1179656 | tf_op jit(solution)/shard_map/ppermute | solution.py:257
  105.1 0.9 copy-start.1
  106.1 0.9 copy-start.2
  107.0 15.6 %copy-start.6 = (bf16[4,192,256]{2,1,0:T(8,128)(2,1)S(1)}, bf16[4,192,256]{2,1,0:T(8,128)(2,1)}, u32[]{:S(2)}) copy-start(bf16[4,192,256]{2,1,0:T(8,128)(2,1)} %copy-done.5) | copy-start | bytes 1179652
  122.6 10.1 %copy-start.4 = (bf16[4,192,256]{2,1,0:T(8,128)(2,1)S(1)}, bf16[4,192,256]{2,1,0:T(8,128)(2,1)}, u32[]{:S(2)}) copy-start(bf16[4,192,256]{2,1,0:T(8,128)(2,1)} %copy-done.3) | copy-start | bytes 1179652
  122.6 10.1 %copy-start.8 = (bf16[4,192,256]{2,1,0:T(8,128)(2,1)S(1)}, bf16[4,192,256]{2,1,0:T(8,128)(2,1)}, u32[]{:S(2)}) copy-start(bf16[4,192,256]{2,1,0:T(8,128)(2,1)} %copy-done.7) | copy-start | bytes 1179652
  138.7 31.0 %collective-permute-start.15 = (bf16[2,192,256]{2,1,0:T(8,128)(2,1)S(1)}, bf16[2,192,256]{2,1,0:T(8,128)(2,1)S(1)}, u32[]{:S(2)}, u32[]{:S(2)}) collective-permute-start(bf16[2,192,256]{2,1,0:T(8,128)(2,1)S(1)} %slice.25), channel_id=1, source_target_pairs={{0,120},{8,0},{16,8},{24,16},{32,24},{40,32},{48,40},{56,48},{64,5... | collective-permute-start | bytes 589832 | tf_op jit(solution)/shard_map/ppermute | solution.py:258
  140.6 29.0 %collective-permute-start.7 = (bf16[2,192,256]{2,1,0:T(8,128)(2,1)S(1)}, bf16[2,192,256]{2,1,0:T(8,128)(2,1)S(1)}, u32[]{:S(2)}, u32[]{:S(2)}) collective-permute-start(bf16[2,192,256]{2,1,0:T(8,128)(2,1)S(1)} %slice.24), channel_id=1, source_target_pairs={{0,8},{8,16},{16,24},{24,32},{32,40},{40,48},{48,56},{56,64},{64,7... | collective-permute-start | bytes 589832 | tf_op jit(solution)/shard_map/ppermute | solution.py:257
  163.5 11.5 %copy-start = (bf16[4096,512]{1,0:T(8,128)(2,1)S(1)}, bf16[4096,512]{1,0:T(8,128)(2,1)}, u32[]{:S(2)}) copy-start(bf16[4096,512]{1,0:T(8,128)(2,1)} %w_ref.3) | copy-start | bytes 12582916
  176.4 4.2 %collective-permute-start.16 = (bf16[4,192,512]{2,1,0:T(8,128)(2,1)S(1)}, bf16[4,192,512]{2,1,0:T(8,128)(2,1)S(1)}, u32[]{:S(2)}, u32[]{:S(2)}) collective-permute-start(bf16[4,192,512]{2,1,0:T(8,128)(2,1)S(1)} %project.3), channel_id=1, source_target_pairs={{0,1},{1,0},{2,3},{3,2},{4,5},{5,4},{6,7},{7,6},{8,9},{9,8},{10,11... | collective-permute-start | bytes 2359304 | tf_op jit(solution)/shard_map/ppermute | solution.py:212
  179.8 17.9 %copy-start.9 = (bf16[192,512]{1,0:T(8,128)(2,1)S(1)}, bf16[192,512]{1,0:T(8,128)(2,1)}, u32[]{:S(2)}) copy-start(bf16[192,512]{1,0:T(8,128)(2,1)} %param.11) | copy-start | bytes 589828
  180.9 11.2 %collective-permute-start.17 = (bf16[192,512]{1,0:T(8,128)(2,1)S(1)}, bf16[192,512]{1,0:T(8,128)(2,1)S(1)}, u32[]{:S(2)}, u32[]{:S(2)}) collective-permute-start(bf16[192,512]{1,0:T(8,128)(2,1)S(1)} %get-tuple-element.53), channel_id=1, source_target_pairs={{0,4},{2,6},{4,0},{6,2},{1,5},{3,7},{5,1},{7,3},{8,12},{10,14},{12... | collective-permute-start | bytes 589832 | tf_op jit(solution)/shard_map/ppermute | solution.py:212
  185.2 10.2 %collective-permute-start.18 = (bf16[192,512]{1,0:T(8,128)(2,1)S(1)}, bf16[192,512]{1,0:T(8,128)(2,1)S(1)}, u32[]{:S(2)}, u32[]{:S(2)}) collective-permute-start(bf16[192,512]{1,0:T(8,128)(2,1)S(1)} %get-tuple-element.55), channel_id=1, source_target_pairs={{0,2},{2,0},{4,6},{6,4},{1,3},{3,1},{5,7},{7,5},{8,10},{10,8},{12,... | collective-permute-start | bytes 589832 | tf_op jit(solution)/shard_map/ppermute | solution.py:212
  188.1 9.5 %collective-permute-start.19 = (bf16[192,512]{1,0:T(8,128)(2,1)S(1)}, bf16[192,512]{1,0:T(8,128)(2,1)S(1)}, u32[]{:S(2)}, u32[]{:S(2)}) collective-permute-start(bf16[192,512]{1,0:T(8,128)(2,1)S(1)} %get-tuple-element.54), channel_id=1, source_target_pairs={{0,6},{2,4},{4,2},{6,0},{1,7},{3,5},{5,3},{7,1},{8,14},{10,12},{12... | collective-permute-start | bytes 589832 | tf_op jit(solution)/shard_map/ppermute | solution.py:212
  197.8 24.6 %collective-permute-start.20 = (bf16[192,512]{1,0:T(8,128)(2,1)S(1)}, bf16[192,512]{1,0:T(8,128)(2,1)S(1)}, u32[]{:S(2)}, u32[]{:S(2)}) collective-permute-start(bf16[192,512]{1,0:T(8,128)(2,1)S(1)} %fusion.3), channel_id=1, source_target_pairs={{8,0},{16,8},{24,16},{32,24},{40,32},{48,40},{56,48},{64,56},{72,6... | collective-permute-start | bytes 589832 | tf_op jit(solution)/shard_map/ppermute | solution.py:265

commit v5 on v4

--- a/solution.py
+++ b/solution.py
@@ -15,7 +15,7 @@
 SLOTS = HEADS * ROWS
 LOW = -1e30
 SLACK = 8.0
-REST = 4
+REST = 2
 SCALE = WIDTH ** -0.5
 Y, Z, X, C = 4, 16, 4, 2
 
@@ -78,7 +78,8 @@
         full, lambda p: (p + ROWS > lo) & (p <= base) & ((p < lo) | (p == base))
     )
     wholes = full // group
-    head = wholes * group
+    fours = (full - wholes * group) // 4
+    head = wholes * group + fours * 4
     rests = (used - head + REST - 1) // REST
     for j in range(REST - 1):
 
@@ -99,6 +100,7 @@
             lane = lax.broadcasted_iota(jnp.int32, (1, ROWS), 1)
             key_at = jnp.concatenate([lane + slot_pos[start + j] for j in range(size)], axis=1)
             row = lax.broadcasted_iota(jnp.int32, (ROWS, size * ROWS), 0) + base
+            row = jnp.concatenate([row, row], axis=0)
             inside = (key_at >= lo) & (key_at <= row)
             s = jnp.where(inside, s, LOW)
         top = jnp.max(s, axis=1, keepdims=True)
@@ -121,15 +123,22 @@
         )
         p_s[rows, :] += jnp.dot(prob.astype(jnp.bfloat16), k1, preferred_element_type=jnp.float32)
 
-    @pl.loop(0, wholes * 2)
+    @pl.loop(0, wholes)
     def _(i):
-        rows = pl.ds(pl.multiple_of(i % 2 * (SLOTS // 2), SLOTS // 2), SLOTS // 2)
-        visit(i // 2 * group, group, rows, False)
-
-    @pl.loop(0, rests * HEADS)
+        visit(i * group, group, pl.ds(0, SLOTS), False)
+
+    def half(i):
+        return pl.ds(pl.multiple_of(i % 2 * (SLOTS // 2), SLOTS // 2), SLOTS // 2)
+
+    if group > 4:
+
+        @pl.loop(0, fours * 2)
+        def _(i):
+            visit(wholes * group + i // 2 * 4, 4, half(i), False)
+
+    @pl.loop(0, rests * 2)
     def _(i):
-        rows = pl.ds(pl.multiple_of(i % HEADS * ROWS, ROWS), ROWS)
-        visit(head + i // HEADS * REST, REST, rows, True)
+        visit(head + i // 2 * REST, REST, half(i), True)
 
     if last:
         l = p_s[:, WIDTH:]
@@ -256,9 +265,10 @@
         last = step == half
         below = lax.ppermute(below[: Y // 2] if last else below, "z", up)
         above = lax.ppermute(above[Y // 2 :] if last else above, "z", down)
-        state = attention(par, pos, done, q, g, arrays, state, False)
-        done += sum(a.shape[0] for a in arrays)
-        arrays = []
+        if step % 2 == 0:
+            state = attention(par, pos, done, q, g, arrays, state, False)
+            done += sum(a.shape[0] for a in arrays)
+            arrays = []
         arrays += [below, above]
     state = attention(par, pos, done, q, g, arrays, state, True)
     hidden = reduce_heads(state, w_query, d_out)

time: 224 us -> 182 us (0.81)
  Pallas kernels: 63.2 us -> 33.6 us
  starting transfers between devices: 94.2 us -> 81.6 us
    pallas_call x9 -> x5, Pallas kernels: 60.5 us -> 30.9 us  [attention(): pl.pallas_call(functools.partial(attend, counts, group, offset, first, la...]
    ppermute x1, starting transfers between devices: 18.7 us -> 4.76 us  [shards(): lax.ppermute(hidden, ('y', 'z'), [(i + 1, i) for i in range(Y * Z - 1)])]
    ppermute x8, starting transfers between devices: 45 us -> 49.8 us  [shards(): above = lax.ppermute(above[Y // 2:] if last else above, 'z', down)]
    ppermute x8, starting transfers between devices: 18.8 us -> 15.3 us  [shards(): below = lax.ppermute(below[:Y // 2] if last else below, 'z', up)]
    ppermute x8, waiting for transfers between devices: 23.8 us -> 26.2 us  [shards(): above = lax.ppermute(above[Y // 2:] if last else above, 'z', down)]
    unnamed x21 -> x13, local copies, waits for them, and re-layouts: 4.78 us -> 3.29 us
  transfers between devices with their start and end apart: 21 -> 21, of which waited for: 15 -> 16; matrix products, arithmetic and copies ran while one was open for 1% -> 1% of each run, Pallas kernels for 25% -> 16%
where the time goes in v5:
time: 182 us; the launch traced here: 181 us
  starting transfers between devices  81.6 us (45%)
  waiting for transfers between devices  44.5 us (24%)
  Pallas kernels  33.6 us (18%)
  blocking collectives  14.9 us (8%)
  local copies, waits for them, and re-layouts  4.6 us (3%)
    ppermute x8, starting transfers between devices, shards(): above = lax.ppermute(above[Y // 2:] if last else above, 'z', down)  49.8 us
    pallas_call x5, Pallas kernels, attention(): pl.pallas_call(functools.partial(attend, counts, group, offset, first, la...  30.9 us
    ppermute x8, waiting for transfers between devices, shards(): above = lax.ppermute(above[Y // 2:] if last else above, 'z', down)  26.2 us
    ppermute x8, starting transfers between devices, shards(): below = lax.ppermute(below[:Y // 2] if last else below, 'z', up)  15.3 us
    all_gather x1, blocking collectives, shards(): mine = lax.all_gather(jnp.concatenate([keys, values], axis=1), 'y', axis=0)  14.9 us
    ppermute x4, starting transfers between devices, exchange(): return lax.ppermute(value, axis, [(i, i ^ mask) for i in range(count)])  11.8 us
    ppermute x4, waiting for transfers between devices, exchange(): return lax.ppermute(value, axis, [(i, i ^ mask) for i in range(count)])  7.71 us
    ppermute x1, waiting for transfers between devices, shards(): lax.ppermute(hidden, ('y', 'z'), [(i + 1, i) for i in range(Y * Z - 1)])  7.06 us
  transfers between devices with their start and end apart: 21, of which 16 were waited for; matrix products, arithmetic and copies ran while one was open for 1% of the time, Pallas kernels for 16%

profile of v5, /device:TPU:24, one launch (start us, length us, event | category | flops | bytes accessed | tf_op | source)
XLA Modules:
  0.0 181.5 jit_solution(15790843692292313654)
XLA Ops:
  0.0 0.8 pad_maximum_fusion
  0.8 14.9 %all-gather = bf16[768,256]{1,0:T(8,128)(2,1)S(1)} all-gather(bf16[192,256]{1,0:T(8,128)(2,1)S(1)} %pad_maximum_fusion), channel_id=2, replica_groups=mesh['y'=4,'z'=16,'x'=4,'core'=2] {'y'}, dimensions={0}, use_global_device_ids=true | all-gather | bytes 491520 | tf_op jit(solution)/shard_map/all_gather | solution.py:250
  15.7 9.5 %collective-permute-start.8 = (bf16[4,192,256]{2,1,0:T(8,128)(2,1)S(1)}, bf16[4,192,256]{2,1,0:T(8,128)(2,1)S(1)}, u32[]{:S(2)}, u32[]{:S(2)}) collective-permute-start(bf16[4,192,256]{2,1,0:T(8,128)(2,1)S(1)} %bitcast.13), channel_id=1, source_target_pairs={{0,120},{8,0},{16,8},{24,16},{32,24},{40,32},{48,40},{56,48},{64,5... | collective-permute-start | bytes 1179656 | tf_op jit(solution)/shard_map/ppermute | solution.py:267
  25.2 1.9 %collective-permute-start = (bf16[4,192,256]{2,1,0:T(8,128)(2,1)S(1)}, bf16[4,192,256]{2,1,0:T(8,128)(2,1)S(1)}, u32[]{:S(2)}, u32[]{:S(2)}) collective-permute-start(bf16[4,192,256]{2,1,0:T(8,128)(2,1)S(1)} %bitcast.14), channel_id=1, source_target_pairs={{0,8},{8,16},{16,24},{24,32},{32,40},{40,48},{48,56},{56,64},{64,7... | collective-permute-start | bytes 1179656 | tf_op jit(solution)/shard_map/ppermute | solution.py:266
  27.1 3.3 %collective-permute-done.8.refs_4_ = bf16[4,192,256]{2,1,0:T(8,128)(2,1)S(1)} collective-permute-done((bf16[4,192,256]{2,1,0:T(8,128)(2,1)S(1)}, bf16[4,192,256]{2,1,0:T(8,128)(2,1)S(1)}, u32[]{:S(2)}, u32[]{:S(2)}) %collective-permute-start.8) | collective-permute-done | bytes 393248 | tf_op jit(solution)/shard_map/ppermute | solution.py:267
  30.5 5.6 %collective-permute-start.9 = (bf16[4,192,256]{2,1,0:T(8,128)(2,1)S(1)}, bf16[4,192,256]{2,1,0:T(8,128)(2,1)S(1)}, u32[]{:S(2)}, u32[]{:S(2)}) collective-permute-start(bf16[4,192,256]{2,1,0:T(8,128)(2,1)S(1)} %collective-permute-done.8.refs_4_), channel_id=1, source_target_pairs={{0,120},{8,0},{16,8},{24,16},{32,24},{40,32},{48,40},{56,48},{64,5... | collective-permute-start | bytes 1179656 | tf_op jit(solution)/shard_map/ppermute | solution.py:267
  36.1 1.9 %collective-permute-start.1 = (bf16[4,192,256]{2,1,0:T(8,128)(2,1)S(1)}, bf16[4,192,256]{2,1,0:T(8,128)(2,1)S(1)}, u32[]{:S(2)}, u32[]{:S(2)}) collective-permute-start(bf16[4,192,256]{2,1,0:T(8,128)(2,1)S(1)} %collective-permute-done.refs_3_), channel_id=1, source_target_pairs={{0,8},{8,16},{16,24},{24,32},{32,40},{40,48},{48,56},{56,64},{64,7... | collective-permute-start | bytes 1179656 | tf_op jit(solution)/shard_map/ppermute | solution.py:266
  38.0 3.5 %collective-permute-done.9.refs_3_ = bf16[4,192,256]{2,1,0:T(8,128)(2,1)S(1)} collective-permute-done((bf16[4,192,256]{2,1,0:T(8,128)(2,1)S(1)}, bf16[4,192,256]{2,1,0:T(8,128)(2,1)S(1)}, u32[]{:S(2)}, u32[]{:S(2)}) %collective-permute-start.9) | collective-permute-done | bytes 393248 | tf_op jit(solution)/shard_map/ppermute | solution.py:267
  41.5 5.6 %collective-permute-start.10 = (bf16[4,192,256]{2,1,0:T(8,128)(2,1)S(1)}, bf16[4,192,256]{2,1,0:T(8,128)(2,1)S(1)}, u32[]{:S(2)}, u32[]{:S(2)}) collective-permute-start(bf16[4,192,256]{2,1,0:T(8,128)(2,1)S(1)} %collective-permute-done.9.refs_3_), channel_id=1, source_target_pairs={{0,120},{8,0},{16,8},{24,16},{32,24},{40,32},{48,40},{56,48},{64,5... | collective-permute-start | bytes 1179656 | tf_op jit(solution)/shard_map/ppermute | solution.py:267
  47.4 1.9 %collective-permute-start.2 = (bf16[4,192,256]{2,1,0:T(8,128)(2,1)S(1)}, bf16[4,192,256]{2,1,0:T(8,128)(2,1)S(1)}, u32[]{:S(2)}, u32[]{:S(2)}) collective-permute-start(bf16[4,192,256]{2,1,0:T(8,128)(2,1)S(1)} %collective-permute-done.1.refs_2_), channel_id=1, source_target_pairs={{0,8},{8,16},{16,24},{24,32},{32,40},{40,48},{48,56},{56,64},{64,7... | collective-permute-start | bytes 1179656 | tf_op jit(solution)/shard_map/ppermute | solution.py:266
  49.3 4.3 %collective-permute-done.10.refs_5_ = bf16[4,192,256]{2,1,0:T(8,128)(2,1)S(1)} collective-permute-done((bf16[4,192,256]{2,1,0:T(8,128)(2,1)S(1)}, bf16[4,192,256]{2,1,0:T(8,128)(2,1)S(1)}, u32[]{:S(2)}, u32[]{:S(2)}) %collective-permute-start.10) | collective-permute-done | bytes 393248 | tf_op jit(solution)/shard_map/ppermute | solution.py:267
  53.6 5.6 %collective-permute-start.11 = (bf16[4,192,256]{2,1,0:T(8,128)(2,1)S(1)}, bf16[4,192,256]{2,1,0:T(8,128)(2,1)S(1)}, u32[]{:S(2)}, u32[]{:S(2)}) collective-permute-start(bf16[4,192,256]{2,1,0:T(8,128)(2,1)S(1)} %collective-permute-done.10.refs_5_), channel_id=1, source_target_pairs={{0,120},{8,0},{16,8},{24,16},{32,24},{40,32},{48,40},{56,48},{64,5... | collective-permute-start | bytes 1179656 | tf_op jit(solution)/shard_map/ppermute | solution.py:267
  59.8 1.9 %collective-permute-start.3 = (bf16[4,192,256]{2,1,0:T(8,128)(2,1)S(1)}, bf16[4,192,256]{2,1,0:T(8,128)(2,1)S(1)}, u32[]{:S(2)}, u32[]{:S(2)}) collective-permute-start(bf16[4,192,256]{2,1,0:T(8,128)(2,1)S(1)} %collective-permute-done.2.refs_4_), channel_id=1, source_target_pairs={{0,8},{8,16},{16,24},{24,32},{32,40},{40,48},{48,56},{56,64},{64,7... | collective-permute-start | bytes 1179656 | tf_op jit(solution)/shard_map/ppermute | solution.py:266
  61.7 0.7 copy-done.3
  62.5 4.4 %collective-permute-done.11.refs_3_ = bf16[4,192,256]{2,1,0:T(8,128)(2,1)S(1)} collective-permute-done((bf16[4,192,256]{2,1,0:T(8,128)(2,1)S(1)}, bf16[4,192,256]{2,1,0:T(8,128)(2,1)S(1)}, u32[]{:S(2)}, u32[]{:S(2)}) %collective-permute-start.11) | collective-permute-done | bytes 393248 | tf_op jit(solution)/shard_map/ppermute | solution.py:267
  66.9 5.6 %collective-permute-start.12 = (bf16[4,192,256]{2,1,0:T(8,128)(2,1)S(1)}, bf16[4,192,256]{2,1,0:T(8,128)(2,1)S(1)}, u32[]{:S(2)}, u32[]{:S(2)}) collective-permute-start(bf16[4,192,256]{2,1,0:T(8,128)(2,1)S(1)} %collective-permute-done.11.refs_3_), channel_id=1, source_target_pairs={{0,120},{8,0},{16,8},{24,16},{32,24},{40,32},{48,40},{56,48},{64,5... | collective-permute-start | bytes 1179656 | tf_op jit(solution)/shard_map/ppermute | solution.py:267
  72.5 0.9 collective-permute-done.3.refs_2_
  73.4 1.9 %collective-permute-start.4 = (bf16[4,192,256]{2,1,0:T(8,128)(2,1)S(1)}, bf16[4,192,256]{2,1,0:T(8,128)(2,1)}, u32[]{:S(2)}, u32[]{:S(2)}) collective-permute-start(bf16[4,192,256]{2,1,0:T(8,128)(2,1)S(1)} %collective-permute-done.3.refs_2_), channel_id=1, source_target_pairs={{0,8},{8,16},{16,24},{24,32},{32,40},{40,48},{48,56},{56,64},{64,7... | collective-permute-start | bytes 1179656 | tf_op jit(solution)/shard_map/ppermute | solution.py:266
  75.3 6.1 %collective-permute-done.12.refs_5_ = bf16[4,192,256]{2,1,0:T(8,128)(2,1)S(1)} collective-permute-done((bf16[4,192,256]{2,1,0:T(8,128)(2,1)S(1)}, bf16[4,192,256]{2,1,0:T(8,128)(2,1)S(1)}, u32[]{:S(2)}, u32[]{:S(2)}) %collective-permute-start.12) | collective-permute-done | bytes 393248 | tf_op jit(solution)/shard_map/ppermute | solution.py:267
  81.4 5.6 %collective-permute-start.13 = (bf16[4,192,256]{2,1,0:T(8,128)(2,1)S(1)}, bf16[4,192,256]{2,1,0:T(8,128)(2,1)}, u32[]{:S(2)}, u32[]{:S(2)}) collective-permute-start(bf16[4,192,256]{2,1,0:T(8,128)(2,1)S(1)} %collective-permute-done.12.refs_5_), channel_id=1, source_target_pairs={{0,120},{8,0},{16,8},{24,16},{32,24},{40,32},{48,40},{56,48},{64,5... | collective-permute-start | bytes 1179656 | tf_op jit(solution)/shard_map/ppermute | solution.py:267
  87.0 0.9 collective-permute-done.4.refs_4_
  87.9 1.9 %collective-permute-start.5 = (bf16[4,192,256]{2,1,0:T(8,128)(2,1)}, bf16[4,192,256]{2,1,0:T(8,128)(2,1)}, u32[]{:S(2)}, u32[]{:S(2)}) collective-permute-start(bf16[4,192,256]{2,1,0:T(8,128)(2,1)} %collective-permute-done.4.refs_4_), channel_id=1, source_target_pairs={{0,8},{8,16},{16,24},{24,32},{32,40},{40,48},{48,56},{56,64},{64,7... | collective-permute-start | bytes 1179656 | tf_op jit(solution)/shard_map/ppermute | solution.py:266
  89.8 1.2 dynamic_slice.3
  91.7 4.5 %collective-permute-done.13.refs_3_ = bf16[4,192,256]{2,1,0:T(8,128)(2,1)} collective-permute-done((bf16[4,192,256]{2,1,0:T(8,128)(2,1)S(1)}, bf16[4,192,256]{2,1,0:T(8,128)(2,1)}, u32[]{:S(2)}, u32[]{:S(2)}) %collective-permute-start.13) | collective-permute-done | bytes 393248 | tf_op jit(solution)/shard_map/ppermute | solution.py:267
  96.3 5.7 %collective-permute-start.14 = (bf16[4,192,256]{2,1,0:T(8,128)(2,1)}, bf16[4,192,256]{2,1,0:T(8,128)(2,1)S(1)}, u32[]{:S(2)}, u32[]{:S(2)}) collective-permute-start(bf16[4,192,256]{2,1,0:T(8,128)(2,1)} %collective-permute-done.13.refs_3_), channel_id=1, source_target_pairs={{0,120},{8,0},{16,8},{24,16},{32,24},{40,32},{48,40},{56,48},{64,5... | collective-permute-start | bytes 1179656 | tf_op jit(solution)/shard_map/ppermute | solution.py:267
  102.0 0.9 collective-permute-done.5.refs_2_
  102.8 1.9 %collective-permute-start.6 = (bf16[4,192,256]{2,1,0:T(8,128)(2,1)}, bf16[4,192,256]{2,1,0:T(8,128)(2,1)S(1)}, u32[]{:S(2)}, u32[]{:S(2)}) collective-permute-start(bf16[4,192,256]{2,1,0:T(8,128)(2,1)} %collective-permute-done.5.refs_2_), channel_id=1, source_target_pairs={{0,8},{8,16},{16,24},{24,32},{32,40},{40,48},{48,56},{56,64},{64,7... | collective-permute-start | bytes 1179656 | tf_op jit(solution)/shard_map/ppermute | solution.py:266
  104.8 0.9 copy-done.1
  105.7 0.9 copy-done.2
  106.6 8.7 %attend.5 = (f32[768,128]{1,0:T(8,128)S(1)}, f32[768,128]{1,0:T(8,128)S(1)}, f32[768,128]{1,0:T(8,128)S(1)}) custom-call(s32[2]{0:T(128)S(1)} %compare_select_fusion.3.par_ref, s32[64]{0:T(128)S(1)} %fusion.6.pos_ref, bf16[192,512]{1,0:T(8,128)(2,1)S(1)} %copy-done.1, bf16[192,512]{1,0:T(8,128)(2,1)S(1)} %copy-done.2, bf16[4,192,256]{2,1,0:T(8,128)(2,1)S(1)} %bitcast.15, ...), custom_call_target="tpu_custom_call" | custom-call | flops 905969664 | bytes 3538944 | tf_op jit(solution)/shard_map/attend/pallas_call | solution.py:170
  115.4 7.4 %attend.6 = (f32[768,128]{1,0:T(8,128)S(1)}, f32[768,128]{1,0:T(8,128)S(1)}, f32[768,128]{1,0:T(8,128)S(1)}) custom-call(s32[2]{0:T(128)S(1)} %compare_select_fusion.3.par_ref, s32[64]{0:T(128)S(1)} %fusion.6.pos_ref, bf16[192,512]{1,0:T(8,128)(2,1)S(1)} %copy-done.1, bf16[192,512]{1,0:T(8,128)(2,1)S(1)} %copy-done.2, ...), custom_call_target="tpu_custom_call" | custom-call | flops 1207959552 | bytes 3932160 | tf_op jit(solution)/shard_map/attend/pallas_call | solution.py:170
  122.8 6.6 %collective-permute-start.15 = (bf16[2,192,256]{2,1,0:T(8,128)(2,1)S(1)}, bf16[2,192,256]{2,1,0:T(8,128)(2,1)S(1)}, u32[]{:S(2)}, u32[]{:S(2)}) collective-permute-start(bf16[2,192,256]{2,1,0:T(8,128)(2,1)S(1)} %slice.25), channel_id=1, source_target_pairs={{0,120},{8,0},{16,8},{24,16},{32,24},{40,32},{48,40},{56,48},{64,5... | collective-permute-start | bytes 589832 | tf_op jit(solution)/shard_map/ppermute | solution.py:267
  129.5 1.9 %collective-permute-start.7 = (bf16[2,192,256]{2,1,0:T(8,128)(2,1)S(1)}, bf16[2,192,256]{2,1,0:T(8,128)(2,1)S(1)}, u32[]{:S(2)}, u32[]{:S(2)}) collective-permute-start(bf16[2,192,256]{2,1,0:T(8,128)(2,1)S(1)} %slice.24), channel_id=1, source_target_pairs={{0,8},{8,16},{16,24},{24,32},{32,40},{40,48},{48,56},{56,64},{64,7... | collective-permute-start | bytes 589832 | tf_op jit(solution)/shard_map/ppermute | solution.py:266
  131.4 5.4 %attend.7 = (f32[768,128]{1,0:T(8,128)S(1)}, f32[768,128]{1,0:T(8,128)S(1)}, f32[768,128]{1,0:T(8,128)S(1)}) custom-call(s32[2]{0:T(128)S(1)} %compare_select_fusion.3.par_ref, s32[64]{0:T(128)S(1)} %fusion.6.pos_ref, bf16[192,512]{1,0:T(8,128)(2,1)S(1)} %copy-done.1, bf16[192,512]{1,0:T(8,128)(2,1)S(1)} %copy-done.2, ...), custom_call_target="tpu_custom_call" | custom-call | flops 1207959552 | bytes 3932160 | tf_op jit(solution)/shard_map/attend/pallas_call | solution.py:170
  136.8 5.9 %attend.8 = (f32[768,128]{1,0:T(8,128)S(1)}, f32[768,128]{1,0:T(8,128)S(1)}, f32[768,128]{1,0:T(8,128)S(1)}) custom-call(s32[2]{0:T(128)S(1)} %compare_select_fusion.3.par_ref, s32[64]{0:T(128)S(1)} %fusion.6.pos_ref, bf16[192,512]{1,0:T(8,128)(2,1)S(1)} %copy-done.1, bf16[192,512]{1,0:T(8,128)(2,1)S(1)} %copy-done.2, ...), custom_call_target="tpu_custom_call" | custom-call | flops 1207959552 | bytes 3932160 | tf_op jit(solution)/shard_map/attend/pallas_call | solution.py:170
  142.8 3.4 %attend.9.gq_ref = bf16[192,512]{1,0:T(8,128)(2,1)S(1)} custom-call(s32[2]{0:T(128)S(1)} %compare_select_fusion.3.par_ref, s32[64]{0:T(128)S(1)} %fusion.6.pos_ref, bf16[192,512]{1,0:T(8,128)(2,1)S(1)} %copy-done.1, bf16[192,512]{1,0:T(8,128)(2,1)S(1)} %copy-done.2, bf16[2,192,256]{2,1,0:T(8,128)(2,1)S(1)} %collective-permute-done.7.refs_2_, ...), custom_call_target="tpu_custom_call" | custom-call | flops 301989888 | bytes 2752512 | tf_op jit(solution)/shard_map/attend/pallas_call | solution.py:170
  146.2 1.4 project.3
  147.6 1.9 %collective-permute-start.16 = (bf16[4,192,512]{2,1,0:T(8,128)(2,1)S(1)}, bf16[4,192,512]{2,1,0:T(8,128)(2,1)S(1)}, u32[]{:S(2)}, u32[]{:S(2)}) collective-permute-start(bf16[4,192,512]{2,1,0:T(8,128)(2,1)S(1)} %project.3), channel_id=1, source_target_pairs={{0,1},{1,0},{2,3},{3,2},{4,5},{5,4},{6,7},{7,6},{8,9},{9,8},{10,11... | collective-permute-start | bytes 2359304 | tf_op jit(solution)/shard_map/ppermute | solution.py:221
  149.6 1.4 project.2
  151.0 0.8 collective-permute-done.16
  152.1 5.0 %collective-permute-start.17 = (bf16[192,512]{1,0:T(8,128)(2,1)S(1)}, bf16[192,512]{1,0:T(8,128)(2,1)S(1)}, u32[]{:S(2)}, u32[]{:S(2)}) collective-permute-start(bf16[192,512]{1,0:T(8,128)(2,1)S(1)} %get-tuple-element.29), channel_id=1, source_target_pairs={{0,4},{2,6},{4,0},{6,2},{1,5},{3,7},{5,1},{7,3},{8,12},{10,14},{12... | collective-permute-start | bytes 589832 | tf_op jit(solution)/shard_map/ppermute | solution.py:221
  157.1 2.2 %collective-permute-start.18 = (bf16[192,512]{1,0:T(8,128)(2,1)S(1)}, bf16[192,512]{1,0:T(8,128)(2,1)S(1)}, u32[]{:S(2)}, u32[]{:S(2)}) collective-permute-start(bf16[192,512]{1,0:T(8,128)(2,1)S(1)} %get-tuple-element.31), channel_id=1, source_target_pairs={{0,2},{2,0},{4,6},{6,4},{1,3},{3,1},{5,7},{7,5},{8,10},{10,8},{12,... | collective-permute-start | bytes 589832 | tf_op jit(solution)/shard_map/ppermute | solution.py:221
  159.3 2.6 %collective-permute-start.19 = (bf16[192,512]{1,0:T(8,128)(2,1)S(1)}, bf16[192,512]{1,0:T(8,128)(2,1)S(1)}, u32[]{:S(2)}, u32[]{:S(2)}) collective-permute-start(bf16[192,512]{1,0:T(8,128)(2,1)S(1)} %get-tuple-element.30), channel_id=1, source_target_pairs={{0,6},{2,4},{4,2},{6,0},{1,7},{3,5},{5,3},{7,1},{8,14},{10,12},{12... | collective-permute-start | bytes 589832 | tf_op jit(solution)/shard_map/ppermute | solution.py:221
  162.0 0.9 collective-permute-done.17
  162.9 3.6 %collective-permute-done.18 = bf16[192,512]{1,0:T(8,128)(2,1)S(1)} collective-permute-done((bf16[192,512]{1,0:T(8,128)(2,1)S(1)}, bf16[192,512]{1,0:T(8,128)(2,1)S(1)}, u32[]{:S(2)}, u32[]{:S(2)}) %collective-permute-start.18) | collective-permute-done | bytes 196640 | tf_op jit(solution)/shard_map/ppermute | solution.py:221
  166.5 2.3 %collective-permute-done.19 = bf16[192,512]{1,0:T(8,128)(2,1)S(1)} collective-permute-done((bf16[192,512]{1,0:T(8,128)(2,1)S(1)}, bf16[192,512]{1,0:T(8,128)(2,1)S(1)}, u32[]{:S(2)}, u32[]{:S(2)}) %collective-permute-start.19) | collective-permute-done | bytes 196640 | tf_op jit(solution)/shard_map/ppermute | solution.py:221
  169.0 4.8 %collective-permute-start.20 = (bf16[192,512]{1,0:T(8,128)(2,1)S(1)}, bf16[192,512]{1,0:T(8,128)(2,1)S(1)}, u32[]{:S(2)}, u32[]{:S(2)}) collective-permute-start(bf16[192,512]{1,0:T(8,128)(2,1)S(1)} %fusion.3), channel_id=1, source_target_pairs={{8,0},{16,8},{24,16},{32,24},{40,32},{48,40},{56,48},{64,56},{72,6... | collective-permute-start | bytes 589832 | tf_op jit(solution)/shard_map/ppermute | solution.py:275
  173.7 7.1 %collective-permute-done.20 = bf16[192,512]{1,0:T(8,128)(2,1)S(1)} collective-permute-done((bf16[192,512]{1,0:T(8,128)(2,1)S(1)}, bf16[192,512]{1,0:T(8,128)(2,1)S(1)}, u32[]{:S(2)}, u32[]{:S(2)}) %collective-permute-start.20) | collective-permute-done | bytes 196640 | tf_op jit(solution)/shard_map/ppermute | solution.py:275
  (26 shorter events, 2.1 us)
Async XLA Ops:
  15.7 14.8 %collective-permute-start.8 = (bf16[4,192,256]{2,1,0:T(8,128)(2,1)S(1)}, bf16[4,192,256]{2,1,0:T(8,128)(2,1)S(1)}, u32[]{:S(2)}, u32[]{:S(2)}) collective-permute-start(bf16[4,192,256]{2,1,0:T(8,128)(2,1)S(1)} %bitcast.13), channel_id=1, source_target_pairs={{0,120},{8,0},{16,8},{24,16},{32,24},{40,32},{48,40},{56,48},{64,5... | collective-permute-start | bytes 1179656 | tf_op jit(solution)/shard_map/ppermute | solution.py:267
  25.2 10.9 %collective-permute-start = (bf16[4,192,256]{2,1,0:T(8,128)(2,1)S(1)}, bf16[4,192,256]{2,1,0:T(8,128)(2,1)S(1)}, u32[]{:S(2)}, u32[]{:S(2)}) collective-permute-start(bf16[4,192,256]{2,1,0:T(8,128)(2,1)S(1)} %bitcast.14), channel_id=1, source_target_pairs={{0,8},{8,16},{16,24},{24,32},{32,40},{40,48},{48,56},{56,64},{64,7... | collective-permute-start | bytes 1179656 | tf_op jit(solution)/shard_map/ppermute | solution.py:266
  30.5 11.0 %collective-permute-start.9 = (bf16[4,192,256]{2,1,0:T(8,128)(2,1)S(1)}, bf16[4,192,256]{2,1,0:T(8,128)(2,1)S(1)}, u32[]{:S(2)}, u32[]{:S(2)}) collective-permute-start(bf16[4,192,256]{2,1,0:T(8,128)(2,1)S(1)} %collective-permute-done.8.refs_4_), channel_id=1, source_target_pairs={{0,120},{8,0},{16,8},{24,16},{32,24},{40,32},{48,40},{56,48},{64,5... | collective-permute-start | bytes 1179656 | tf_op jit(solution)/shard_map/ppermute | solution.py:267
  36.1 11.3 %collective-permute-start.1 = (bf16[4,192,256]{2,1,0:T(8,128)(2,1)S(1)}, bf16[4,192,256]{2,1,0:T(8,128)(2,1)S(1)}, u32[]{:S(2)}, u32[]{:S(2)}) collective-permute-start(bf16[4,192,256]{2,1,0:T(8,128)(2,1)S(1)} %collective-permute-done.refs_3_), channel_id=1, source_target_pairs={{0,8},{8,16},{16,24},{24,32},{32,40},{40,48},{48,56},{56,64},{64,7... | collective-permute-start | bytes 1179656 | tf_op jit(solution)/shard_map/ppermute | solution.py:266
  41.5 12.1 %collective-permute-start.10 = (bf16[4,192,256]{2,1,0:T(8,128)(2,1)S(1)}, bf16[4,192,256]{2,1,0:T(8,128)(2,1)S(1)}, u32[]{:S(2)}, u32[]{:S(2)}) collective-permute-start(bf16[4,192,256]{2,1,0:T(8,128)(2,1)S(1)} %collective-permute-done.9.refs_3_), channel_id=1, source_target_pairs={{0,120},{8,0},{16,8},{24,16},{32,24},{40,32},{48,40},{56,48},{64,5... | collective-permute-start | bytes 1179656 | tf_op jit(solution)/shard_map/ppermute | solution.py:267
  47.4 12.4 %collective-permute-start.2 = (bf16[4,192,256]{2,1,0:T(8,128)(2,1)S(1)}, bf16[4,192,256]{2,1,0:T(8,128)(2,1)S(1)}, u32[]{:S(2)}, u32[]{:S(2)}) collective-permute-start(bf16[4,192,256]{2,1,0:T(8,128)(2,1)S(1)} %collective-permute-done.1.refs_2_), channel_id=1, source_target_pairs={{0,8},{8,16},{16,24},{24,32},{32,40},{40,48},{48,56},{56,64},{64,7... | collective-permute-start | bytes 1179656 | tf_op jit(solution)/shard_map/ppermute | solution.py:266
  53.6 13.3 %collective-permute-start.11 = (bf16[4,192,256]{2,1,0:T(8,128)(2,1)S(1)}, bf16[4,192,256]{2,1,0:T(8,128)(2,1)S(1)}, u32[]{:S(2)}, u32[]{:S(2)}) collective-permute-start(bf16[4,192,256]{2,1,0:T(8,128)(2,1)S(1)} %collective-permute-done.10.refs_5_), channel_id=1, source_target_pairs={{0,120},{8,0},{16,8},{24,16},{32,24},{40,32},{48,40},{56,48},{64,5... | collective-permute-start | bytes 1179656 | tf_op jit(solution)/shard_map/ppermute | solution.py:267
  59.8 13.6 %collective-permute-start.3 = (bf16[4,192,256]{2,1,0:T(8,128)(2,1)S(1)}, bf16[4,192,256]{2,1,0:T(8,128)(2,1)S(1)}, u32[]{:S(2)}, u32[]{:S(2)}) collective-permute-start(bf16[4,192,256]{2,1,0:T(8,128)(2,1)S(1)} %collective-permute-done.2.refs_4_), channel_id=1, source_target_pairs={{0,8},{8,16},{16,24},{24,32},{32,40},{40,48},{48,56},{56,64},{64,7... | collective-permute-start | bytes 1179656 | tf_op jit(solution)/shard_map/ppermute | solution.py:266
  61.7 0.8 copy-start.3
  66.9 14.4 %collective-permute-start.12 = (bf16[4,192,256]{2,1,0:T(8,128)(2,1)S(1)}, bf16[4,192,256]{2,1,0:T(8,128)(2,1)S(1)}, u32[]{:S(2)}, u32[]{:S(2)}) collective-permute-start(bf16[4,192,256]{2,1,0:T(8,128)(2,1)S(1)} %collective-permute-done.11.refs_3_), channel_id=1, source_target_pairs={{0,120},{8,0},{16,8},{24,16},{32,24},{40,32},{48,40},{56,48},{64,5... | collective-permute-start | bytes 1179656 | tf_op jit(solution)/shard_map/ppermute | solution.py:267
  73.4 14.5 %collective-permute-start.4 = (bf16[4,192,256]{2,1,0:T(8,128)(2,1)S(1)}, bf16[4,192,256]{2,1,0:T(8,128)(2,1)}, u32[]{:S(2)}, u32[]{:S(2)}) collective-permute-start(bf16[4,192,256]{2,1,0:T(8,128)(2,1)S(1)} %collective-permute-done.3.refs_2_), channel_id=1, source_target_pairs={{0,8},{8,16},{16,24},{24,32},{32,40},{40,48},{48,56},{56,64},{64,7... | collective-permute-start | bytes 1179656 | tf_op jit(solution)/shard_map/ppermute | solution.py:266
  81.4 14.9 %collective-permute-start.13 = (bf16[4,192,256]{2,1,0:T(8,128)(2,1)S(1)}, bf16[4,192,256]{2,1,0:T(8,128)(2,1)}, u32[]{:S(2)}, u32[]{:S(2)}) collective-permute-start(bf16[4,192,256]{2,1,0:T(8,128)(2,1)S(1)} %collective-permute-done.12.refs_5_), channel_id=1, source_target_pairs={{0,120},{8,0},{16,8},{24,16},{32,24},{40,32},{48,40},{56,48},{64,5... | collective-permute-start | bytes 1179656 | tf_op jit(solution)/shard_map/ppermute | solution.py:267
  87.9 14.9 %collective-permute-start.5 = (bf16[4,192,256]{2,1,0:T(8,128)(2,1)}, bf16[4,192,256]{2,1,0:T(8,128)(2,1)}, u32[]{:S(2)}, u32[]{:S(2)}) collective-permute-start(bf16[4,192,256]{2,1,0:T(8,128)(2,1)} %collective-permute-done.4.refs_4_), channel_id=1, source_target_pairs={{0,8},{8,16},{16,24},{24,32},{32,40},{40,48},{48,56},{56,64},{64,7... | collective-permute-start | bytes 1179656 | tf_op jit(solution)/shard_map/ppermute | solution.py:266
  96.3 26.5 %collective-permute-start.14 = (bf16[4,192,256]{2,1,0:T(8,128)(2,1)}, bf16[4,192,256]{2,1,0:T(8,128)(2,1)S(1)}, u32[]{:S(2)}, u32[]{:S(2)}) collective-permute-start(bf16[4,192,256]{2,1,0:T(8,128)(2,1)} %collective-permute-done.13.refs_3_), channel_id=1, source_target_pairs={{0,120},{8,0},{16,8},{24,16},{32,24},{40,32},{48,40},{56,48},{64,5... | collective-permute-start | bytes 1179656 | tf_op jit(solution)/shard_map/ppermute | solution.py:267
  102.8 26.6 %collective-permute-start.6 = (bf16[4,192,256]{2,1,0:T(8,128)(2,1)}, bf16[4,192,256]{2,1,0:T(8,128)(2,1)S(1)}, u32[]{:S(2)}, u32[]{:S(2)}) collective-permute-start(bf16[4,192,256]{2,1,0:T(8,128)(2,1)} %collective-permute-done.5.refs_2_), channel_id=1, source_target_pairs={{0,8},{8,16},{16,24},{24,32},{32,40},{40,48},{48,56},{56,64},{64,7... | collective-permute-start | bytes 1179656 | tf_op jit(solution)/shard_map/ppermute | solution.py:266
  104.8 0.9 copy-start.1
  105.7 0.9 copy-start.2
  106.6 8.7 %copy-start.4 = (bf16[4,192,256]{2,1,0:T(8,128)(2,1)S(1)}, bf16[4,192,256]{2,1,0:T(8,128)(2,1)}, u32[]{:S(2)}) copy-start(bf16[4,192,256]{2,1,0:T(8,128)(2,1)} %copy-done.3) | copy-start | bytes 1179652
  122.8 20.0 %collective-permute-start.15 = (bf16[2,192,256]{2,1,0:T(8,128)(2,1)S(1)}, bf16[2,192,256]{2,1,0:T(8,128)(2,1)S(1)}, u32[]{:S(2)}, u32[]{:S(2)}) collective-permute-start(bf16[2,192,256]{2,1,0:T(8,128)(2,1)S(1)} %slice.25), channel_id=1, source_target_pairs={{0,120},{8,0},{16,8},{24,16},{32,24},{40,32},{48,40},{56,48},{64,5... | collective-permute-start | bytes 589832 | tf_op jit(solution)/shard_map/ppermute | solution.py:267
  129.5 13.3 %collective-permute-start.7 = (bf16[2,192,256]{2,1,0:T(8,128)(2,1)S(1)}, bf16[2,192,256]{2,1,0:T(8,128)(2,1)S(1)}, u32[]{:S(2)}, u32[]{:S(2)}) collective-permute-start(bf16[2,192,256]{2,1,0:T(8,128)(2,1)S(1)} %slice.24), channel_id=1, source_target_pairs={{0,8},{8,16},{16,24},{24,32},{32,40},{40,48},{48,56},{56,64},{64,7... | collective-permute-start | bytes 589832 | tf_op jit(solution)/shard_map/ppermute | solution.py:266
  136.8 9.4 %copy-start = (bf16[4096,512]{1,0:T(8,128)(2,1)S(1)}, bf16[4096,512]{1,0:T(8,128)(2,1)}, u32[]{:S(2)}) copy-start(bf16[4096,512]{1,0:T(8,128)(2,1)} %w_ref.3) | copy-start | bytes 12582916
  147.6 4.2 %collective-permute-start.16 = (bf16[4,192,512]{2,1,0:T(8,128)(2,1)S(1)}, bf16[4,192,512]{2,1,0:T(8,128)(2,1)S(1)}, u32[]{:S(2)}, u32[]{:S(2)}) collective-permute-start(bf16[4,192,512]{2,1,0:T(8,128)(2,1)S(1)} %project.3), channel_id=1, source_target_pairs={{0,1},{1,0},{2,3},{3,2},{4,5},{5,4},{6,7},{7,6},{8,9},{9,8},{10,11... | collective-permute-start | bytes 2359304 | tf_op jit(solution)/shard_map/ppermute | solution.py:221
  150.9 17.9 %copy-start.5 = (bf16[192,512]{1,0:T(8,128)(2,1)S(1)}, bf16[192,512]{1,0:T(8,128)(2,1)}, u32[]{:S(2)}) copy-start(bf16[192,512]{1,0:T(8,128)(2,1)} %param.11) | copy-start | bytes 589828
  152.1 10.8 %collective-permute-start.17 = (bf16[192,512]{1,0:T(8,128)(2,1)S(1)}, bf16[192,512]{1,0:T(8,128)(2,1)S(1)}, u32[]{:S(2)}, u32[]{:S(2)}) collective-permute-start(bf16[192,512]{1,0:T(8,128)(2,1)S(1)} %get-tuple-element.29), channel_id=1, source_target_pairs={{0,4},{2,6},{4,0},{6,2},{1,5},{3,7},{5,1},{7,3},{8,12},{10,14},{12... | collective-permute-start | bytes 589832 | tf_op jit(solution)/shard_map/ppermute | solution.py:221
  157.1 9.4 %collective-permute-start.18 = (bf16[192,512]{1,0:T(8,128)(2,1)S(1)}, bf16[192,512]{1,0:T(8,128)(2,1)S(1)}, u32[]{:S(2)}, u32[]{:S(2)}) collective-permute-start(bf16[192,512]{1,0:T(8,128)(2,1)S(1)} %get-tuple-element.31), channel_id=1, source_target_pairs={{0,2},{2,0},{4,6},{6,4},{1,3},{3,1},{5,7},{7,5},{8,10},{10,8},{12,... | collective-permute-start | bytes 589832 | tf_op jit(solution)/shard_map/ppermute | solution.py:221
  159.3 9.5 %collective-permute-start.19 = (bf16[192,512]{1,0:T(8,128)(2,1)S(1)}, bf16[192,512]{1,0:T(8,128)(2,1)S(1)}, u32[]{:S(2)}, u32[]{:S(2)}) collective-permute-start(bf16[192,512]{1,0:T(8,128)(2,1)S(1)} %get-tuple-element.30), channel_id=1, source_target_pairs={{0,6},{2,4},{4,2},{6,0},{1,7},{3,5},{5,3},{7,1},{8,14},{10,12},{12... | collective-permute-start | bytes 589832 | tf_op jit(solution)/shard_map/ppermute | solution.py:221
  169.0 11.8 %collective-permute-start.20 = (bf16[192,512]{1,0:T(8,128)(2,1)S(1)}, bf16[192,512]{1,0:T(8,128)(2,1)S(1)}, u32[]{:S(2)}, u32[]{:S(2)}) collective-permute-start(bf16[192,512]{1,0:T(8,128)(2,1)S(1)} %fusion.3), channel_id=1, source_target_pairs={{8,0},{16,8},{24,16},{32,24},{40,32},{48,40},{56,48},{64,56},{72,6... | collective-permute-start | bytes 589832 | tf_op jit(solution)/shard_map/ppermute | solution.py:275
